TPU v7x, 256 devices: a whole 4x4x8 slice. The times are simulated.
256 devices in a mesh: tm: 64 (over y, x_hi, z), space: 4 (over x_lo, core).
Axes of the slice: x: 4 (x_hi: 2, x_lo: 2; x = x_hi * 2 + x_lo), y: 4, z: 8, core: 2. Of those that a mesh axis runs over, the one named last changes fastest.
Arguments:
- states: float32 [64, 3, 256, 1024], P('tm', None, 'space'), may hold values from -3 to 3
- background: float32 [3, 256, 1024], P(None, 'space'), may hold values from -3 to 3
- obs_cells: int32 [64, 4, 1024], P('tm'), may hold values from 0 to 262143
- obs_values: float32 [64, 4, 1024], P('tm'), may hold values from -3 to 3
- land_mask: int32 [256, 1024], P('space'), may hold values 0 or 1
Outputs:
- gradient: float32 [64, 3, 256, 1024], P('tm', None, 'space')
- next_states: float32 [64, 3, 256, 1024], P('tm', None, 'space')
All inputs are finite; a program needn't handle non-finite values. No bound on the sum of `land_mask` on one device may be relied on, other than what follows from the above.
Results may differ from a plain program's by a relative error of at most 0.0003.
Values sent between devices are 32-bit elements; how exact they have to be, the bound alone decides.
No kernel may reach another device: no remote copies, remote signals or barrier semaphores. Data moves between devices by JAX's collectives and lax.ppermute only.
A program may use at most 64 MiB of HBM per device.

v0:
```python
import jax
import jax.numpy as jnp
from jax import lax
from jax.experimental import pallas as pl
from jax.experimental.pallas import tpu as pltpu
from jax.sharding import PartitionSpec as P

NSTEP = 4
HALO = 8
BLK = 8

advect = 0.25
coriolis = 0.1
diffuse = 0.1
defect_weight = 2.0
obs_weight = 4.0
step_length = 0.1

VMEM_LIMIT = 48 * 1024 * 1024


def vmem():
    return pl.BlockSpec(memory_space=pltpu.VMEM)


def smem():
    return pl.BlockSpec(memory_space=pltpu.SMEM)


def east(x):
    return pltpu.roll(x, x.shape[1] - 1, axis=1)


def west(x):
    return pltpu.roll(x, 1, axis=1)


def below(x, after):
    first = lax.broadcasted_iota(jnp.int32, x.shape, 0) == 0
    return pltpu.roll(jnp.where(first, after, x), BLK - 1, axis=0)


def above(x, before):
    last = lax.broadcasted_iota(jnp.int32, x.shape, 0) == BLK - 1
    return pltpu.roll(jnp.where(last, before, x), 1, axis=0)


def maps_kernel(pos_ref, cells_ref, values_ref, count_ref, total_ref):
    rows, columns = count_ref.shape[1:]
    observed = cells_ref.shape[2]
    shift = columns.bit_length() - 1
    assert columns == 1 << shift
    width = 256
    base = pos_ref[0]
    row_iota = lax.broadcasted_iota(jnp.int32, (rows, observed), 0)
    col_iota = lax.broadcasted_iota(jnp.int32, (width, observed), 0)
    for step in range(NSTEP):
        cells = cells_ref[0, step : step + 1, :]
        values = obs_weight * values_ref[0, step : step + 1, :]
        row = lax.shift_right_logical(cells, shift)
        col = cells - lax.shift_left(row, shift)
        inside = row_iota == row - base
        first = values.astype(jnp.bfloat16).astype(jnp.float32)
        rest = values - first
        second = rest.astype(jnp.bfloat16).astype(jnp.float32)
        third = rest - second
        zero = jnp.zeros((rows, observed), jnp.float32)
        parts = [
            jnp.where(inside, jnp.broadcast_to(part, (rows, observed)), zero).astype(jnp.bfloat16)
            for part in (first, second, third)
        ]
        picks = jnp.where(inside, jnp.float32(obs_weight), zero).astype(jnp.bfloat16)
        left = jnp.concatenate([picks] + parts, axis=0)
        for start in range(0, columns, width):
            hot = jnp.where(col_iota == col - start, jnp.float32(1), jnp.float32(0))
            hot = hot.astype(jnp.bfloat16)
            out = lax.dot_general(
                left, hot, (((1,), (1,)), ((), ())), preferred_element_type=jnp.float32
            )
            count_ref[step, :, start : start + width] = out[:rows]
            total_ref[step, :, start : start + width] = (
                out[rows : 2 * rows] + out[2 * rows : 3 * rows] + out[3 * rows :]
            )


def forward_kernel(
    pos_ref, states_ref, up_ref, down_ref, mask_ref, path_ref, land_ref, ends_ref
):
    strip = states_ref.shape[2]
    rows = strip + 2 * HALO
    blocks = rows // BLK
    columns = states_ref.shape[3]
    base = pos_ref[0]
    grid_rows = pos_ref[1]
    path_ref[0, :, :HALO] = up_ref[:3]
    path_ref[0, :, HALO : HALO + strip] = states_ref[0]
    path_ref[0, :, HALO + strip :] = down_ref[:3]
    land_ref[:HALO] = up_ref[3]
    land_ref[HALO : HALO + strip] = mask_ref[...].astype(jnp.float32)
    land_ref[HALO + strip :] = down_ref[3]

    for step in range(NSTEP):
        for i in range(blocks):
            at = slice(i * BLK, (i + 1) * BLK)
            prior = slice(max(i - 1, 0) * BLK, (max(i - 1, 0) + 1) * BLK)
            follow = slice(min(i + 1, blocks - 1) * BLK, (min(i + 1, blocks - 1) + 1) * BLK)
            h, u, v = (path_ref[step, f, at] for f in range(3))
            h0, u0, v0 = (path_ref[step, f, prior] for f in range(3))
            h2, u2, v2 = (path_ref[step, f, follow] for f in range(3))
            hn, un, vn = below(h, h2), below(u, u2), below(v, v2)
            hs, us, vs = above(h, h0), above(u, u0), above(v, v0)
            land = land_ref[at]
            half = advect / 2.0
            dh = diffuse * h
            fx = half * ((1.0 + h) * u)
            gy = half * ((1.0 + hn) * vn - (1.0 + hs) * vs)
            keep = 1.0 - 4.0 * diffuse
            h_new = keep * h + diffuse * (hn + hs) - gy + east(dh - fx) + west(dh + fx)
            du = diffuse * u
            sx = half * h
            u_new = land * (
                keep * u + coriolis * v + diffuse * (un + us) + east(du - sx) + west(du + sx)
            )
            v_new = land * (
                keep * v
                - coriolis * u
                + diffuse * (vn + vs + east(v) + west(v))
                - half * (hn - hs)
            )
            number = base + i * BLK + lax.broadcasted_iota(jnp.int32, (BLK, columns), 0)
            inside = (number >= 0) & (number < grid_rows)
            h_new = jnp.where(inside, h_new, 0.0)
            path_ref[step + 1, 0, at] = h_new
            path_ref[step + 1, 1, at] = u_new
            path_ref[step + 1, 2, at] = v_new
    ends_ref[...] = path_ref[NSTEP, :, HALO : HALO + strip]


def adjoint_kernel(
    pos_ref, path_ref, land_ref, count_ref, total_ref, next_ref, rim_ref, out_ref, send_ref, work
):
    strip = out_ref.shape[1]
    rows = strip + 2 * HALO
    blocks = rows // BLK
    columns = out_ref.shape[2]
    base = pos_ref[0]
    grid_rows = pos_ref[1]
    weight = jnp.where(pos_ref[2] == 1, 0.0, defect_weight).astype(jnp.float32)
    half = advect / 2.0
    keep = 1.0 - 4.0 * diffuse

    def put(slot, step, i, lam):
        at = slice(i * BLK, (i + 1) * BLK)
        number = base + i * BLK + lax.broadcasted_iota(jnp.int32, (BLK, columns), 0)
        inside = (number >= 0) & (number < grid_rows)
        force = count_ref[step, at] * path_ref[step + 1, 0, at] - total_ref[step, at]
        land = land_ref[at]
        work[slot, 0, at] = jnp.where(inside, lam[0] + force, 0.0)
        work[slot, 1, at] = land * lam[1]
        work[slot, 2, at] = land * lam[2]

    for i in range(blocks):
        at = slice(i * BLK, (i + 1) * BLK)
        lam = []
        for f in range(3):
            if i == 0 or i == blocks - 1:
                ahead = rim_ref[f]
            else:
                ahead = next_ref[f, (i - 1) * BLK : i * BLK]
            lam.append(weight * (path_ref[NSTEP, f, at] - ahead))
        put(0, NSTEP - 1, i, lam)

    slot = 0
    for step in reversed(range(NSTEP)):
        inner = range(blocks) if step > 0 else range(1, blocks - 1)
        for i in inner:
            at = slice(i * BLK, (i + 1) * BLK)
            prior = slice(max(i - 1, 0) * BLK, (max(i - 1, 0) + 1) * BLK)
            follow = slice(min(i + 1, blocks - 1) * BLK, (min(i + 1, blocks - 1) + 1) * BLK)
            a, b, c = (work[slot, f, at] for f in range(3))
            a0, b0, c0 = (work[slot, f, prior] for f in range(3))
            a2, b2, c2 = (work[slot, f, follow] for f in range(3))
            an, bn, cn = below(a, a2), below(b, b2), below(c, c2)
            as_, bs, cs = above(a, a0), above(b, b0), above(c, c0)
            ae, aw = east(a), west(a)
            be, bw = east(b), west(b)
            ce, cw = east(c), west(c)
            h, u, v = (path_ref[step, f, at] for f in range(3))
            fx = half * (ae - aw)
            gy = half * (an - as_)
            depth = 1.0 + h
            lh = (
                keep * a
                + diffuse * (ae + aw + an + as_)
                + u * fx
                + v * gy
                + half * (be - bw + cn - cs)
            )
            lu = depth * fx + keep * b - coriolis * c + diffuse * (be + bw + bn + bs)
            lv = depth * gy + keep * c + coriolis * b + diffuse * (ce + cw + cn + cs)
            if step > 0:
                put(1 - slot, step - 1, i, (lh, lu, lv))
            else:
                here = slice((i - 1) * BLK, i * BLK)
                for f, (lam, x) in enumerate(((lh, h), (lu, u), (lv, v))):
                    out_ref[f, here] = lam
                    send_ref[f, here] = (
                        1.0 - step_length * defect_weight
                    ) * x - step_length * lam
        slot = 1 - slot


def shifted(block, axis, distance):
    devices = range(lax.axis_size(axis))
    route = [(i - distance, i) for i in devices if i - distance in devices]
    return lax.ppermute(block, axis, route)


def local(states, background, obs_cells, obs_values, land_mask):
    strip, columns = states.shape[2], states.shape[3]
    rows = strip + 2 * HALO
    at_first = lax.axis_index("tm") == 0
    at_final = lax.axis_index("tm") == lax.axis_size("tm") - 1
    base = lax.axis_index("space") * strip - HALO
    pos = jnp.stack(
        [base, jnp.int32(strip) * lax.axis_size("space"), at_final.astype(jnp.int32)]
    ).astype(jnp.int32)
    f32 = jnp.float32
    params = pltpu.CompilerParams(vmem_limit_bytes=VMEM_LIMIT)

    ahead = shifted(states[0], "tm", -1)
    top = jnp.concatenate([states[0, :, :HALO], land_mask[None, :HALO].astype(f32)])
    bottom = jnp.concatenate(
        [states[0, :, strip - HALO :], land_mask[None, strip - HALO :].astype(f32)]
    )
    up = shifted(bottom, "space", 1)
    down = shifted(top, "space", -1)

    half_rows = lax.broadcasted_iota(jnp.int32, (3, HALO, columns), 1) < HALO // 2
    rim = shifted(jnp.where(half_rows, down[:3], up[:3]), "tm", -1)

    count, total = pl.pallas_call(
        maps_kernel,
        out_shape=(
            jax.ShapeDtypeStruct((NSTEP, rows, columns), f32),
            jax.ShapeDtypeStruct((NSTEP, rows, columns), f32),
        ),
        in_specs=[smem(), vmem(), vmem()],
        out_specs=(vmem(), vmem()),
        compiler_params=params,
        name="maps",
    )(pos, obs_cells, obs_values)

    path, land, ends = pl.pallas_call(
        forward_kernel,
        out_shape=(
            jax.ShapeDtypeStruct((NSTEP + 1, 3, rows, columns), f32),
            jax.ShapeDtypeStruct((rows, columns), f32),
            jax.ShapeDtypeStruct((3, strip, columns), f32),
        ),
        in_specs=[smem()] + [vmem()] * 4,
        out_specs=(vmem(), vmem(), vmem()),
        compiler_params=params,
        name="forward",
    )(pos, states, up, down, land_mask)

    previous = shifted(ends, "tm", 1)

    adjoint, send = pl.pallas_call(
        adjoint_kernel,
        out_shape=(
            jax.ShapeDtypeStruct((3, strip, columns), f32),
            jax.ShapeDtypeStruct((3, strip, columns), f32),
        ),
        in_specs=[smem()] + [vmem()] * 6,
        out_specs=(vmem(), vmem()),
        scratch_shapes=[pltpu.VMEM((2, 3, rows, columns), f32)],
        compiler_params=params,
        name="adjoint",
    )(pos, path, land, count, total, ahead, rim)

    arriving = shifted(send, "tm", -1)
    previous = jnp.where(at_first, background, previous)
    gradient = defect_weight * (states[0] - previous) + adjoint
    share = jnp.where(at_final, 1.0, step_length * defect_weight).astype(f32)
    next_state = arriving + share * ends
    return (gradient[None], next_state[None])


def solution(mesh):
    in_specs = (
        P("tm", None, "space", None),
        P(None, "space", None),
        P("tm", None, None),
        P("tm", None, None),
        P("space", None),
    )
    out_specs = (P("tm", None, "space", None), P("tm", None, "space", None))
    return jax.shard_map(local, mesh=mesh, in_specs=in_specs, out_specs=out_specs, check_vma=False)
```

profile of v0, /device:TPU:25, one launch (start us, length us, event | category | flops | bytes accessed | tf_op | source)
XLA Modules:
  0.0 72.4 jit_solution(14892610360676292611)
XLA Ops:
  0.6 0.0 copy-start
  0.6 0.0 copy-start.2
  0.6 0.0 copy-start.3
  0.7 10.3 %collective-permute-start.3 = (f32[3,64,1024]{2,1,0:T(8,128)}, f32[3,64,1024]{2,1,0:T(8,128)S(1)}, u32[]{:S(2)}, u32[]{:S(2)}) collective-permute-start(f32[3,64,1024]{2,1,0:T(8,128)} %bitcast.16), channel_id=1, source_target_pairs={{4,0},{8,4},{12,8},{16,12},{20,16},{24,20},{28,24},{32,28},{36,32}... | collective-permute-start | bytes 2359304 | tf_op jit(solution)/shard_map/ppermute | solution.py:216
  10.9 1.0 %slice_bitcast_fusion = (f32[3,8,1024]{2,1,0:T(8,128)S(1)}, f32[3,8,1024]{2,1,0:T(8,128)S(1)}) fusion(f32[1,3,64,1024]{3,2,1,0:T(8,128)} %states_ref.1), kind=kLoop, calls=%fused_computation.5 | loop fusion | bytes 393216 | tf_op jit(solution)/shard_map/squeeze | solution.py:232
  11.9 0.8 %convert_bitcast_fusion = (f32[1,8,1024]{2,1,0:T(8,128)S(1)}, f32[1,8,1024]{2,1,0:T(8,128)S(1)}) fusion(s32[64,1024]{1,0:T(8,128)} %mask_ref.1), kind=kLoop, calls=%fused_computation.7 | loop fusion | flops 16384 | bytes 131072 | tf_op jit(solution)/shard_map/convert_element_type | solution.py:232
  12.7 3.1 %collective-permute-start = (f32[4,8,1024]{2,1,0:T(8,128)S(1)}, f32[4,8,1024]{2,1,0:T(8,128)S(1)}, u32[]{:S(2)}, u32[]{:S(2)}) collective-permute-start(f32[4,8,1024]{2,1,0:T(8,128)S(1)} %pad_maximum_fusion), channel_id=1, source_target_pairs={{0,1},{1,2},{2,3},{4,5},{5,6},{6,7},{8,9},{9,10},{10,11},{12,13},{... | collective-permute-start | bytes 393224 | tf_op jit(solution)/shard_map/ppermute | solution.py:216
  15.8 1.9 %collective-permute-start.1 = (f32[4,8,1024]{2,1,0:T(8,128)S(1)}, f32[4,8,1024]{2,1,0:T(8,128)S(1)}, u32[]{:S(2)}, u32[]{:S(2)}) collective-permute-start(f32[4,8,1024]{2,1,0:T(8,128)S(1)} %pad_maximum_fusion.1), channel_id=1, source_target_pairs={{1,0},{2,1},{3,2},{5,4},{6,5},{7,6},{9,8},{10,9},{11,10},{13,12},{... | collective-permute-start | bytes 393224 | tf_op jit(solution)/shard_map/ppermute | solution.py:216
  17.7 0.1 pad_add_fusion.pos_ref
  17.8 0.0 collective-permute-done.up_ref
  17.8 4.6 %collective-permute-done.1.down_ref = f32[4,8,1024]{2,1,0:T(8,128)S(1)} collective-permute-done((f32[4,8,1024]{2,1,0:T(8,128)S(1)}, f32[4,8,1024]{2,1,0:T(8,128)S(1)}, u32[]{:S(2)}, u32[]{:S(2)}) %collective-permute-start.1) | collective-permute-done | bytes 131104 | tf_op jit(solution)/shard_map/ppermute | solution.py:216
  22.4 0.0 copy-done
  22.4 0.0 copy-start.1
  22.4 0.9 %copy-done.1 = s32[64,1024]{1,0:T(8,128)S(1)} copy-done((s32[64,1024]{1,0:T(8,128)S(1)}, s32[64,1024]{1,0:T(8,128)}, u32[]{:S(2)}) %copy-start.1) | copy-done | bytes 262168
  23.3 5.7 %forward.1 = (f32[5,3,80,1024]{3,2,1,0:T(8,128)}, f32[80,1024]{1,0:T(8,128)S(1)}, f32[3,64,1024]{2,1,0:T(8,128)S(1)}) custom-call(s32[3]{0:T(128)S(1)} %pad_add_fusion.pos_ref, f32[1,3,64,1024]{3,2,1,0:T(8,128)S(1)} %copy-done, f32[4,8,1024]{2,1,0:T(8,128)S(1)} %collective-permute-done.up_ref, f32[4,8,1024]{2,1,0:T(8,128)S(1)} %collective-permute-done.1.down_ref, ...), custom_call_target="tpu_custom_call" | custom-call | tf_op jit(solution)/shard_map/forward/pallas_call | solution.py:254
  29.0 1.9 %collective-permute-start.2 = (f32[3,64,1024]{2,1,0:T(8,128)S(1)}, f32[3,64,1024]{2,1,0:T(8,128)}, u32[]{:S(2)}, u32[]{:S(2)}) collective-permute-start(f32[3,64,1024]{2,1,0:T(8,128)S(1)} %get-tuple-element.9), channel_id=1, source_target_pairs={{0,4},{4,8},{8,12},{12,16},{16,20},{20,24},{24,28},{28,32},{32,36}... | collective-permute-start | bytes 2359304 | tf_op jit(solution)/shard_map/ppermute | solution.py:216
  30.9 0.1 slice_select_fusion
  31.0 14.4 %collective-permute-start.4 = (f32[3,8,1024]{2,1,0:T(8,128)S(1)}, f32[3,8,1024]{2,1,0:T(8,128)S(1)}, u32[]{:S(2)}, u32[]{:S(2)}) collective-permute-start(f32[3,8,1024]{2,1,0:T(8,128)S(1)} %slice_select_fusion), channel_id=1, source_target_pairs={{4,0},{8,4},{12,8},{16,12},{20,16},{24,20},{28,24},{32,28},{36,32}... | collective-permute-start | bytes 294920 | tf_op jit(solution)/shard_map/ppermute | solution.py:216
  45.4 0.0 copy-done.2
  45.4 0.0 copy-done.3
  45.5 3.5 %maps.1 = (f32[4,80,1024]{2,1,0:T(8,128)S(1)}, f32[4,80,1024]{2,1,0:T(8,128)S(1)}) custom-call(s32[3]{0:T(128)S(1)} %pad_add_fusion.pos_ref, s32[1,4,1024]{2,1,0:T(4,128)S(1)} %copy-done.2, f32[1,4,1024]{2,1,0:T(4,128)S(1)} %copy-done.3), custom_call_target="tpu_custom_call" | custom-call | tf_op jit(solution)/shard_map/maps/pallas_call | solution.py:242
  48.9 0.0 collective-permute-done.4.rim_ref
  48.9 0.0 collective-permute-done.3.next_ref
  48.9 6.4 %adjoint.1 = (f32[3,64,1024]{2,1,0:T(8,128)S(1)}, f32[3,64,1024]{2,1,0:T(8,128)}) custom-call(s32[3]{0:T(128)S(1)} %pad_add_fusion.pos_ref, f32[5,3,80,1024]{3,2,1,0:T(8,128)} %get-tuple-element.10.path_ref, f32[80,1024]{1,0:T(8,128)S(1)} %get-tuple-element.11.land_ref, f32[4,80,1024]{2,1,0:T(8,128)S(1)} %get-tuple-element.12.count_ref, ...), custom_call_target="tpu_custom_call" | custom-call | tf_op jit(solution)/shard_map/adjoint/pallas_call | solution.py:269
  55.4 6.4 %collective-permute-start.5 = (f32[3,64,1024]{2,1,0:T(8,128)}, f32[3,64,1024]{2,1,0:T(8,128)S(1)}, u32[]{:S(2)}, u32[]{:S(2)}) collective-permute-start(f32[3,64,1024]{2,1,0:T(8,128)} %get-tuple-element.15), channel_id=1, source_target_pairs={{4,0},{8,4},{12,8},{16,12},{20,16},{24,20},{28,24},{32,28},{36,32}... | collective-permute-start | bytes 2359304 | tf_op jit(solution)/shard_map/ppermute | solution.py:216
  61.7 0.0 collective-permute-done.2
  61.7 2.3 %add_bitcast_fusion.1 = f32[1,3,64,1024]{3,2,1,0:T(8,128)} fusion(f32[3,64,1024]{2,1,0:T(8,128)S(1)} %get-tuple-element.14, f32[3,64,1024]{2,1,0:T(8,128)} %param.6, f32[3,64,1024]{2,1,0:T(8,128)} %collective-permute-done.2, pred[]{:T(512)S(6)} %eq.6, f32[1,3,64,1024]{3,2,1,0:T(8,128)S(1)} %copy-done), kind=kLoop, calls=%fused_computation.1 | loop fusion | flops 786432 | bytes 3932161 | tf_op jit(solution)/shard_map/broadcast_in_dim | solution.py:287
  64.0 7.3 %collective-permute-done.5 = f32[3,64,1024]{2,1,0:T(8,128)S(1)} collective-permute-done((f32[3,64,1024]{2,1,0:T(8,128)}, f32[3,64,1024]{2,1,0:T(8,128)S(1)}, u32[]{:S(2)}, u32[]{:S(2)}) %collective-permute-start.5) | collective-permute-done | bytes 786464 | tf_op jit(solution)/shard_map/ppermute | solution.py:216
  71.4 1.0 %add_bitcast_fusion = f32[1,3,64,1024]{3,2,1,0:T(8,128)} fusion(f32[3,64,1024]{2,1,0:T(8,128)S(1)} %collective-permute-done.5, f32[3,64,1024]{2,1,0:T(8,128)S(1)} %get-tuple-element.9, f32[]{:T(128)S(6)} %select_n.19), kind=kLoop, calls=%fused_computation | loop fusion | flops 393216 | bytes 2359300 | tf_op jit(solution)/shard_map/broadcast_in_dim | solution.py:287
  (3 shorter events, 0.0 us)
Async XLA Ops:
  0.6 21.7 %copy-start = (f32[1,3,64,1024]{3,2,1,0:T(8,128)S(1)}, f32[1,3,64,1024]{3,2,1,0:T(8,128)}, u32[]{:S(2)}) copy-start(f32[1,3,64,1024]{3,2,1,0:T(8,128)} %states_ref.1) | copy-start | bytes 2359300
  0.6 44.8 %copy-start.2 = (s32[1,4,1024]{2,1,0:T(4,128)S(1)}, s32[1,4,1024]{2,1,0:T(4,128)}, u32[]{:S(2)}) copy-start(s32[1,4,1024]{2,1,0:T(4,128)} %cells_ref.1) | copy-start | bytes 49156
  0.6 44.8 %copy-start.3 = (f32[1,4,1024]{2,1,0:T(4,128)S(1)}, f32[1,4,1024]{2,1,0:T(4,128)}, u32[]{:S(2)}) copy-start(f32[1,4,1024]{2,1,0:T(4,128)} %values_ref.1) | copy-start | bytes 49156
  0.7 48.3 %collective-permute-start.3 = (f32[3,64,1024]{2,1,0:T(8,128)}, f32[3,64,1024]{2,1,0:T(8,128)S(1)}, u32[]{:S(2)}, u32[]{:S(2)}) collective-permute-start(f32[3,64,1024]{2,1,0:T(8,128)} %bitcast.16), channel_id=1, source_target_pairs={{4,0},{8,4},{12,8},{16,12},{20,16},{24,20},{28,24},{32,28},{36,32}... | collective-permute-start | bytes 2359304 | tf_op jit(solution)/shard_map/ppermute | solution.py:216
  12.7 5.1 %collective-permute-start = (f32[4,8,1024]{2,1,0:T(8,128)S(1)}, f32[4,8,1024]{2,1,0:T(8,128)S(1)}, u32[]{:S(2)}, u32[]{:S(2)}) collective-permute-start(f32[4,8,1024]{2,1,0:T(8,128)S(1)} %pad_maximum_fusion), channel_id=1, source_target_pairs={{0,1},{1,2},{2,3},{4,5},{5,6},{6,7},{8,9},{9,10},{10,11},{12,13},{... | collective-permute-start | bytes 393224 | tf_op jit(solution)/shard_map/ppermute | solution.py:216
  15.8 6.6 %collective-permute-start.1 = (f32[4,8,1024]{2,1,0:T(8,128)S(1)}, f32[4,8,1024]{2,1,0:T(8,128)S(1)}, u32[]{:S(2)}, u32[]{:S(2)}) collective-permute-start(f32[4,8,1024]{2,1,0:T(8,128)S(1)} %pad_maximum_fusion.1), channel_id=1, source_target_pairs={{1,0},{2,1},{3,2},{5,4},{6,5},{7,6},{9,8},{10,9},{11,10},{13,12},{... | collective-permute-start | bytes 393224 | tf_op jit(solution)/shard_map/ppermute | solution.py:216
  22.4 1.0 %copy-start.1 = (s32[64,1024]{1,0:T(8,128)S(1)}, s32[64,1024]{1,0:T(8,128)}, u32[]{:S(2)}) copy-start(s32[64,1024]{1,0:T(8,128)} %mask_ref.1) | copy-start | bytes 786436
  29.0 32.7 %collective-permute-start.2 = (f32[3,64,1024]{2,1,0:T(8,128)S(1)}, f32[3,64,1024]{2,1,0:T(8,128)}, u32[]{:S(2)}, u32[]{:S(2)}) collective-permute-start(f32[3,64,1024]{2,1,0:T(8,128)S(1)} %get-tuple-element.9), channel_id=1, source_target_pairs={{0,4},{4,8},{8,12},{12,16},{16,20},{20,24},{24,28},{28,32},{32,36}... | collective-permute-start | bytes 2359304 | tf_op jit(solution)/shard_map/ppermute | solution.py:216
  31.0 17.9 %collective-permute-start.4 = (f32[3,8,1024]{2,1,0:T(8,128)S(1)}, f32[3,8,1024]{2,1,0:T(8,128)S(1)}, u32[]{:S(2)}, u32[]{:S(2)}) collective-permute-start(f32[3,8,1024]{2,1,0:T(8,128)S(1)} %slice_select_fusion), channel_id=1, source_target_pairs={{4,0},{8,4},{12,8},{16,12},{20,16},{24,20},{28,24},{32,28},{36,32}... | collective-permute-start | bytes 294920 | tf_op jit(solution)/shard_map/ppermute | solution.py:216
  55.4 16.0 %collective-permute-start.5 = (f32[3,64,1024]{2,1,0:T(8,128)}, f32[3,64,1024]{2,1,0:T(8,128)S(1)}, u32[]{:S(2)}, u32[]{:S(2)}) collective-permute-start(f32[3,64,1024]{2,1,0:T(8,128)} %get-tuple-element.15), channel_id=1, source_target_pairs={{4,0},{8,4},{12,8},{16,12},{20,16},{24,20},{28,24},{32,28},{36,32}... | collective-permute-start | bytes 2359304 | tf_op jit(solution)/shard_map/ppermute | solution.py:216
where the time goes:
time: 72.8 us; the launch traced here: 72.4 us
  starting transfers between devices  37.9 us (52%)
  Pallas kernels  15.6 us (21%)
  waiting for transfers between devices  11.9 us (16%)
  other arithmetic  4.26 us (6%)
  local copies, waits for them, and re-layouts  1.92 us (3%)
  between operations  0.8 us (1%)
    ppermute x6, starting transfers between devices, shifted(): return lax.ppermute(block, axis, route)  37.9 us
    ppermute x6, waiting for transfers between devices, shifted(): return lax.ppermute(block, axis, route)  11.9 us
    pallas_call x1, Pallas kernels, local(): pl.pallas_call(adjoint_kernel, out_shape=(jax.ShapeDtypeStruct((3, strip,...  6.42 us
    pallas_call x1, Pallas kernels, local(): pl.pallas_call(forward_kernel, out_shape=(jax.ShapeDtypeStruct((NSTEP + 1...  5.71 us
    pallas_call x1, Pallas kernels, local(): pl.pallas_call(maps_kernel, out_shape=(jax.ShapeDtypeStruct((NSTEP, rows,...  3.45 us
    broadcast_in_dim x2, other arithmetic, local(): return (gradient[None], next_state[None])  3.29 us
  transfers between devices with their start and end apart: 6, of which 2 were waited for; matrix products, arithmetic and copies ran while one was open for 6% of the time, Pallas kernels for 22%

commit v1 on v0

v1 whole, which is shorter than its diff:
```python
import jax
import jax.numpy as jnp
from jax import lax
from jax.experimental import pallas as pl
from jax.experimental.pallas import tpu as pltpu
from jax.sharding import PartitionSpec as P

NSTEP = 4
HALO = 8
BLK = 8

advect = 0.25
coriolis = 0.1
diffuse = 0.1
defect_weight = 2.0
obs_weight = 4.0
step_length = 0.1


def vmem():
    return pl.BlockSpec(memory_space=pltpu.VMEM)


def smem():
    return pl.BlockSpec(memory_space=pltpu.SMEM)


def east(x):
    return pltpu.roll(x, x.shape[1] - 1, axis=1)


def west(x):
    return pltpu.roll(x, 1, axis=1)


def below(x, after):
    first = lax.broadcasted_iota(jnp.int32, x.shape, 0) == 0
    return pltpu.roll(jnp.where(first, after, x), BLK - 1, axis=0)


def above(x, before):
    last = lax.broadcasted_iota(jnp.int32, x.shape, 0) == BLK - 1
    return pltpu.roll(jnp.where(last, before, x), 1, axis=0)


def maps_kernel(pos_ref, cells_ref, values_ref, count_ref, total_ref):
    rows, columns = count_ref.shape[1:]
    observed = cells_ref.shape[2]
    shift = columns.bit_length() - 1
    assert columns == 1 << shift
    width = 256
    base = pos_ref[0]
    row_iota = lax.broadcasted_iota(jnp.int32, (rows, observed), 0)
    col_iota = lax.broadcasted_iota(jnp.int32, (width, observed), 0)
    for step in range(NSTEP):
        cells = cells_ref[0, step : step + 1, :]
        values = obs_weight * values_ref[0, step : step + 1, :]
        row = lax.shift_right_logical(cells, shift)
        col = cells - lax.shift_left(row, shift)
        inside = row_iota == row - base
        first = values.astype(jnp.bfloat16).astype(jnp.float32)
        rest = values - first
        second = rest.astype(jnp.bfloat16).astype(jnp.float32)
        third = rest - second
        zero = jnp.zeros((rows, observed), jnp.float32)
        parts = [
            jnp.where(inside, jnp.broadcast_to(part, (rows, observed)), zero).astype(jnp.bfloat16)
            for part in (first, second, third)
        ]
        picks = jnp.where(inside, jnp.float32(obs_weight), zero).astype(jnp.bfloat16)
        left = jnp.concatenate([picks] + parts, axis=0)
        for start in range(0, columns, width):
            hot = jnp.where(col_iota == col - start, jnp.float32(1), jnp.float32(0))
            hot = hot.astype(jnp.bfloat16)
            out = lax.dot_general(
                left, hot, (((1,), (1,)), ((), ())), preferred_element_type=jnp.float32
            )
            count_ref[step, :, start : start + width] = out[:rows]
            total_ref[step, :, start : start + width] = (
                out[rows : 2 * rows] + out[2 * rows : 3 * rows] + out[3 * rows :]
            )


def forward_kernel(
    pos_ref, states_ref, up_ref, down_ref, mask_ref, count_ref, land_ref, ends_ref, *path_ref
):
    strip = states_ref.shape[2]
    rows = strip + 2 * HALO
    blocks = rows // BLK
    columns = states_ref.shape[3]
    base = pos_ref[0]
    grid_rows = pos_ref[1]
    path_ref[0][:, :HALO] = up_ref[:3]
    path_ref[0][:, HALO : HALO + strip] = states_ref[0]
    path_ref[0][:, HALO + strip :] = down_ref[:3]
    land_ref[:HALO] = up_ref[3]
    land_ref[HALO : HALO + strip] = mask_ref[...].astype(jnp.float32)
    land_ref[HALO + strip :] = down_ref[3]

    for step in range(NSTEP):
        for i in range(blocks):
            at = slice(i * BLK, (i + 1) * BLK)
            prior = slice(max(i - 1, 0) * BLK, (max(i - 1, 0) + 1) * BLK)
            follow = slice(min(i + 1, blocks - 1) * BLK, (min(i + 1, blocks - 1) + 1) * BLK)
            h, u, v = (path_ref[step][f, at] for f in range(3))
            h0, u0, v0 = (path_ref[step][f, prior] for f in range(3))
            h2, u2, v2 = (path_ref[step][f, follow] for f in range(3))
            hn, un, vn = below(h, h2), below(u, u2), below(v, v2)
            hs, us, vs = above(h, h0), above(u, u0), above(v, v0)
            land = land_ref[at]
            half = advect / 2.0
            dh = diffuse * h
            fx = half * ((1.0 + h) * u)
            gy = half * ((1.0 + hn) * vn - (1.0 + hs) * vs)
            keep = 1.0 - 4.0 * diffuse
            h_new = keep * h + diffuse * (hn + hs) - gy + east(dh - fx) + west(dh + fx)
            du = diffuse * u
            sx = half * h
            u_new = land * (
                keep * u + coriolis * v + diffuse * (un + us) + east(du - sx) + west(du + sx)
            )
            v_new = land * (
                keep * v
                - coriolis * u
                + diffuse * (vn + vs + east(v) + west(v))
                - half * (hn - hs)
            )
            number = base + i * BLK + lax.broadcasted_iota(jnp.int32, (BLK, columns), 0)
            inside = (number >= 0) & (number < grid_rows)
            h_new = jnp.where(inside, h_new, 0.0)
            path_ref[step + 1][0, at] = h_new
            path_ref[step + 1][1, at] = u_new
            path_ref[step + 1][2, at] = v_new
    ends_ref[...] = path_ref[NSTEP][:, HALO : HALO + strip]


def adjoint_kernel(part):
    def kernel(*refs):
        if part == "middle":
            pos_ref, land_ref, count_ref, total_ref, *path_ref = refs[: NSTEP + 5]
            next_ref, out_ref, send_ref, work = refs[NSTEP + 5 :]
        else:
            pos_ref, land_ref, count_ref, total_ref, *path_ref = refs[: NSTEP + 5]
            rim_ref, work_ref, out_ref, send_ref, work = refs[NSTEP + 5 :]
        rows, columns = land_ref.shape
        blocks = rows // BLK
        base = pos_ref[0]
        grid_rows = pos_ref[1]
        weight = jnp.where(pos_ref[2] == 1, 0.0, defect_weight).astype(jnp.float32)
        half = advect / 2.0
        keep = 1.0 - 4.0 * diffuse
        edge = (0, 1, blocks - 2, blocks - 1)
        if part == "middle":
            first = range(1, blocks - 1)
            inner = range(1, blocks - 1)
            final = range(2, blocks - 2)
        else:
            first = (0, blocks - 1)
            inner = edge
            final = (1, blocks - 2)

        def get(step, f, i):
            at = slice(i * BLK, (i + 1) * BLK)
            if part == "edge" and (i not in edge or (step == NSTEP - 1 and i in (1, blocks - 2))):
                return work_ref[step, f, at]
            return work[step, f, at]

        def put(step, i, lam):
            at = slice(i * BLK, (i + 1) * BLK)
            number = base + i * BLK + lax.broadcasted_iota(jnp.int32, (BLK, columns), 0)
            inside = (number >= 0) & (number < grid_rows)
            force = count_ref[step, at] * path_ref[step + 1][0, at] - total_ref[step, at]
            land = land_ref[at]
            work[step, 0, at] = jnp.where(inside, lam[0] + force, 0.0)
            work[step, 1, at] = land * lam[1]
            work[step, 2, at] = land * lam[2]

        for i in first:
            at = slice(i * BLK, (i + 1) * BLK)
            if part == "middle":
                ahead = [next_ref[f, (i - 1) * BLK : i * BLK] for f in range(3)]
            else:
                ahead = [rim_ref[f] for f in range(3)]
            put(
                NSTEP - 1,
                i,
                [weight * (path_ref[NSTEP][f, at] - ahead[f]) for f in range(3)],
            )

        for step in reversed(range(NSTEP)):
            for n, i in enumerate(inner if step > 0 else final):
                at = slice(i * BLK, (i + 1) * BLK)
                before, after = max(i - 1, first[0]), min(i + 1, first[-1])
                a, b, c = (get(step, f, i) for f in range(3))
                a0, b0, c0 = (get(step, f, before) for f in range(3))
                a2, b2, c2 = (get(step, f, after) for f in range(3))
                an, bn, cn = below(a, a2), below(b, b2), below(c, c2)
                as_, bs, cs = above(a, a0), above(b, b0), above(c, c0)
                ae, aw = east(a), west(a)
                be, bw = east(b), west(b)
                ce, cw = east(c), west(c)
                h, u, v = (path_ref[step][f, at] for f in range(3))
                fx = half * (ae - aw)
                gy = half * (an - as_)
                depth = 1.0 + h
                lh = (
                    keep * a
                    + diffuse * (ae + aw + an + as_)
                    + u * fx
                    + v * gy
                    + half * (be - bw + cn - cs)
                )
                lu = depth * fx + keep * b - coriolis * c + diffuse * (be + bw + bn + bs)
                lv = depth * gy + keep * c + coriolis * b + diffuse * (ce + cw + cn + cs)
                if step > 0:
                    put(step - 1, i, (lh, lu, lv))
                else:
                    here = slice(n * BLK, (n + 1) * BLK)
                    for f, (lam, x) in enumerate(((lh, h), (lu, u), (lv, v))):
                        out_ref[f, here] = lam
                        send_ref[f, here] = (
                            1.0 - step_length * defect_weight
                        ) * x - step_length * lam

    return kernel


def shifted(block, axis, distance):
    devices = range(lax.axis_size(axis))
    route = [(i - distance, i) for i in devices if i - distance in devices]
    return lax.ppermute(block, axis, route)


def local(states, background, obs_cells, obs_values, land_mask):
    strip, columns = states.shape[2], states.shape[3]
    rows = strip + 2 * HALO
    at_first = lax.axis_index("tm") == 0
    at_final = lax.axis_index("tm") == lax.axis_size("tm") - 1
    base = lax.axis_index("space") * strip - HALO
    pos = jnp.stack(
        [base, jnp.int32(strip) * lax.axis_size("space"), at_final.astype(jnp.int32)]
    ).astype(jnp.int32)
    f32 = jnp.float32

    def params(megabytes):
        return pltpu.CompilerParams(vmem_limit_bytes=megabytes * 1024 * 1024)

    def cost(us):
        return pl.CostEstimate(
            flops=1000, transcendentals=0, bytes_accessed=int(us * 3.0e6)
        )

    top = jnp.concatenate([states[0, :, :HALO], land_mask[None, :HALO].astype(f32)])
    bottom = jnp.concatenate(
        [states[0, :, strip - HALO :], land_mask[None, strip - HALO :].astype(f32)]
    )
    share = jnp.where(at_final, 1.0, step_length * defect_weight).astype(f32)
    top, bottom, moving, pos, at_first, share = lax.optimization_barrier(
        (top, bottom, states[0], pos, at_first, share)
    )
    up = shifted(bottom, "space", 1)
    down = shifted(top, "space", -1)
    ahead = shifted(moving, "tm", -1)

    count, total = pl.pallas_call(
        maps_kernel,
        out_shape=(
            jax.ShapeDtypeStruct((NSTEP, rows, columns), f32),
            jax.ShapeDtypeStruct((NSTEP, rows, columns), f32),
        ),
        in_specs=[smem(), vmem(), vmem()],
        out_specs=(vmem(), vmem()),
        compiler_params=params(16),
        cost_estimate=cost(3.5),
        name="maps",
    )(pos, obs_cells, obs_values)

    half_rows = lax.broadcasted_iota(jnp.int32, (3, HALO, columns), 1) < HALO // 2
    rim = jnp.where(half_rows, down[:3], up[:3])
    rim, up, down = lax.optimization_barrier((rim, up, down))
    rim = shifted(rim, "tm", -1)

    land, ends, *path = pl.pallas_call(
        forward_kernel,
        out_shape=(
            jax.ShapeDtypeStruct((rows, columns), f32),
            jax.ShapeDtypeStruct((3, strip, columns), f32),
        )
        + (jax.ShapeDtypeStruct((3, rows, columns), f32),) * (NSTEP + 1),
        in_specs=[smem()] + [vmem()] * 4 + [pl.BlockSpec(memory_space=pl.ANY)],
        out_specs=(vmem(),) * (NSTEP + 3),
        compiler_params=params(16),
        cost_estimate=cost(5),
        name="forward",
    )(pos, states, up, down, land_mask, count)

    previous = shifted(ends, "tm", 1)

    def adjoint(part, height, *operands):
        shapes = [jax.ShapeDtypeStruct((3, height, columns), f32)] * 2
        scratch = [pltpu.VMEM((NSTEP, 3, rows, columns), f32)]
        if part == "middle":
            shapes.append(jax.ShapeDtypeStruct((NSTEP, 3, rows, columns), f32))
            scratch = []
        return pl.pallas_call(
            adjoint_kernel(part),
            out_shape=tuple(shapes),
            in_specs=[smem()] + [vmem()] * len(operands),
            out_specs=(vmem(),) * len(shapes),
            scratch_shapes=scratch,
            compiler_params=params(24),
            cost_estimate=cost(4 if part == "middle" else 2),
            name="adjoint_" + part,
        )(pos, *operands)

    shared = (land, count, total, *path)
    mid_adj, mid_send, work = adjoint("middle", strip - 2 * BLK, *shared, ahead)
    mid_next = shifted(mid_send, "tm", -1)
    edge_adj, edge_send = adjoint("edge", 2 * BLK, *shared, rim, work)
    edge_next = shifted(edge_send, "tm", -1)

    def joined(middle, edge):
        return jnp.concatenate([edge[:, :BLK], middle, edge[:, BLK:]], axis=1)

    previous = jnp.where(at_first, background, previous)
    gradient = defect_weight * (states[0] - previous) + joined(mid_adj, edge_adj)
    next_state = joined(mid_next, edge_next) + share * ends
    return (gradient[None], next_state[None])


def solution(mesh):
    in_specs = (
        P("tm", None, "space", None),
        P(None, "space", None),
        P("tm", None, None),
        P("tm", None, None),
        P("space", None),
    )
    out_specs = (P("tm", None, "space", None), P("tm", None, "space", None))
    return jax.shard_map(local, mesh=mesh, in_specs=in_specs, out_specs=out_specs, check_vma=False)
```

time: 72.8 us -> 64.8 us (0.89)
  the two profiles are of different devices: /device:TPU:25 before, /device:TPU:24 now
where the time goes in v1:
time: 64.8 us; the launch traced here: 64.1 us
  starting transfers between devices  32.5 us (50%)
  waiting for transfers between devices  13 us (20%)
  Pallas kernels  12 us (19%)
  other arithmetic  3.23 us (5%)
  local copies, waits for them, and re-layouts  2.43 us (4%)
  between operations  0.84 us (1%)
    ppermute x7, starting transfers between devices, shifted(): return lax.ppermute(block, axis, route)  32.5 us
    ppermute x7, waiting for transfers between devices, shifted(): return lax.ppermute(block, axis, route)  13 us
    pallas_call x2, Pallas kernels, adjoint(): pl.pallas_call(adjoint_kernel(part), out_shape=tuple(shapes), in_specs=[s...  4.89 us
    pallas_call x1, Pallas kernels, local(): pl.pallas_call(forward_kernel, out_shape=(jax.ShapeDtypeStruct((rows, col...  3.66 us
    pallas_call x1, Pallas kernels, local(): pl.pallas_call(maps_kernel, out_shape=(jax.ShapeDtypeStruct((NSTEP, rows,...  3.45 us
    broadcast_in_dim x2, other arithmetic, local(): return (gradient[None], next_state[None])  2.19 us
    unnamed x10, local copies, waits for them, and re-layouts  1.45 us
  transfers between devices with their start and end apart: 7, of which 2 were waited for; matrix products, arithmetic and copies ran while one was open for 2% of the time, Pallas kernels for 19%

profile of v1, /device:TPU:24, one launch (start us, length us, event | category | flops | bytes accessed | tf_op | source)
XLA Modules:
  0.0 64.1 jit_solution(8301876290516875259)
XLA Ops:
  0.6 0.0 copy-start.1
  0.6 0.0 copy-start
  0.7 0.9 %convert_bitcast_fusion = (f32[1,8,1024]{2,1,0:T(8,128)S(1)}, f32[1,8,1024]{2,1,0:T(8,128)S(1)}) fusion(s32[64,1024]{1,0:T(8,128)} %mask_ref.1), kind=kLoop, calls=%fused_computation.9 | loop fusion | flops 16384 | bytes 131072 | tf_op jit(solution)/shard_map/convert_element_type | solution.py:255
  1.5 1.0 %slice_bitcast_fusion = (f32[3,8,1024]{2,1,0:T(8,128)S(1)}, f32[3,8,1024]{2,1,0:T(8,128)S(1)}) fusion(f32[1,3,64,1024]{3,2,1,0:T(8,128)} %states_ref.1), kind=kLoop, calls=%fused_computation.7 | loop fusion | bytes 393216 | tf_op jit(solution)/shard_map/squeeze | solution.py:255
  2.5 0.1 pad_add_fusion.pos_ref.refs_0_
  2.6 1.7 %collective-permute-start.1 = (f32[4,8,1024]{2,1,0:T(8,128)S(1)}, f32[4,8,1024]{2,1,0:T(8,128)S(1)}, u32[]{:S(2)}, u32[]{:S(2)}) collective-permute-start(f32[4,8,1024]{2,1,0:T(8,128)S(1)} %get-tuple-element.28), channel_id=1, source_target_pairs={{0,1},{1,2},{2,3},{4,5},{5,6},{6,7},{8,9},{9,10},{10,11},{12,13},{... | collective-permute-start | bytes 393224 | tf_op jit(solution)/shard_map/ppermute | solution.py:231
  4.3 1.3 %collective-permute-start = (f32[4,8,1024]{2,1,0:T(8,128)S(1)}, f32[4,8,1024]{2,1,0:T(8,128)S(1)}, u32[]{:S(2)}, u32[]{:S(2)}) collective-permute-start(f32[4,8,1024]{2,1,0:T(8,128)S(1)} %get-tuple-element.27), channel_id=1, source_target_pairs={{1,0},{2,1},{3,2},{5,4},{6,5},{7,6},{9,8},{10,9},{11,10},{13,12},{... | collective-permute-start | bytes 393224 | tf_op jit(solution)/shard_map/ppermute | solution.py:231
  5.6 10.4 %collective-permute-start.4 = (f32[3,64,1024]{2,1,0:T(8,128)}, f32[3,64,1024]{2,1,0:T(8,128)S(1)}, u32[]{:S(2)}, u32[]{:S(2)}) collective-permute-start(f32[3,64,1024]{2,1,0:T(8,128)} %bitcast.16), channel_id=1, source_target_pairs={{4,0},{8,4},{12,8},{16,12},{20,16},{24,20},{28,24},{32,28},{36,32}... | collective-permute-start | bytes 2359304 | tf_op jit(solution)/shard_map/ppermute | solution.py:231
  16.1 0.0 copy-start.2
  16.1 0.7 %copy-done.2 = s32[1,4,1024]{2,1,0:T(4,128)S(1)} copy-done((s32[1,4,1024]{2,1,0:T(4,128)S(1)}, s32[1,4,1024]{2,1,0:T(4,128)}, u32[]{:S(2)}) %copy-start.2) | copy-done | bytes 16408
  16.8 0.0 copy-start.3
  16.8 0.7 %copy-done.3 = f32[1,4,1024]{2,1,0:T(4,128)S(1)} copy-done((f32[1,4,1024]{2,1,0:T(4,128)S(1)}, f32[1,4,1024]{2,1,0:T(4,128)}, u32[]{:S(2)}) %copy-start.3) | copy-done | bytes 16408
  17.5 3.5 %maps.1 = (f32[4,80,1024]{2,1,0:T(8,128)S(1)}, f32[4,80,1024]{2,1,0:T(8,128)S(1)}) custom-call(s32[3]{0:T(128)S(1)} %pad_add_fusion.pos_ref.refs_0_, s32[1,4,1024]{2,1,0:T(4,128)S(1)} %copy-done.2, f32[1,4,1024]{2,1,0:T(4,128)S(1)} %copy-done.3), custom_call_target="tpu_custom_call" | custom-call | flops 1000 | bytes 10500000 | tf_op jit(solution)/shard_map/maps/pallas_call | solution.py:265
  21.0 0.0 collective-permute-done.1.up_ref
  21.0 0.0 collective-permute-done.down_ref
  21.0 0.1 slice_select_fusion
  21.1 0.0 copy-done.1
  21.1 0.0 copy-done
  21.1 3.7 %forward.1 = (f32[80,1024]{1,0:T(8,128)S(1)}, f32[3,64,1024]{2,1,0:T(8,128)S(1)}, f32[3,80,1024]{2,1,0:T(8,128)S(1)}, f32[3,80,1024]{2,1,0:T(8,128)S(1)}, f32[3,...) custom-call(s32[3]{0:T(128)S(1)} %pad_add_fusion.pos_ref.refs_0_, ...), custom_call_target="tpu_custom_call" | custom-call | flops 1000 | bytes 15000000 | tf_op jit(solution)/shard_map/forward/pallas_call | solution.py:283
  24.8 1.9 %collective-permute-start.2 = (f32[3,64,1024]{2,1,0:T(8,128)S(1)}, f32[3,64,1024]{2,1,0:T(8,128)S(1)}, u32[]{:S(2)}, u32[]{:S(2)}) collective-permute-start(f32[3,64,1024]{2,1,0:T(8,128)S(1)} %get-tuple-element.32), channel_id=1, source_target_pairs={{0,4},{4,8},{8,12},{12,16},{16,20},{20,24},{24,28},{28,32},{32,36}... | collective-permute-start | bytes 2359304 | tf_op jit(solution)/shard_map/ppermute | solution.py:231
  26.7 8.4 %collective-permute-start.3 = (f32[3,8,1024]{2,1,0:T(8,128)S(1)}, f32[3,8,1024]{2,1,0:T(8,128)S(1)}, u32[]{:S(2)}, u32[]{:S(2)}) collective-permute-start(f32[3,8,1024]{2,1,0:T(8,128)S(1)} %slice_select_fusion), channel_id=1, source_target_pairs={{4,0},{8,4},{12,8},{16,12},{20,16},{24,20},{28,24},{32,28},{36,32}... | collective-permute-start | bytes 294920 | tf_op jit(solution)/shard_map/ppermute | solution.py:231
  35.1 0.0 collective-permute-done.4.refs_9_
  35.1 3.2 %adjoint_middle.1 = (f32[3,48,1024]{2,1,0:T(8,128)S(1)}, f32[3,48,1024]{2,1,0:T(8,128)S(1)}, f32[4,3,80,1024]{3,2,1,0:T(8,128)S(1)}) custom-call(s32[3]{0:T(128)S(1)} %pad_add_fusion.pos_ref.refs_0_, f32[80,1024]{1,0:T(8,128)S(1)} %get-tuple-element.33.refs_1_, f32[4,80,1024]{2,1,0:T(8,128)S(1)} %get-tuple-element.31.count_ref.refs_2_, ...), custom_call_target="tpu_custom_call" | custom-call | flops 1000 | bytes 12000000 | tf_op jit(solution)/shard_map/adjoint_middle/pallas_call | solution.py:305
  38.3 6.8 %collective-permute-start.6 = (f32[3,48,1024]{2,1,0:T(8,128)S(1)}, f32[3,48,1024]{2,1,0:T(8,128)S(1)}, u32[]{:S(2)}, u32[]{:S(2)}) collective-permute-start(f32[3,48,1024]{2,1,0:T(8,128)S(1)} %get-tuple-element.46), channel_id=1, source_target_pairs={{4,0},{8,4},{12,8},{16,12},{20,16},{24,20},{28,24},{32,28},{36,32}... | collective-permute-start | bytes 1769480 | tf_op jit(solution)/shard_map/ppermute | solution.py:231
  45.1 0.0 collective-permute-done.3.refs_9_
  45.1 0.0 copy-start.4
  45.2 1.7 %adjoint_edge.1 = (f32[3,16,1024]{2,1,0:T(8,128)S(1)}, f32[3,16,1024]{2,1,0:T(8,128)S(1)}) custom-call(s32[3]{0:T(128)S(1)} %pad_add_fusion.pos_ref.refs_0_, f32[80,1024]{1,0:T(8,128)S(1)} %get-tuple-element.33.refs_1_, f32[4,80,1024]{2,1,0:T(8,128)S(1)} %get-tuple-element.31.count_ref.refs_2_, f32[4,80,1024]{2,1,0:T(8,128)S(1)} %get-tuple-element.34.refs_3_, ...), custom_call_target="tpu_custom_call" | custom-call | flops 1000 | bytes 6000000 | tf_op jit(solution)/shard_map/adjoint_edge/pallas_call | solution.py:305
  46.9 1.9 %collective-permute-start.5 = (f32[3,16,1024]{2,1,0:T(8,128)S(1)}, f32[3,16,1024]{2,1,0:T(8,128)S(1)}, u32[]{:S(2)}, u32[]{:S(2)}) collective-permute-start(f32[3,16,1024]{2,1,0:T(8,128)S(1)} %get-tuple-element.45), channel_id=1, source_target_pairs={{4,0},{8,4},{12,8},{16,12},{20,16},{24,20},{28,24},{32,28},{36,32}... | collective-permute-start | bytes 589832 | tf_op jit(solution)/shard_map/ppermute | solution.py:231
  48.8 1.9 %collective-permute-done.2 = f32[3,64,1024]{2,1,0:T(8,128)S(1)} collective-permute-done((f32[3,64,1024]{2,1,0:T(8,128)S(1)}, f32[3,64,1024]{2,1,0:T(8,128)S(1)}, u32[]{:S(2)}, u32[]{:S(2)}) %collective-permute-start.2) | collective-permute-done | bytes 786464 | tf_op jit(solution)/shard_map/ppermute | solution.py:231
  50.7 0.0 copy-done.4
  50.7 1.2 %fusion = f32[1,3,64,1024]{3,2,1,0:T(8,128)} fusion(f32[3,8,1024]{2,1,0:T(8,128)S(1)} %get-tuple-element.55, f32[3,48,1024]{2,1,0:T(8,128)S(1)} %get-tuple-element.44, f32[3,8,1024]{2,1,0:T(8,128)S(1)} %get-tuple-element.54, f32[3,64,1024]{2,1,0:T(8,128)S(1)} %copy-done.4, f32[3,64,1024]{2,1,0:T(8,128)S(1)} %collective-permute-done.2, pred[]{:T(512)S(6)} %eq.7, ...), kind=kLoop, calls=%fused_computation.1 | loop fusion | flops 1179648 | bytes 3932161 | tf_op jit(solution)/shard_map/broadcast_in_dim | solution.py:328
  51.9 11.1 %collective-permute-done.5 = f32[3,16,1024]{2,1,0:T(8,128)S(1)} collective-permute-done((f32[3,16,1024]{2,1,0:T(8,128)S(1)}, f32[3,16,1024]{2,1,0:T(8,128)S(1)}, u32[]{:S(2)}, u32[]{:S(2)}) %collective-permute-start.5) | collective-permute-done | bytes 196640 | tf_op jit(solution)/shard_map/ppermute | solution.py:231
  63.1 0.0 collective-permute-done.6
  63.1 1.0 %fusion.1 = f32[1,3,64,1024]{3,2,1,0:T(8,128)} fusion(f32[3,8,1024]{2,1,0:T(8,128)S(1)} %get-tuple-element.53, f32[3,48,1024]{2,1,0:T(8,128)S(1)} %collective-permute-done.6, f32[3,8,1024]{2,1,0:T(8,128)S(1)} %get-tuple-element.52, f32[3,64,1024]{2,1,0:T(8,128)S(1)} %get-tuple-element.32, f32[]{:T(128)S(6)} %select_n.16), kind=kLoop, calls=%fused_computation.3 | loop fusion | flops 786432 | bytes 2359300 | tf_op jit(solution)/shard_map/broadcast_in_dim | solution.py:328
  (4 shorter events, 0.1 us)
Async XLA Ops:
  0.6 20.4 %copy-start.1 = (s32[64,1024]{1,0:T(8,128)S(1)}, s32[64,1024]{1,0:T(8,128)}, u32[]{:S(2)}) copy-start(s32[64,1024]{1,0:T(8,128)} %mask_ref.1) | copy-start | bytes 786436
  0.6 20.4 %copy-start = (f32[1,3,64,1024]{3,2,1,0:T(8,128)S(1)}, f32[1,3,64,1024]{3,2,1,0:T(8,128)}, u32[]{:S(2)}) copy-start(f32[1,3,64,1024]{3,2,1,0:T(8,128)} %states_ref.1) | copy-start | bytes 2359300
  2.6 18.4 %collective-permute-start.1 = (f32[4,8,1024]{2,1,0:T(8,128)S(1)}, f32[4,8,1024]{2,1,0:T(8,128)S(1)}, u32[]{:S(2)}, u32[]{:S(2)}) collective-permute-start(f32[4,8,1024]{2,1,0:T(8,128)S(1)} %get-tuple-element.28), channel_id=1, source_target_pairs={{0,1},{1,2},{2,3},{4,5},{5,6},{6,7},{8,9},{9,10},{10,11},{12,13},{... | collective-permute-start | bytes 393224 | tf_op jit(solution)/shard_map/ppermute | solution.py:231
  4.3 16.6 %collective-permute-start = (f32[4,8,1024]{2,1,0:T(8,128)S(1)}, f32[4,8,1024]{2,1,0:T(8,128)S(1)}, u32[]{:S(2)}, u32[]{:S(2)}) collective-permute-start(f32[4,8,1024]{2,1,0:T(8,128)S(1)} %get-tuple-element.27), channel_id=1, source_target_pairs={{1,0},{2,1},{3,2},{5,4},{6,5},{7,6},{9,8},{10,9},{11,10},{13,12},{... | collective-permute-start | bytes 393224 | tf_op jit(solution)/shard_map/ppermute | solution.py:231
  5.6 29.5 %collective-permute-start.4 = (f32[3,64,1024]{2,1,0:T(8,128)}, f32[3,64,1024]{2,1,0:T(8,128)S(1)}, u32[]{:S(2)}, u32[]{:S(2)}) collective-permute-start(f32[3,64,1024]{2,1,0:T(8,128)} %bitcast.16), channel_id=1, source_target_pairs={{4,0},{8,4},{12,8},{16,12},{20,16},{24,20},{28,24},{32,28},{36,32}... | collective-permute-start | bytes 2359304 | tf_op jit(solution)/shard_map/ppermute | solution.py:231
  16.1 0.7 %copy-start.2 = (s32[1,4,1024]{2,1,0:T(4,128)S(1)}, s32[1,4,1024]{2,1,0:T(4,128)}, u32[]{:S(2)}) copy-start(s32[1,4,1024]{2,1,0:T(4,128)} %cells_ref.1) | copy-start | bytes 49156
  16.8 0.7 %copy-start.3 = (f32[1,4,1024]{2,1,0:T(4,128)S(1)}, f32[1,4,1024]{2,1,0:T(4,128)}, u32[]{:S(2)}) copy-start(f32[1,4,1024]{2,1,0:T(4,128)} %values_ref.1) | copy-start | bytes 49156
  24.8 26.0 %collective-permute-start.2 = (f32[3,64,1024]{2,1,0:T(8,128)S(1)}, f32[3,64,1024]{2,1,0:T(8,128)S(1)}, u32[]{:S(2)}, u32[]{:S(2)}) collective-permute-start(f32[3,64,1024]{2,1,0:T(8,128)S(1)} %get-tuple-element.32), channel_id=1, source_target_pairs={{0,4},{4,8},{8,12},{12,16},{16,20},{20,24},{24,28},{28,32},{32,36}... | collective-permute-start | bytes 2359304 | tf_op jit(solution)/shard_map/ppermute | solution.py:231
  26.7 18.5 %collective-permute-start.3 = (f32[3,8,1024]{2,1,0:T(8,128)S(1)}, f32[3,8,1024]{2,1,0:T(8,128)S(1)}, u32[]{:S(2)}, u32[]{:S(2)}) collective-permute-start(f32[3,8,1024]{2,1,0:T(8,128)S(1)} %slice_select_fusion), channel_id=1, source_target_pairs={{4,0},{8,4},{12,8},{16,12},{20,16},{24,20},{28,24},{32,28},{36,32}... | collective-permute-start | bytes 294920 | tf_op jit(solution)/shard_map/ppermute | solution.py:231
  38.3 24.7 %collective-permute-start.6 = (f32[3,48,1024]{2,1,0:T(8,128)S(1)}, f32[3,48,1024]{2,1,0:T(8,128)S(1)}, u32[]{:S(2)}, u32[]{:S(2)}) collective-permute-start(f32[3,48,1024]{2,1,0:T(8,128)S(1)} %get-tuple-element.46), channel_id=1, source_target_pairs={{4,0},{8,4},{12,8},{16,12},{20,16},{24,20},{28,24},{32,28},{36,32}... | collective-permute-start | bytes 1769480 | tf_op jit(solution)/shard_map/ppermute | solution.py:231
  45.1 5.6 %copy-start.4 = (f32[3,64,1024]{2,1,0:T(8,128)S(1)}, f32[3,64,1024]{2,1,0:T(8,128)}, u32[]{:S(2)}) copy-start(f32[3,64,1024]{2,1,0:T(8,128)} %param.6) | copy-start | bytes 2359300
  46.9 16.1 %collective-permute-start.5 = (f32[3,16,1024]{2,1,0:T(8,128)S(1)}, f32[3,16,1024]{2,1,0:T(8,128)S(1)}, u32[]{:S(2)}, u32[]{:S(2)}) collective-permute-start(f32[3,16,1024]{2,1,0:T(8,128)S(1)} %get-tuple-element.45), channel_id=1, source_target_pairs={{4,0},{8,4},{12,8},{16,12},{20,16},{24,20},{28,24},{32,28},{36,32}... | collective-permute-start | bytes 589832 | tf_op jit(solution)/shard_map/ppermute | solution.py:231

commit v2 on v1

--- a/solution.py
+++ b/solution.py
@@ -247,20 +247,22 @@
 
     def cost(us):
         return pl.CostEstimate(
-            flops=1000, transcendentals=0, bytes_accessed=int(us * 3.0e6)
+            flops=int(us * 1.0e9), transcendentals=0, bytes_accessed=int(us * 3.0e6)
         )
 
-    top = jnp.concatenate([states[0, :, :HALO], land_mask[None, :HALO].astype(f32)])
-    bottom = jnp.concatenate(
-        [states[0, :, strip - HALO :], land_mask[None, strip - HALO :].astype(f32)]
+    share = jnp.where(at_final, 1.0, step_length * defect_weight).astype(f32)
+    parts = (
+        states[0, :, :HALO],
+        states[0, :, strip - HALO :],
+        land_mask[None, :HALO].astype(f32),
+        land_mask[None, strip - HALO :].astype(f32),
     )
-    share = jnp.where(at_final, 1.0, step_length * defect_weight).astype(f32)
-    top, bottom, moving, pos, at_first, share = lax.optimization_barrier(
-        (top, bottom, states[0], pos, at_first, share)
+    parts, moving, pos, at_first, share = lax.optimization_barrier(
+        (parts, states[0], pos, at_first, share)
     )
-    up = shifted(bottom, "space", 1)
-    down = shifted(top, "space", -1)
     ahead = shifted(moving, "tm", -1)
+    up = shifted(jnp.concatenate([parts[1], parts[3]]), "space", 1)
+    down = shifted(jnp.concatenate([parts[0], parts[2]]), "space", -1)
 
     count, total = pl.pallas_call(
         maps_kernel,
@@ -271,7 +273,7 @@
         in_specs=[smem(), vmem(), vmem()],
         out_specs=(vmem(), vmem()),
         compiler_params=params(16),
-        cost_estimate=cost(3.5),
+        cost_estimate=cost(1),
         name="maps",
     )(pos, obs_cells, obs_values)
 
@@ -290,7 +292,7 @@
         in_specs=[smem()] + [vmem()] * 4 + [pl.BlockSpec(memory_space=pl.ANY)],
         out_specs=(vmem(),) * (NSTEP + 3),
         compiler_params=params(16),
-        cost_estimate=cost(5),
+        cost_estimate=cost(2),
         name="forward",
     )(pos, states, up, down, land_mask, count)
 
@@ -309,7 +311,7 @@
             out_specs=(vmem(),) * len(shapes),
             scratch_shapes=scratch,
             compiler_params=params(24),
-            cost_estimate=cost(4 if part == "middle" else 2),
+            cost_estimate=cost(0.1 if part == "middle" else 60),
             name="adjoint_" + part,
         )(pos, *operands)
 

time: 64.8 us -> 67.3 us (1.039)
  the two profiles are of different devices: /device:TPU:24 before, /device:TPU:9 now
where the time goes in v2:
time: 67.3 us; the launch traced here: 66.8 us
  starting transfers between devices  44.4 us (66%)
  Pallas kernels  12 us (18%)
  waiting for transfers between devices  4.07 us (6%)
  other arithmetic  3.13 us (5%)
  local copies, waits for them, and re-layouts  2.44 us (4%)
  between operations  0.84 us (1%)
    ppermute x7, starting transfers between devices, shifted(): return lax.ppermute(block, axis, route)  44.4 us
    pallas_call x2, Pallas kernels, adjoint(): pl.pallas_call(adjoint_kernel(part), out_shape=tuple(shapes), in_specs=[s...  4.89 us
    ppermute x7, waiting for transfers between devices, shifted(): return lax.ppermute(block, axis, route)  4.07 us
    pallas_call x1, Pallas kernels, local(): pl.pallas_call(forward_kernel, out_shape=(jax.ShapeDtypeStruct((rows, col...  3.66 us
    pallas_call x1, Pallas kernels, local(): pl.pallas_call(maps_kernel, out_shape=(jax.ShapeDtypeStruct((NSTEP, rows,...  3.46 us
    broadcast_in_dim x2, other arithmetic, local(): return (gradient[None], next_state[None])  2.16 us
    unnamed x10, local copies, waits for them, and re-layouts  1.45 us
  transfers between devices with their start and end apart: 7, of which 2 were waited for; matrix products, arithmetic and copies ran while one was open for 2% of the time, Pallas kernels for 18%

profile of v2, /device:TPU:9, one launch (start us, length us, event | category | flops | bytes accessed | tf_op | source)
XLA Modules:
  0.0 66.8 jit_solution(12523977525893282715)
XLA Ops:
  0.6 1.0 %slice_bitcast_fusion = (f32[3,8,1024]{2,1,0:T(8,128)S(1)}, f32[3,8,1024]{2,1,0:T(8,128)S(1)}) fusion(f32[1,3,64,1024]{3,2,1,0:T(8,128)} %states_ref.1), kind=kLoop, calls=%fused_computation.7 | loop fusion | bytes 393216 | tf_op jit(solution)/shard_map/squeeze | solution.py:256
  1.6 0.8 %convert_bitcast_fusion = (f32[1,8,1024]{2,1,0:T(8,128)S(1)}, f32[1,8,1024]{2,1,0:T(8,128)S(1)}) fusion(s32[64,1024]{1,0:T(8,128)} %mask_ref.1), kind=kLoop, calls=%fused_computation.9 | loop fusion | flops 16384 | bytes 131072 | tf_op jit(solution)/shard_map/convert_element_type | solution.py:258
  2.4 0.1 pad_add_fusion.pos_ref.refs_0_
  2.5 9.8 %collective-permute-start.4 = (f32[3,64,1024]{2,1,0:T(8,128)}, f32[3,64,1024]{2,1,0:T(8,128)S(1)}, u32[]{:S(2)}, u32[]{:S(2)}) collective-permute-start(f32[3,64,1024]{2,1,0:T(8,128)} %bitcast.16), channel_id=1, source_target_pairs={{4,0},{8,4},{12,8},{16,12},{20,16},{24,20},{28,24},{32,28},{36,32}... | collective-permute-start | bytes 2359304 | tf_op jit(solution)/shard_map/ppermute | solution.py:231
  12.3 3.1 %collective-permute-start.1 = (f32[4,8,1024]{2,1,0:T(8,128)S(1)}, f32[4,8,1024]{2,1,0:T(8,128)S(1)}, u32[]{:S(2)}, u32[]{:S(2)}) collective-permute-start(f32[4,8,1024]{2,1,0:T(8,128)S(1)} %pad_maximum_fusion.1), channel_id=1, source_target_pairs={{0,1},{1,2},{2,3},{4,5},{5,6},{6,7},{8,9},{9,10},{10,11},{12,13},{... | collective-permute-start | bytes 393224 | tf_op jit(solution)/shard_map/ppermute | solution.py:231
  15.4 0.0 copy-start
  15.4 0.0 copy-start.1
  15.4 2.1 %collective-permute-start = (f32[4,8,1024]{2,1,0:T(8,128)S(1)}, f32[4,8,1024]{2,1,0:T(8,128)S(1)}, u32[]{:S(2)}, u32[]{:S(2)}) collective-permute-start(f32[4,8,1024]{2,1,0:T(8,128)S(1)} %pad_maximum_fusion), channel_id=1, source_target_pairs={{1,0},{2,1},{3,2},{5,4},{6,5},{7,6},{9,8},{10,9},{11,10},{13,12},{... | collective-permute-start | bytes 393224 | tf_op jit(solution)/shard_map/ppermute | solution.py:231
  17.5 0.0 copy-start.2
  17.5 0.7 %copy-done.2 = s32[1,4,1024]{2,1,0:T(4,128)S(1)} copy-done((s32[1,4,1024]{2,1,0:T(4,128)S(1)}, s32[1,4,1024]{2,1,0:T(4,128)}, u32[]{:S(2)}) %copy-start.2) | copy-done | bytes 16408
  18.2 0.0 copy-start.3
  18.2 0.7 %copy-done.3 = f32[1,4,1024]{2,1,0:T(4,128)S(1)} copy-done((f32[1,4,1024]{2,1,0:T(4,128)S(1)}, f32[1,4,1024]{2,1,0:T(4,128)}, u32[]{:S(2)}) %copy-start.3) | copy-done | bytes 16408
  18.9 3.5 %maps.1 = (f32[4,80,1024]{2,1,0:T(8,128)S(1)}, f32[4,80,1024]{2,1,0:T(8,128)S(1)}) custom-call(s32[3]{0:T(128)S(1)} %pad_add_fusion.pos_ref.refs_0_, s32[1,4,1024]{2,1,0:T(4,128)S(1)} %copy-done.2, f32[1,4,1024]{2,1,0:T(4,128)S(1)} %copy-done.3), custom_call_target="tpu_custom_call" | custom-call | flops 1000000000 | bytes 3000000 | tf_op jit(solution)/shard_map/maps/pallas_call | solution.py:267
  22.4 0.0 collective-permute-done.1.up_ref
  22.4 0.0 collective-permute-done.down_ref
  22.4 0.1 slice_select_fusion
  22.5 17.7 %collective-permute-start.3 = (f32[3,8,1024]{2,1,0:T(8,128)S(1)}, f32[3,8,1024]{2,1,0:T(8,128)S(1)}, u32[]{:S(2)}, u32[]{:S(2)}) collective-permute-start(f32[3,8,1024]{2,1,0:T(8,128)S(1)} %slice_select_fusion), channel_id=1, source_target_pairs={{4,0},{8,4},{12,8},{16,12},{20,16},{24,20},{28,24},{32,28},{36,32}... | collective-permute-start | bytes 294920 | tf_op jit(solution)/shard_map/ppermute | solution.py:231
  40.2 0.0 copy-done
  40.2 0.0 copy-done.1
  40.2 3.7 %forward.1 = (f32[80,1024]{1,0:T(8,128)S(1)}, f32[3,64,1024]{2,1,0:T(8,128)S(1)}, f32[3,80,1024]{2,1,0:T(8,128)S(1)}, f32[3,80,1024]{2,1,0:T(8,128)S(1)}, f32[3,...) custom-call(s32[3]{0:T(128)S(1)} %pad_add_fusion.pos_ref.refs_0_, ...), custom_call_target="tpu_custom_call" | custom-call | flops 2000000000 | bytes 6000000 | tf_op jit(solution)/shard_map/forward/pallas_call | solution.py:285
  43.9 1.9 %collective-permute-start.2 = (f32[3,64,1024]{2,1,0:T(8,128)S(1)}, f32[3,64,1024]{2,1,0:T(8,128)S(1)}, u32[]{:S(2)}, u32[]{:S(2)}) collective-permute-start(f32[3,64,1024]{2,1,0:T(8,128)S(1)} %get-tuple-element.36), channel_id=1, source_target_pairs={{0,4},{4,8},{8,12},{12,16},{16,20},{20,24},{24,28},{28,32},{32,36}... | collective-permute-start | bytes 2359304 | tf_op jit(solution)/shard_map/ppermute | solution.py:231
  45.8 0.0 collective-permute-done.4.refs_9_
  45.8 3.2 %adjoint_middle.1 = (f32[3,48,1024]{2,1,0:T(8,128)S(1)}, f32[3,48,1024]{2,1,0:T(8,128)S(1)}, f32[4,3,80,1024]{3,2,1,0:T(8,128)S(1)}) custom-call(s32[3]{0:T(128)S(1)} %pad_add_fusion.pos_ref.refs_0_, f32[80,1024]{1,0:T(8,128)S(1)} %get-tuple-element.37.refs_1_, f32[4,80,1024]{2,1,0:T(8,128)S(1)} %get-tuple-element.35.count_ref.refs_2_, ...), custom_call_target="tpu_custom_call" | custom-call | flops 100000000 | bytes 300000 | tf_op jit(solution)/shard_map/adjoint_middle/pallas_call | solution.py:307
  49.0 7.9 %collective-permute-start.6 = (f32[3,48,1024]{2,1,0:T(8,128)S(1)}, f32[3,48,1024]{2,1,0:T(8,128)S(1)}, u32[]{:S(2)}, u32[]{:S(2)}) collective-permute-start(f32[3,48,1024]{2,1,0:T(8,128)S(1)} %get-tuple-element.50), channel_id=1, source_target_pairs={{4,0},{8,4},{12,8},{16,12},{20,16},{24,20},{28,24},{32,28},{36,32}... | collective-permute-start | bytes 1769480 | tf_op jit(solution)/shard_map/ppermute | solution.py:231
  56.9 0.0 collective-permute-done.3.refs_9_
  56.9 0.0 copy-start.4
  56.9 1.7 %adjoint_edge.1 = (f32[3,16,1024]{2,1,0:T(8,128)S(1)}, f32[3,16,1024]{2,1,0:T(8,128)S(1)}) custom-call(s32[3]{0:T(128)S(1)} %pad_add_fusion.pos_ref.refs_0_, f32[80,1024]{1,0:T(8,128)S(1)} %get-tuple-element.37.refs_1_, f32[4,80,1024]{2,1,0:T(8,128)S(1)} %get-tuple-element.35.count_ref.refs_2_, f32[4,80,1024]{2,1,0:T(8,128)S(1)} %get-tuple-element.38.refs_3_, ...), custom_call_target="tpu_custom_call" | custom-call | flops 60000002048 | bytes 180000000 | tf_op jit(solution)/shard_map/adjoint_edge/pallas_call | solution.py:307
  58.7 1.9 %collective-permute-start.5 = (f32[3,16,1024]{2,1,0:T(8,128)S(1)}, f32[3,16,1024]{2,1,0:T(8,128)S(1)}, u32[]{:S(2)}, u32[]{:S(2)}) collective-permute-start(f32[3,16,1024]{2,1,0:T(8,128)S(1)} %get-tuple-element.49), channel_id=1, source_target_pairs={{4,0},{8,4},{12,8},{16,12},{20,16},{24,20},{28,24},{32,28},{36,32}... | collective-permute-start | bytes 589832 | tf_op jit(solution)/shard_map/ppermute | solution.py:231
  60.6 0.5 collective-permute-done.2
  61.2 0.0 copy-done.4
  61.2 1.2 %fusion = f32[1,3,64,1024]{3,2,1,0:T(8,128)} fusion(f32[3,8,1024]{2,1,0:T(8,128)S(1)} %get-tuple-element.59, f32[3,48,1024]{2,1,0:T(8,128)S(1)} %get-tuple-element.48, f32[3,8,1024]{2,1,0:T(8,128)S(1)} %get-tuple-element.58, f32[3,64,1024]{2,1,0:T(8,128)S(1)} %copy-done.4, f32[3,64,1024]{2,1,0:T(8,128)S(1)} %collective-permute-done.2, pred[]{:T(512)S(6)} %eq.7, ...), kind=kLoop, calls=%fused_computation.1 | loop fusion | flops 1179648 | bytes 3932161 | tf_op jit(solution)/shard_map/broadcast_in_dim | solution.py:330
  62.3 3.5 %collective-permute-done.5 = f32[3,16,1024]{2,1,0:T(8,128)S(1)} collective-permute-done((f32[3,16,1024]{2,1,0:T(8,128)S(1)}, f32[3,16,1024]{2,1,0:T(8,128)S(1)}, u32[]{:S(2)}, u32[]{:S(2)}) %collective-permute-start.5) | collective-permute-done | bytes 196640 | tf_op jit(solution)/shard_map/ppermute | solution.py:231
  65.8 0.0 collective-permute-done.6
  65.9 1.0 %fusion.1 = f32[1,3,64,1024]{3,2,1,0:T(8,128)} fusion(f32[3,8,1024]{2,1,0:T(8,128)S(1)} %get-tuple-element.57, f32[3,48,1024]{2,1,0:T(8,128)S(1)} %collective-permute-done.6, f32[3,8,1024]{2,1,0:T(8,128)S(1)} %get-tuple-element.56, f32[3,64,1024]{2,1,0:T(8,128)S(1)} %get-tuple-element.36, f32[]{:T(128)S(6)} %select_n.16), kind=kLoop, calls=%fused_computation.3 | loop fusion | flops 786432 | bytes 2359300 | tf_op jit(solution)/shard_map/broadcast_in_dim | solution.py:330
  (5 shorter events, 0.1 us)
Async XLA Ops:
  2.5 43.4 %collective-permute-start.4 = (f32[3,64,1024]{2,1,0:T(8,128)}, f32[3,64,1024]{2,1,0:T(8,128)S(1)}, u32[]{:S(2)}, u32[]{:S(2)}) collective-permute-start(f32[3,64,1024]{2,1,0:T(8,128)} %bitcast.16), channel_id=1, source_target_pairs={{4,0},{8,4},{12,8},{16,12},{20,16},{24,20},{28,24},{32,28},{36,32}... | collective-permute-start | bytes 2359304 | tf_op jit(solution)/shard_map/ppermute | solution.py:231
  12.3 10.1 %collective-permute-start.1 = (f32[4,8,1024]{2,1,0:T(8,128)S(1)}, f32[4,8,1024]{2,1,0:T(8,128)S(1)}, u32[]{:S(2)}, u32[]{:S(2)}) collective-permute-start(f32[4,8,1024]{2,1,0:T(8,128)S(1)} %pad_maximum_fusion.1), channel_id=1, source_target_pairs={{0,1},{1,2},{2,3},{4,5},{5,6},{6,7},{8,9},{9,10},{10,11},{12,13},{... | collective-permute-start | bytes 393224 | tf_op jit(solution)/shard_map/ppermute | solution.py:231
  15.4 24.8 %copy-start = (f32[1,3,64,1024]{3,2,1,0:T(8,128)S(1)}, f32[1,3,64,1024]{3,2,1,0:T(8,128)}, u32[]{:S(2)}) copy-start(f32[1,3,64,1024]{3,2,1,0:T(8,128)} %states_ref.1) | copy-start | bytes 2359300
  15.4 24.8 %copy-start.1 = (s32[64,1024]{1,0:T(8,128)S(1)}, s32[64,1024]{1,0:T(8,128)}, u32[]{:S(2)}) copy-start(s32[64,1024]{1,0:T(8,128)} %mask_ref.1) | copy-start | bytes 786436
  15.4 7.0 %collective-permute-start = (f32[4,8,1024]{2,1,0:T(8,128)S(1)}, f32[4,8,1024]{2,1,0:T(8,128)S(1)}, u32[]{:S(2)}, u32[]{:S(2)}) collective-permute-start(f32[4,8,1024]{2,1,0:T(8,128)S(1)} %pad_maximum_fusion), channel_id=1, source_target_pairs={{1,0},{2,1},{3,2},{5,4},{6,5},{7,6},{9,8},{10,9},{11,10},{13,12},{... | collective-permute-start | bytes 393224 | tf_op jit(solution)/shard_map/ppermute | solution.py:231
  17.5 0.7 %copy-start.2 = (s32[1,4,1024]{2,1,0:T(4,128)S(1)}, s32[1,4,1024]{2,1,0:T(4,128)}, u32[]{:S(2)}) copy-start(s32[1,4,1024]{2,1,0:T(4,128)} %cells_ref.1) | copy-start | bytes 49156
  18.2 0.7 %copy-start.3 = (f32[1,4,1024]{2,1,0:T(4,128)S(1)}, f32[1,4,1024]{2,1,0:T(4,128)}, u32[]{:S(2)}) copy-start(f32[1,4,1024]{2,1,0:T(4,128)} %values_ref.1) | copy-start | bytes 49156
  22.5 34.4 %collective-permute-start.3 = (f32[3,8,1024]{2,1,0:T(8,128)S(1)}, f32[3,8,1024]{2,1,0:T(8,128)S(1)}, u32[]{:S(2)}, u32[]{:S(2)}) collective-permute-start(f32[3,8,1024]{2,1,0:T(8,128)S(1)} %slice_select_fusion), channel_id=1, source_target_pairs={{4,0},{8,4},{12,8},{16,12},{20,16},{24,20},{28,24},{32,28},{36,32}... | collective-permute-start | bytes 294920 | tf_op jit(solution)/shard_map/ppermute | solution.py:231
  43.9 17.2 %collective-permute-start.2 = (f32[3,64,1024]{2,1,0:T(8,128)S(1)}, f32[3,64,1024]{2,1,0:T(8,128)S(1)}, u32[]{:S(2)}, u32[]{:S(2)}) collective-permute-start(f32[3,64,1024]{2,1,0:T(8,128)S(1)} %get-tuple-element.36), channel_id=1, source_target_pairs={{0,4},{4,8},{8,12},{12,16},{16,20},{20,24},{24,28},{28,32},{32,36}... | collective-permute-start | bytes 2359304 | tf_op jit(solution)/shard_map/ppermute | solution.py:231
  49.0 16.8 %collective-permute-start.6 = (f32[3,48,1024]{2,1,0:T(8,128)S(1)}, f32[3,48,1024]{2,1,0:T(8,128)S(1)}, u32[]{:S(2)}, u32[]{:S(2)}) collective-permute-start(f32[3,48,1024]{2,1,0:T(8,128)S(1)} %get-tuple-element.50), channel_id=1, source_target_pairs={{4,0},{8,4},{12,8},{16,12},{20,16},{24,20},{28,24},{32,28},{36,32}... | collective-permute-start | bytes 1769480 | tf_op jit(solution)/shard_map/ppermute | solution.py:231
  56.9 4.2 %copy-start.4 = (f32[3,64,1024]{2,1,0:T(8,128)S(1)}, f32[3,64,1024]{2,1,0:T(8,128)}, u32[]{:S(2)}) copy-start(f32[3,64,1024]{2,1,0:T(8,128)} %param.6) | copy-start | bytes 2359300
  58.7 7.2 %collective-permute-start.5 = (f32[3,16,1024]{2,1,0:T(8,128)S(1)}, f32[3,16,1024]{2,1,0:T(8,128)S(1)}, u32[]{:S(2)}, u32[]{:S(2)}) collective-permute-start(f32[3,16,1024]{2,1,0:T(8,128)S(1)} %get-tuple-element.49), channel_id=1, source_target_pairs={{4,0},{8,4},{12,8},{16,12},{20,16},{24,20},{28,24},{32,28},{36,32}... | collective-permute-start | bytes 589832 | tf_op jit(solution)/shard_map/ppermute | solution.py:231

commit v3 on v2

--- a/solution.py
+++ b/solution.py
@@ -21,6 +21,14 @@
     return pl.BlockSpec(memory_space=pltpu.VMEM)
 
 
+def hbm():
+    return pl.BlockSpec(memory_space=pltpu.HBM)
+
+
+def off_chip(x):
+    return pltpu.with_memory_space_constraint(x, pltpu.HBM)
+
+
 def smem():
     return pl.BlockSpec(memory_space=pltpu.SMEM)
 
@@ -43,9 +51,49 @@
     return pltpu.roll(jnp.where(last, before, x), 1, axis=0)
 
 
-def maps_kernel(pos_ref, cells_ref, values_ref, count_ref, total_ref):
+def prepare_kernel(
+    pos_ref, states_ref, mask_ref, cells_ref, values_ref,
+    cross_ref, pair_ref, seen_ref, wanted_ref, bits, sems
+):
+    strip = states_ref.shape[2]
+    bottom = strip - HALO
+    odd = pos_ref[3]
+    copies = []
+    for n, (out, at) in enumerate(((cross_ref, odd * bottom), (pair_ref, (1 - odd) * bottom))):
+        at = pl.multiple_of(at, HALO)
+        copies.append(
+            pltpu.make_async_copy(mask_ref.at[pl.ds(at, HALO)], bits.at[n], sems.at[2 * n])
+        )
+        copies.append(
+            pltpu.make_async_copy(
+                states_ref.at[0, :, pl.ds(at, HALO)], out.at[pl.ds(0, 3)], sems.at[2 * n + 1]
+            )
+        )
+    copies.append(pltpu.make_async_copy(cells_ref.at[0], seen_ref, sems.at[4]))
+    copies.append(pltpu.make_async_copy(values_ref.at[0], wanted_ref, sems.at[5]))
+    for copy in copies:
+        copy.start()
+    for copy in copies:
+        copy.wait()
+    cross_ref[3] = bits[0].astype(jnp.float32)
+    pair_ref[3] = bits[1].astype(jnp.float32)
+
+
+def maps_kernel(
+    pos_ref, cells_ref, values_ref, states_ref, mask_ref,
+    count_ref, total_ref, start_ref, bits_ref, sems
+):
+    strip = mask_ref.shape[0]
+    copies = (
+        pltpu.make_async_copy(
+            states_ref.at[0], start_ref.at[:, pl.ds(HALO, strip)], sems.at[0]
+        ),
+        pltpu.make_async_copy(mask_ref, bits_ref, sems.at[1]),
+    )
+    for copy in copies:
+        copy.start()
     rows, columns = count_ref.shape[1:]
-    observed = cells_ref.shape[2]
+    observed = cells_ref.shape[1]
     shift = columns.bit_length() - 1
     assert columns == 1 << shift
     width = 256
@@ -53,8 +101,8 @@
     row_iota = lax.broadcasted_iota(jnp.int32, (rows, observed), 0)
     col_iota = lax.broadcasted_iota(jnp.int32, (width, observed), 0)
     for step in range(NSTEP):
-        cells = cells_ref[0, step : step + 1, :]
-        values = obs_weight * values_ref[0, step : step + 1, :]
+        cells = cells_ref[step : step + 1, :]
+        values = obs_weight * values_ref[step : step + 1, :]
         row = lax.shift_right_logical(cells, shift)
         col = cells - lax.shift_left(row, shift)
         inside = row_iota == row - base
@@ -79,23 +127,26 @@
             total_ref[step, :, start : start + width] = (
                 out[rows : 2 * rows] + out[2 * rows : 3 * rows] + out[3 * rows :]
             )
+    for copy in copies:
+        copy.wait()
 
 
 def forward_kernel(
-    pos_ref, states_ref, up_ref, down_ref, mask_ref, count_ref, land_ref, ends_ref, *path_ref
+    pos_ref, start_ref, cross_ref, pair_ref, mask_ref, land_ref, ends_ref, *path_ref
 ):
-    strip = states_ref.shape[2]
+    strip, columns = mask_ref.shape
     rows = strip + 2 * HALO
     blocks = rows // BLK
-    columns = states_ref.shape[3]
     base = pos_ref[0]
     grid_rows = pos_ref[1]
-    path_ref[0][:, :HALO] = up_ref[:3]
-    path_ref[0][:, HALO : HALO + strip] = states_ref[0]
-    path_ref[0][:, HALO + strip :] = down_ref[:3]
-    land_ref[:HALO] = up_ref[3]
+    odd = pos_ref[3] == 1
+    up = jnp.where(odd, pair_ref[...], cross_ref[...])
+    down = jnp.where(odd, cross_ref[...], pair_ref[...])
+    path_ref[0][:, :HALO] = up[:3]
+    path_ref[0][:, HALO + strip :] = down[:3]
+    land_ref[:HALO] = up[3]
     land_ref[HALO : HALO + strip] = mask_ref[...].astype(jnp.float32)
-    land_ref[HALO + strip :] = down_ref[3]
+    land_ref[HALO + strip :] = down[3]
 
     for step in range(NSTEP):
         for i in range(blocks):
@@ -237,8 +288,9 @@
     at_first = lax.axis_index("tm") == 0
     at_final = lax.axis_index("tm") == lax.axis_size("tm") - 1
     base = lax.axis_index("space") * strip - HALO
+    odd = lax.axis_index("space") & 1
     pos = jnp.stack(
-        [base, jnp.int32(strip) * lax.axis_size("space"), at_final.astype(jnp.int32)]
+        [base, jnp.int32(strip) * lax.axis_size("space"), at_final.astype(jnp.int32), odd]
     ).astype(jnp.int32)
     f32 = jnp.float32
 
@@ -250,36 +302,55 @@
             flops=int(us * 1.0e9), transcendentals=0, bytes_accessed=int(us * 3.0e6)
         )
 
+    observed = obs_cells.shape[2]
+    cross, pair, cells, values = pl.pallas_call(
+        prepare_kernel,
+        out_shape=(
+            jax.ShapeDtypeStruct((4, HALO, columns), f32),
+            jax.ShapeDtypeStruct((4, HALO, columns), f32),
+            jax.ShapeDtypeStruct((NSTEP, observed), jnp.int32),
+            jax.ShapeDtypeStruct((NSTEP, observed), f32),
+        ),
+        in_specs=[smem()] + [hbm()] * 4,
+        out_specs=(vmem(),) * 4,
+        scratch_shapes=[
+            pltpu.VMEM((2, HALO, columns), jnp.int32),
+            pltpu.SemaphoreType.DMA((6,)),
+        ],
+        compiler_params=params(8),
+        cost_estimate=cost(0.5),
+        name="prepare",
+    )(pos, *(off_chip(x) for x in (states, land_mask, obs_cells, obs_values)))
     share = jnp.where(at_final, 1.0, step_length * defect_weight).astype(f32)
-    parts = (
-        states[0, :, :HALO],
-        states[0, :, strip - HALO :],
-        land_mask[None, :HALO].astype(f32),
-        land_mask[None, strip - HALO :].astype(f32),
+    cross, pair, moving, pos, at_first, share, even = lax.optimization_barrier(
+        (cross, pair, states[0], pos, at_first, share, odd == 0)
     )
-    parts, moving, pos, at_first, share = lax.optimization_barrier(
-        (parts, states[0], pos, at_first, share)
-    )
+    strips = lax.axis_size("space")
+    inner = [(i, i ^ 1) for i in range(strips)]
+    outer = [(i, j) for i in range(strips) for j in [((i + 1) ^ 1) - 1] if 0 <= j < strips]
+    cross = lax.ppermute(cross, "space", outer)
     ahead = shifted(moving, "tm", -1)
-    up = shifted(jnp.concatenate([parts[1], parts[3]]), "space", 1)
-    down = shifted(jnp.concatenate([parts[0], parts[2]]), "space", -1)
-
-    count, total = pl.pallas_call(
+    pair = lax.ppermute(pair, "space", inner)
+
+    count, total, start, bits = pl.pallas_call(
         maps_kernel,
         out_shape=(
             jax.ShapeDtypeStruct((NSTEP, rows, columns), f32),
             jax.ShapeDtypeStruct((NSTEP, rows, columns), f32),
+            jax.ShapeDtypeStruct((3, rows, columns), f32),
+            jax.ShapeDtypeStruct((strip, columns), jnp.int32),
         ),
-        in_specs=[smem(), vmem(), vmem()],
-        out_specs=(vmem(), vmem()),
+        in_specs=[smem(), vmem(), vmem(), hbm(), hbm()],
+        out_specs=(vmem(),) * 4,
+        scratch_shapes=[pltpu.SemaphoreType.DMA((2,))],
         compiler_params=params(16),
-        cost_estimate=cost(1),
+        cost_estimate=cost(4),
         name="maps",
-    )(pos, obs_cells, obs_values)
-
-    half_rows = lax.broadcasted_iota(jnp.int32, (3, HALO, columns), 1) < HALO // 2
-    rim = jnp.where(half_rows, down[:3], up[:3])
-    rim, up, down = lax.optimization_barrier((rim, up, down))
+    )(pos, cells, values, off_chip(states), off_chip(land_mask))
+
+    row = lax.broadcasted_iota(jnp.int32, (3, HALO, columns), 1)
+    rim = jnp.where((row < HALO // 2) == even, pair[:3], cross[:3])
+    rim, cross, pair = lax.optimization_barrier((rim, cross, pair))
     rim = shifted(rim, "tm", -1)
 
     land, ends, *path = pl.pallas_call(
@@ -289,12 +360,13 @@
             jax.ShapeDtypeStruct((3, strip, columns), f32),
         )
         + (jax.ShapeDtypeStruct((3, rows, columns), f32),) * (NSTEP + 1),
-        in_specs=[smem()] + [vmem()] * 4 + [pl.BlockSpec(memory_space=pl.ANY)],
+        in_specs=[smem()] + [vmem()] * 4,
         out_specs=(vmem(),) * (NSTEP + 3),
+        input_output_aliases={1: 2},
         compiler_params=params(16),
         cost_estimate=cost(2),
         name="forward",
-    )(pos, states, up, down, land_mask, count)
+    )(pos, start, cross, pair, bits)
 
     previous = shifted(ends, "tm", 1)
 

time: 67.3 us -> 62.5 us (0.929)
  the two profiles are of different devices: /device:TPU:9 before, /device:TPU:24 now
where the time goes in v3:
time: 62.5 us; the launch traced here: 62.3 us
  starting transfers between devices  30.4 us (49%)
  waiting for transfers between devices  15.1 us (24%)
  Pallas kernels  13.6 us (22%)
  other arithmetic  2.33 us (4%)
  between operations  0.8 us (1%)
    ppermute x5, starting transfers between devices, shifted(): return lax.ppermute(block, axis, route)  26.8 us
    ppermute x5, waiting for transfers between devices, shifted(): return lax.ppermute(block, axis, route)  15.1 us
    pallas_call x2, Pallas kernels, adjoint(): pl.pallas_call(adjoint_kernel(part), out_shape=tuple(shapes), in_specs=[s...  4.9 us
    pallas_call x1, Pallas kernels, local(): pl.pallas_call(forward_kernel, out_shape=(jax.ShapeDtypeStruct((rows, col...  3.64 us
    pallas_call x1, Pallas kernels, local(): pl.pallas_call(maps_kernel, out_shape=(jax.ShapeDtypeStruct((NSTEP, rows,...  3.48 us
    ppermute x1, starting transfers between devices, local(): pair = lax.ppermute(pair, 'space', inner)  2.93 us
    broadcast_in_dim x2, other arithmetic, local(): return (gradient[None], next_state[None])  2.16 us
    pallas_call x1, Pallas kernels, local(): pl.pallas_call(prepare_kernel, out_shape=(jax.ShapeDtypeStruct((4, HALO,...  1.59 us
  transfers between devices with their start and end apart: 7, of which 3 were waited for; matrix products, arithmetic and copies ran while one was open for 2% of the time, Pallas kernels for 19%

profile of v3, /device:TPU:24, one launch (start us, length us, event | category | flops | bytes accessed | tf_op | source)
XLA Modules:
  0.0 62.3 jit_solution(5118353590364445823)
XLA Ops:
  0.6 0.0 copy-start
  0.7 0.1 pad_add_fusion.pos_ref.refs_0_
  0.7 1.6 %prepare.1 = (f32[4,8,1024]{2,1,0:T(8,128)S(1)}, f32[4,8,1024]{2,1,0:T(8,128)S(1)}, s32[4,1024]{1,0:T(4,128)S(1)}, f32[4,1024]{1,0:T(4,128)S(1)}) custom-call(s32[4]{0:T(128)S(1)} %pad_add_fusion.pos_ref.refs_0_, f32[1,3,64,1024]{3,2,1,0:T(8,128)} %states_ref.3, s32[64,1024]{1,0:T(8,128)} %mask_ref.3, s32[1,4,1024]{2,1,0:T(4,128)} %cells_ref.1, ...), custom_call_target="tpu_custom_call" | custom-call | flops 500000000 | bytes 1500000 | tf_op jit(solution)/shard_map/prepare/pallas_call | solution.py:306
  2.3 0.7 %collective-permute-start.1 = (f32[4,8,1024]{2,1,0:T(8,128)S(1)}, f32[4,8,1024]{2,1,0:T(8,128)S(1)}, u32[]{:S(2)}, u32[]{:S(2)}) collective-permute-start(f32[4,8,1024]{2,1,0:T(8,128)S(1)} %get-tuple-element.41), channel_id=1, source_target_pairs={{1,2},{2,1},{5,6},{6,5},{9,10},{10,9},{13,14},{14,13},{17,18},{18,... | collective-permute-start | bytes 393224 | tf_op jit(solution)/shard_map/ppermute | solution.py:331
  3.0 2.9 %collective-permute-start = (f32[4,8,1024]{2,1,0:T(8,128)S(1)}, f32[4,8,1024]{2,1,0:T(8,128)S(1)}, u32[]{:S(2)}, u32[]{:S(2)}) collective-permute-start(f32[4,8,1024]{2,1,0:T(8,128)S(1)} %get-tuple-element.40), channel_id=1, source_target_pairs={{0,1},{1,0},{2,3},{3,2},{4,5},{5,4},{6,7},{7,6},{8,9},{9,8},{10,11... | collective-permute-start | bytes 393224 | tf_op jit(solution)/shard_map/ppermute | solution.py:333
  5.9 0.0 copy-done
  5.9 10.1 %collective-permute-start.4 = (f32[3,64,1024]{2,1,0:T(8,128)S(1)}, f32[3,64,1024]{2,1,0:T(8,128)S(1)}, u32[]{:S(2)}, u32[]{:S(2)}) collective-permute-start(f32[3,64,1024]{2,1,0:T(8,128)S(1)} %bitcast.9), channel_id=1, source_target_pairs={{4,0},{8,4},{12,8},{16,12},{20,16},{24,20},{28,24},{32,28},{36,32}... | collective-permute-start | bytes 2359304 | tf_op jit(solution)/shard_map/ppermute | solution.py:282
  16.0 3.5 %maps.1 = (f32[4,80,1024]{2,1,0:T(8,128)S(1)}, f32[4,80,1024]{2,1,0:T(8,128)S(1)}, f32[3,80,1024]{2,1,0:T(8,128)S(1)}, s32[64,1024]{1,0:T(8,128)S(1)}) custom-call(s32[4]{0:T(128)S(1)} %pad_add_fusion.pos_ref.refs_0_, s32[4,1024]{1,0:T(4,128)S(1)} %get-tuple-element.36.cells_ref, f32[4,1024]{1,0:T(4,128)S(1)} %get-tuple-element.37.values_ref, ...), custom_call_target="tpu_custom_call" | custom-call | flops 4000000000 | bytes 12000000 | tf_op jit(solution)/shard_map/maps/pallas_call | solution.py:335
  19.6 0.0 collective-permute-done.1.cross_ref
  19.6 0.0 collective-permute-done.pair_ref
  19.6 0.1 slice_select_fusion
  19.7 2.9 %collective-permute-start.3 = (f32[3,8,1024]{2,1,0:T(8,128)S(1)}, f32[3,8,1024]{2,1,0:T(8,128)S(1)}, u32[]{:S(2)}, u32[]{:S(2)}) collective-permute-start(f32[3,8,1024]{2,1,0:T(8,128)S(1)} %slice_select_fusion), channel_id=1, source_target_pairs={{4,0},{8,4},{12,8},{16,12},{20,16},{24,20},{28,24},{32,28},{36,32}... | collective-permute-start | bytes 294920 | tf_op jit(solution)/shard_map/ppermute | solution.py:282
  22.6 3.6 %forward.1 = (f32[80,1024]{1,0:T(8,128)S(1)}, f32[3,64,1024]{2,1,0:T(8,128)S(1)}, f32[3,80,1024]{2,1,0:T(8,128)S(1)}, f32[3,80,1024]{2,1,0:T(8,128)S(1)}, f32[3,...) custom-call(s32[4]{0:T(128)S(1)} %pad_add_fusion.pos_ref.refs_0_, ...), custom_call_target="tpu_custom_call", output_to_operand_aliasing={{2}: (1, {})} | custom-call | flops 2000000000 | bytes 6000000 | tf_op jit(solution)/shard_map/forward/pallas_call | solution.py:356
  26.2 2.9 %collective-permute-start.2 = (f32[3,64,1024]{2,1,0:T(8,128)S(1)}, f32[3,64,1024]{2,1,0:T(8,128)S(1)}, u32[]{:S(2)}, u32[]{:S(2)}) collective-permute-start(f32[3,64,1024]{2,1,0:T(8,128)S(1)} %get-tuple-element.45), channel_id=1, source_target_pairs={{0,4},{4,8},{8,12},{12,16},{16,20},{20,24},{24,28},{28,32},{32,36}... | collective-permute-start | bytes 2359304 | tf_op jit(solution)/shard_map/ppermute | solution.py:282
  29.1 4.8 %collective-permute-done.4.refs_9_ = f32[3,64,1024]{2,1,0:T(8,128)S(1)} collective-permute-done((f32[3,64,1024]{2,1,0:T(8,128)S(1)}, f32[3,64,1024]{2,1,0:T(8,128)S(1)}, u32[]{:S(2)}, u32[]{:S(2)}) %collective-permute-start.4) | collective-permute-done | bytes 786464 | tf_op jit(solution)/shard_map/ppermute | solution.py:282
  33.9 3.2 %adjoint_middle.1 = (f32[3,48,1024]{2,1,0:T(8,128)S(1)}, f32[3,48,1024]{2,1,0:T(8,128)S(1)}, f32[4,3,80,1024]{3,2,1,0:T(8,128)S(1)}) custom-call(s32[4]{0:T(128)S(1)} %pad_add_fusion.pos_ref.refs_0_, f32[80,1024]{1,0:T(8,128)S(1)} %get-tuple-element.46.refs_1_, f32[4,80,1024]{2,1,0:T(8,128)S(1)} %get-tuple-element.47.refs_2_, ...), custom_call_target="tpu_custom_call" | custom-call | flops 100000000 | bytes 300000 | tf_op jit(solution)/shard_map/adjoint_middle/pallas_call | solution.py:379
  37.1 8.9 %collective-permute-start.6 = (f32[3,48,1024]{2,1,0:T(8,128)S(1)}, f32[3,48,1024]{2,1,0:T(8,128)S(1)}, u32[]{:S(2)}, u32[]{:S(2)}) collective-permute-start(f32[3,48,1024]{2,1,0:T(8,128)S(1)} %get-tuple-element.60), channel_id=1, source_target_pairs={{4,0},{8,4},{12,8},{16,12},{20,16},{24,20},{28,24},{32,28},{36,32}... | collective-permute-start | bytes 1769480 | tf_op jit(solution)/shard_map/ppermute | solution.py:282
  46.0 0.0 collective-permute-done.3.refs_9_
  46.1 0.0 copy-start.1
  46.1 0.0 copy-start.2
  46.1 1.7 %adjoint_edge.1 = (f32[3,16,1024]{2,1,0:T(8,128)S(1)}, f32[3,16,1024]{2,1,0:T(8,128)S(1)}) custom-call(s32[4]{0:T(128)S(1)} %pad_add_fusion.pos_ref.refs_0_, f32[80,1024]{1,0:T(8,128)S(1)} %get-tuple-element.46.refs_1_, f32[4,80,1024]{2,1,0:T(8,128)S(1)} %get-tuple-element.47.refs_2_, f32[4,80,1024]{2,1,0:T(8,128)S(1)} %get-tuple-element.48.refs_3_, ...), custom_call_target="tpu_custom_call" | custom-call | flops 60000002048 | bytes 180000000 | tf_op jit(solution)/shard_map/adjoint_edge/pallas_call | solution.py:379
  47.8 1.9 %collective-permute-start.5 = (f32[3,16,1024]{2,1,0:T(8,128)S(1)}, f32[3,16,1024]{2,1,0:T(8,128)S(1)}, u32[]{:S(2)}, u32[]{:S(2)}) collective-permute-start(f32[3,16,1024]{2,1,0:T(8,128)S(1)} %get-tuple-element.59), channel_id=1, source_target_pairs={{4,0},{8,4},{12,8},{16,12},{20,16},{24,20},{28,24},{32,28},{36,32}... | collective-permute-start | bytes 589832 | tf_op jit(solution)/shard_map/ppermute | solution.py:282
  49.8 1.8 %collective-permute-done.2 = f32[3,64,1024]{2,1,0:T(8,128)S(1)} collective-permute-done((f32[3,64,1024]{2,1,0:T(8,128)S(1)}, f32[3,64,1024]{2,1,0:T(8,128)S(1)}, u32[]{:S(2)}, u32[]{:S(2)}) %collective-permute-start.2) | collective-permute-done | bytes 786464 | tf_op jit(solution)/shard_map/ppermute | solution.py:282
  51.5 0.0 copy-done.1
  51.5 0.0 copy-done.2
  51.5 1.2 %fusion = f32[1,3,64,1024]{3,2,1,0:T(8,128)} fusion(f32[3,8,1024]{2,1,0:T(8,128)S(1)} %get-tuple-element.65, f32[3,48,1024]{2,1,0:T(8,128)S(1)} %get-tuple-element.58, f32[3,8,1024]{2,1,0:T(8,128)S(1)} %get-tuple-element.64, f32[3,64,1024]{2,1,0:T(8,128)S(1)} %copy-done.2, f32[3,64,1024]{2,1,0:T(8,128)S(1)} %collective-permute-done.2, pred[]{:T(512)S(6)} %eq.17, ...), kind=kLoop, calls=%fused_computation.1 | loop fusion | flops 1179648 | bytes 3932161 | tf_op jit(solution)/shard_map/broadcast_in_dim | solution.py:402
  52.7 8.5 %collective-permute-done.5 = f32[3,16,1024]{2,1,0:T(8,128)S(1)} collective-permute-done((f32[3,16,1024]{2,1,0:T(8,128)S(1)}, f32[3,16,1024]{2,1,0:T(8,128)S(1)}, u32[]{:S(2)}, u32[]{:S(2)}) %collective-permute-start.5) | collective-permute-done | bytes 196640 | tf_op jit(solution)/shard_map/ppermute | solution.py:282
  61.3 0.0 collective-permute-done.6
  61.3 1.0 %fusion.1 = f32[1,3,64,1024]{3,2,1,0:T(8,128)} fusion(f32[3,8,1024]{2,1,0:T(8,128)S(1)} %get-tuple-element.63, f32[3,48,1024]{2,1,0:T(8,128)S(1)} %collective-permute-done.6, f32[3,8,1024]{2,1,0:T(8,128)S(1)} %get-tuple-element.62, f32[3,64,1024]{2,1,0:T(8,128)S(1)} %get-tuple-element.45, f32[]{:T(128)S(6)} %select_n.16), kind=kLoop, calls=%fused_computation.3 | loop fusion | flops 786432 | bytes 2359300 | tf_op jit(solution)/shard_map/broadcast_in_dim | solution.py:402
  (3 shorter events, 0.0 us)
Async XLA Ops:
  0.6 5.3 %copy-start = (f32[1,3,64,1024]{3,2,1,0:T(8,128)S(1)}, f32[1,3,64,1024]{3,2,1,0:T(8,128)}, u32[]{:S(2)}) copy-start(f32[1,3,64,1024]{3,2,1,0:T(8,128)} %states_ref.3) | copy-start | bytes 2359300
  2.3 17.2 %collective-permute-start.1 = (f32[4,8,1024]{2,1,0:T(8,128)S(1)}, f32[4,8,1024]{2,1,0:T(8,128)S(1)}, u32[]{:S(2)}, u32[]{:S(2)}) collective-permute-start(f32[4,8,1024]{2,1,0:T(8,128)S(1)} %get-tuple-element.41), channel_id=1, source_target_pairs={{1,2},{2,1},{5,6},{6,5},{9,10},{10,9},{13,14},{14,13},{17,18},{18,... | collective-permute-start | bytes 393224 | tf_op jit(solution)/shard_map/ppermute | solution.py:331
  3.0 16.6 %collective-permute-start = (f32[4,8,1024]{2,1,0:T(8,128)S(1)}, f32[4,8,1024]{2,1,0:T(8,128)S(1)}, u32[]{:S(2)}, u32[]{:S(2)}) collective-permute-start(f32[4,8,1024]{2,1,0:T(8,128)S(1)} %get-tuple-element.40), channel_id=1, source_target_pairs={{0,1},{1,0},{2,3},{3,2},{4,5},{5,4},{6,7},{7,6},{8,9},{9,8},{10,11... | collective-permute-start | bytes 393224 | tf_op jit(solution)/shard_map/ppermute | solution.py:333
  5.9 28.0 %collective-permute-start.4 = (f32[3,64,1024]{2,1,0:T(8,128)S(1)}, f32[3,64,1024]{2,1,0:T(8,128)S(1)}, u32[]{:S(2)}, u32[]{:S(2)}) collective-permute-start(f32[3,64,1024]{2,1,0:T(8,128)S(1)} %bitcast.9), channel_id=1, source_target_pairs={{4,0},{8,4},{12,8},{16,12},{20,16},{24,20},{28,24},{32,28},{36,32}... | collective-permute-start | bytes 2359304 | tf_op jit(solution)/shard_map/ppermute | solution.py:282
  19.7 26.4 %collective-permute-start.3 = (f32[3,8,1024]{2,1,0:T(8,128)S(1)}, f32[3,8,1024]{2,1,0:T(8,128)S(1)}, u32[]{:S(2)}, u32[]{:S(2)}) collective-permute-start(f32[3,8,1024]{2,1,0:T(8,128)S(1)} %slice_select_fusion), channel_id=1, source_target_pairs={{4,0},{8,4},{12,8},{16,12},{20,16},{24,20},{28,24},{32,28},{36,32}... | collective-permute-start | bytes 294920 | tf_op jit(solution)/shard_map/ppermute | solution.py:282
  26.2 25.3 %collective-permute-start.2 = (f32[3,64,1024]{2,1,0:T(8,128)S(1)}, f32[3,64,1024]{2,1,0:T(8,128)S(1)}, u32[]{:S(2)}, u32[]{:S(2)}) collective-permute-start(f32[3,64,1024]{2,1,0:T(8,128)S(1)} %get-tuple-element.45), channel_id=1, source_target_pairs={{0,4},{4,8},{8,12},{12,16},{16,20},{20,24},{24,28},{28,32},{32,36}... | collective-permute-start | bytes 2359304 | tf_op jit(solution)/shard_map/ppermute | solution.py:282
  37.1 24.1 %collective-permute-start.6 = (f32[3,48,1024]{2,1,0:T(8,128)S(1)}, f32[3,48,1024]{2,1,0:T(8,128)S(1)}, u32[]{:S(2)}, u32[]{:S(2)}) collective-permute-start(f32[3,48,1024]{2,1,0:T(8,128)S(1)} %get-tuple-element.60), channel_id=1, source_target_pairs={{4,0},{8,4},{12,8},{16,12},{20,16},{24,20},{28,24},{32,28},{36,32}... | collective-permute-start | bytes 1769480 | tf_op jit(solution)/shard_map/ppermute | solution.py:282
  46.1 5.5 %copy-start.1 = (f32[1,3,64,1024]{3,2,1,0:T(8,128)S(1)}, f32[1,3,64,1024]{3,2,1,0:T(8,128)}, u32[]{:S(2)}) copy-start(f32[1,3,64,1024]{3,2,1,0:T(8,128)} %states_ref.3) | copy-start | bytes 2359300
  46.1 5.5 %copy-start.2 = (f32[3,64,1024]{2,1,0:T(8,128)S(1)}, f32[3,64,1024]{2,1,0:T(8,128)}, u32[]{:S(2)}) copy-start(f32[3,64,1024]{2,1,0:T(8,128)} %param.6) | copy-start | bytes 2359300
  47.8 13.4 %collective-permute-start.5 = (f32[3,16,1024]{2,1,0:T(8,128)S(1)}, f32[3,16,1024]{2,1,0:T(8,128)S(1)}, u32[]{:S(2)}, u32[]{:S(2)}) collective-permute-start(f32[3,16,1024]{2,1,0:T(8,128)S(1)} %get-tuple-element.59), channel_id=1, source_target_pairs={{4,0},{8,4},{12,8},{16,12},{20,16},{24,20},{28,24},{32,28},{36,32}... | collective-permute-start | bytes 589832 | tf_op jit(solution)/shard_map/ppermute | solution.py:282

commit v4 on v3

--- a/solution.py
+++ b/solution.py
@@ -53,7 +53,7 @@
 
 def prepare_kernel(
     pos_ref, states_ref, mask_ref, cells_ref, values_ref,
-    cross_ref, pair_ref, seen_ref, wanted_ref, bits, sems
+    cross_ref, pair_ref, seen_ref, wanted_ref, near_ref, far_ref, bits, sems
 ):
     strip = states_ref.shape[2]
     bottom = strip - HALO
@@ -69,6 +69,11 @@
                 states_ref.at[0, :, pl.ds(at, HALO)], out.at[pl.ds(0, 3)], sems.at[2 * n + 1]
             )
         )
+    cut = near_ref.shape[1]
+    copies.append(pltpu.make_async_copy(states_ref.at[0, :, pl.ds(0, cut)], near_ref, sems.at[6]))
+    copies.append(
+        pltpu.make_async_copy(states_ref.at[0, :, pl.ds(cut, strip - cut)], far_ref, sems.at[7])
+    )
     copies.append(pltpu.make_async_copy(cells_ref.at[0], seen_ref, sems.at[4]))
     copies.append(pltpu.make_async_copy(values_ref.at[0], wanted_ref, sems.at[5]))
     for copy in copies:
@@ -185,36 +190,36 @@
     ends_ref[...] = path_ref[NSTEP][:, HALO : HALO + strip]
 
 
+def near_blocks(blocks):
+    return blocks // 2 + 1
+
+
 def adjoint_kernel(part):
     def kernel(*refs):
-        if part == "middle":
-            pos_ref, land_ref, count_ref, total_ref, *path_ref = refs[: NSTEP + 5]
-            next_ref, out_ref, send_ref, work = refs[NSTEP + 5 :]
-        else:
-            pos_ref, land_ref, count_ref, total_ref, *path_ref = refs[: NSTEP + 5]
-            rim_ref, work_ref, out_ref, send_ref, work = refs[NSTEP + 5 :]
+        pos_ref, land_ref, count_ref, total_ref, *path_ref = refs[: NSTEP + 5]
+        ahead_ref = refs[NSTEP + 5]
+        out_ref, send_ref, work = refs[-3:]
         rows, columns = land_ref.shape
         blocks = rows // BLK
+        last = blocks - 2
+        cut = near_blocks(last)
         base = pos_ref[0]
         grid_rows = pos_ref[1]
         weight = jnp.where(pos_ref[2] == 1, 0.0, defect_weight).astype(jnp.float32)
         half = advect / 2.0
         keep = 1.0 - 4.0 * diffuse
-        edge = (0, 1, blocks - 2, blocks - 1)
-        if part == "middle":
-            first = range(1, blocks - 1)
-            inner = range(1, blocks - 1)
-            final = range(2, blocks - 2)
+        if part == "near":
+            first, inner, final = range(1, cut + 1), range(1, cut + 1), range(2, cut)
+            low, high = 1, cut
+        elif part == "far":
+            first, inner, final = range(cut + 1, last + 1), range(cut, last + 1), range(cut, last)
+            low, high = cut - 1, last
         else:
-            first = (0, blocks - 1)
-            inner = edge
-            final = (1, blocks - 2)
+            first, inner, final = (0, last + 1), (0, 1, last, last + 1), (1, last)
+            low, high = 0, last + 1
 
         def get(step, f, i):
-            at = slice(i * BLK, (i + 1) * BLK)
-            if part == "edge" and (i not in edge or (step == NSTEP - 1 and i in (1, blocks - 2))):
-                return work_ref[step, f, at]
-            return work[step, f, at]
+            return work[step, f, i * BLK : (i + 1) * BLK]
 
         def put(step, i, lam):
             at = slice(i * BLK, (i + 1) * BLK)
@@ -228,10 +233,11 @@
 
         for i in first:
             at = slice(i * BLK, (i + 1) * BLK)
-            if part == "middle":
-                ahead = [next_ref[f, (i - 1) * BLK : i * BLK] for f in range(3)]
+            if part == "edge":
+                ahead = [ahead_ref[f] for f in range(3)]
             else:
-                ahead = [rim_ref[f] for f in range(3)]
+                here = slice((i - first[0]) * BLK, (i - first[0] + 1) * BLK)
+                ahead = [ahead_ref[f, here] for f in range(3)]
             put(
                 NSTEP - 1,
                 i,
@@ -241,7 +247,7 @@
         for step in reversed(range(NSTEP)):
             for n, i in enumerate(inner if step > 0 else final):
                 at = slice(i * BLK, (i + 1) * BLK)
-                before, after = max(i - 1, first[0]), min(i + 1, first[-1])
+                before, after = max(i - 1, low), min(i + 1, high)
                 a, b, c = (get(step, f, i) for f in range(3))
                 a0, b0, c0 = (get(step, f, before) for f in range(3))
                 a2, b2, c2 = (get(step, f, after) for f in range(3))
@@ -276,6 +282,65 @@
     return kernel
 
 
+def settle_kernel(places):
+    def kernel(*refs):
+        pos_ref, ends_ref, got_ref = refs[:3]
+        out_ref, buffer, sems = refs[-3:]
+        share = jnp.where(pos_ref[2] == 1, 1.0, step_length * defect_weight).astype(jnp.float32)
+        copies = []
+        at = 0
+        for n, (low, height) in enumerate(places):
+            here = slice(at, at + height)
+            buffer[:, here] = got_ref[:, here] + share * ends_ref[:, low : low + height]
+            copies.append(
+                pltpu.make_async_copy(
+                    buffer.at[:, pl.ds(at, height)],
+                    out_ref.at[0, :, pl.ds(low, height)],
+                    sems.at[n],
+                )
+            )
+            copies[-1].start()
+            at += height
+        for copy in copies:
+            copy.wait()
+
+    return kernel
+
+
+def gradient_kernel(
+    pos_ref, start_ref, previous_ref, background_ref, near_ref, far_ref, edge_ref,
+    out_ref, buffer, held, sems
+):
+    strip = out_ref.shape[2]
+
+    def fill(source):
+        def place(low, height, source_adj):
+            here = slice(low, low + height)
+            state = start_ref[:, HALO + low : HALO + low + height]
+            buffer[:, here] = defect_weight * (state - source[:, here]) + source_adj
+
+        cut = BLK + near_ref.shape[1]
+        place(0, BLK, edge_ref[:, :BLK])
+        place(BLK, near_ref.shape[1], near_ref[...])
+        place(cut, far_ref.shape[1], far_ref[...])
+        place(strip - BLK, BLK, edge_ref[:, BLK:])
+
+    @pl.when(pos_ref[4] == 1)
+    def _():
+        copy = pltpu.make_async_copy(background_ref, held, sems.at[0])
+        copy.start()
+        copy.wait()
+        fill(held)
+
+    @pl.when(pos_ref[4] != 1)
+    def _():
+        fill(previous_ref)
+
+    copy = pltpu.make_async_copy(buffer, out_ref.at[0], sems.at[1])
+    copy.start()
+    copy.wait()
+
+
 def shifted(block, axis, distance):
     devices = range(lax.axis_size(axis))
     route = [(i - distance, i) for i in devices if i - distance in devices]
@@ -290,7 +355,13 @@
     base = lax.axis_index("space") * strip - HALO
     odd = lax.axis_index("space") & 1
     pos = jnp.stack(
-        [base, jnp.int32(strip) * lax.axis_size("space"), at_final.astype(jnp.int32), odd]
+        [
+            base,
+            jnp.int32(strip) * lax.axis_size("space"),
+            at_final.astype(jnp.int32),
+            odd,
+            at_first.astype(jnp.int32),
+        ]
     ).astype(jnp.int32)
     f32 = jnp.float32
 
@@ -303,34 +374,37 @@
         )
 
     observed = obs_cells.shape[2]
-    cross, pair, cells, values = pl.pallas_call(
+    cut = near_blocks(strip // BLK) * BLK
+    cross, pair, cells, values, near, far = pl.pallas_call(
         prepare_kernel,
         out_shape=(
             jax.ShapeDtypeStruct((4, HALO, columns), f32),
             jax.ShapeDtypeStruct((4, HALO, columns), f32),
             jax.ShapeDtypeStruct((NSTEP, observed), jnp.int32),
             jax.ShapeDtypeStruct((NSTEP, observed), f32),
+            jax.ShapeDtypeStruct((3, cut, columns), f32),
+            jax.ShapeDtypeStruct((3, strip - cut, columns), f32),
         ),
         in_specs=[smem()] + [hbm()] * 4,
-        out_specs=(vmem(),) * 4,
+        out_specs=(vmem(),) * 6,
         scratch_shapes=[
             pltpu.VMEM((2, HALO, columns), jnp.int32),
-            pltpu.SemaphoreType.DMA((6,)),
+            pltpu.SemaphoreType.DMA((8,)),
         ],
         compiler_params=params(8),
         cost_estimate=cost(0.5),
         name="prepare",
     )(pos, *(off_chip(x) for x in (states, land_mask, obs_cells, obs_values)))
-    share = jnp.where(at_final, 1.0, step_length * defect_weight).astype(f32)
-    cross, pair, moving, pos, at_first, share, even = lax.optimization_barrier(
-        (cross, pair, states[0], pos, at_first, share, odd == 0)
+    cross, pair, near, far, pos, even = lax.optimization_barrier(
+        (cross, pair, near, far, pos, odd == 0)
     )
     strips = lax.axis_size("space")
     inner = [(i, i ^ 1) for i in range(strips)]
     outer = [(i, j) for i in range(strips) for j in [((i + 1) ^ 1) - 1] if 0 <= j < strips]
     cross = lax.ppermute(cross, "space", outer)
-    ahead = shifted(moving, "tm", -1)
     pair = lax.ppermute(pair, "space", inner)
+    far = shifted(far, "tm", -1)
+    near = shifted(near, "tm", -1)
 
     count, total, start, bits = pl.pallas_call(
         maps_kernel,
@@ -349,7 +423,7 @@
     )(pos, cells, values, off_chip(states), off_chip(land_mask))
 
     row = lax.broadcasted_iota(jnp.int32, (3, HALO, columns), 1)
-    rim = jnp.where((row < HALO // 2) == even, pair[:3], cross[:3])
+    rim = jnp.where((row < HALO // 2) != even, cross[:3], pair[:3])
     rim, cross, pair = lax.optimization_barrier((rim, cross, pair))
     rim = shifted(rim, "tm", -1)
 
@@ -371,35 +445,61 @@
     previous = shifted(ends, "tm", 1)
 
     def adjoint(part, height, *operands):
-        shapes = [jax.ShapeDtypeStruct((3, height, columns), f32)] * 2
-        scratch = [pltpu.VMEM((NSTEP, 3, rows, columns), f32)]
-        if part == "middle":
-            shapes.append(jax.ShapeDtypeStruct((NSTEP, 3, rows, columns), f32))
-            scratch = []
+        work = jax.ShapeDtypeStruct((NSTEP, 3, rows, columns), f32)
         return pl.pallas_call(
             adjoint_kernel(part),
-            out_shape=tuple(shapes),
+            out_shape=(jax.ShapeDtypeStruct((3, height, columns), f32),) * 2 + (work,),
             in_specs=[smem()] + [vmem()] * len(operands),
-            out_specs=(vmem(),) * len(shapes),
-            scratch_shapes=scratch,
+            out_specs=(vmem(),) * 3,
+            input_output_aliases={} if part == "near" else {len(operands): 2},
             compiler_params=params(24),
-            cost_estimate=cost(0.1 if part == "middle" else 60),
+            cost_estimate=cost({"near": 0.1, "far": 60, "edge": 0.5}[part]),
             name="adjoint_" + part,
         )(pos, *operands)
 
     shared = (land, count, total, *path)
-    mid_adj, mid_send, work = adjoint("middle", strip - 2 * BLK, *shared, ahead)
-    mid_next = shifted(mid_send, "tm", -1)
-    edge_adj, edge_send = adjoint("edge", 2 * BLK, *shared, rim, work)
-    edge_next = shifted(edge_send, "tm", -1)
-
-    def joined(middle, edge):
-        return jnp.concatenate([edge[:, :BLK], middle, edge[:, BLK:]], axis=1)
-
-    previous = jnp.where(at_first, background, previous)
-    gradient = defect_weight * (states[0] - previous) + joined(mid_adj, edge_adj)
-    next_state = joined(mid_next, edge_next) + share * ends
-    return (gradient[None], next_state[None])
+    first, near_send, work = adjoint("near", cut - 2 * BLK, *shared, near)
+    second, far_send, work = adjoint("far", strip - cut, *shared, far, work)
+    outer, edge_send, work = adjoint("edge", 2 * BLK, *shared, rim, work)
+    edge_sent = shifted(edge_send, "tm", -1)
+    far_sent = shifted(far_send, "tm", -1)
+    near_sent = shifted(near_send, "tm", -1)
+
+    def settle(name, places, arrived, *held):
+        height = arrived.shape[1]
+        return pl.pallas_call(
+            settle_kernel(places),
+            out_shape=jax.ShapeDtypeStruct(states.shape, f32),
+            in_specs=[smem()] + [vmem()] * 2 + [hbm()] * len(held),
+            out_specs=hbm(),
+            scratch_shapes=[
+                pltpu.VMEM((3, height, columns), f32),
+                pltpu.SemaphoreType.DMA((len(places),)),
+            ],
+            input_output_aliases={3: 0} if held else {},
+            compiler_params=params(8),
+            cost_estimate=cost(0.01),
+            name="settle_" + name,
+        )(pos, ends, arrived, *(off_chip(x) for x in held))
+
+    gradient = pl.pallas_call(
+        gradient_kernel,
+        out_shape=jax.ShapeDtypeStruct(states.shape, f32),
+        in_specs=[smem(), vmem(), vmem(), hbm(), vmem(), vmem(), vmem()],
+        out_specs=hbm(),
+        scratch_shapes=[
+            pltpu.VMEM((3, strip, columns), f32),
+            pltpu.VMEM((3, strip, columns), f32),
+            pltpu.SemaphoreType.DMA((2,)),
+        ],
+        compiler_params=params(12),
+        cost_estimate=cost(0.01),
+        name="gradient",
+    )(pos, path[0], previous, off_chip(background), first, second, outer)
+    next_state = settle("near", [(BLK, cut - 2 * BLK)], near_sent)
+    next_state = settle("far", [(cut - BLK, strip - cut)], far_sent, next_state, gradient)
+    next_state = settle("edge", [(0, BLK), (strip - BLK, BLK)], edge_sent, next_state)
+    return (gradient, next_state)
 
 
 def solution(mesh):

time: 62.5 us -> 59.3 us (0.949)
  waiting for transfers between devices: 15.1 us -> 4.16 us
  Pallas kernels: 13.6 us -> 20.1 us
  starting transfers between devices: 30.4 us -> 33.7 us
  other arithmetic: 2.33 us -> 0.09 us
    ppermute x5 -> x7, waiting for transfers between devices: 15.1 us -> 4.15 us  [shifted(): return lax.ppermute(block, axis, route)]
    pallas_call x2 -> x7, Pallas kernels: 4.9 us -> 11.1 us  [the longest x3 5.74 us: adjoint(): pl.pallas_call(adjoint_kernel(part), out_shape=(jax.ShapeDtypeStruct((3,...]
    ppermute x5 -> x7, starting transfers between devices: 26.8 us -> 30.1 us  [shifted(): return lax.ppermute(block, axis, route)]
    broadcast_in_dim x2 -> x0, other arithmetic: 2.16 us -> none  [local(): return (gradient[None], next_state[None])]
  transfers between devices with their start and end apart: 7 -> 9, of which waited for: 3 -> 2; matrix products, arithmetic and copies ran while one was open for 2% -> 0% of each run, Pallas kernels for 19% -> 29%
where the time goes in v4:
time: 59.3 us; the launch traced here: 59 us
  starting transfers between devices  33.7 us (57%)
  Pallas kernels  20.1 us (34%)
  waiting for transfers between devices  4.16 us (7%)
  between operations  0.83 us (1%)
    ppermute x7, starting transfers between devices, shifted(): return lax.ppermute(block, axis, route)  30.1 us
    pallas_call x3, Pallas kernels, adjoint(): pl.pallas_call(adjoint_kernel(part), out_shape=(jax.ShapeDtypeStruct((3,...  5.74 us
    ppermute x7, waiting for transfers between devices, shifted(): return lax.ppermute(block, axis, route)  4.15 us
    pallas_call x3, Pallas kernels, settle(): pl.pallas_call(settle_kernel(places), out_shape=jax.ShapeDtypeStruct(stat...  3.84 us
    pallas_call x1, Pallas kernels, local(): pl.pallas_call(forward_kernel, out_shape=(jax.ShapeDtypeStruct((rows, col...  3.64 us
    pallas_call x1, Pallas kernels, local(): pl.pallas_call(maps_kernel, out_shape=(jax.ShapeDtypeStruct((NSTEP, rows,...  3.48 us
    ppermute x1, starting transfers between devices, local(): pair = lax.ppermute(pair, 'space', inner)  2.93 us
    pallas_call x1, Pallas kernels, local(): pl.pallas_call(prepare_kernel, out_shape=(jax.ShapeDtypeStruct((4, HALO,...  1.87 us
  transfers between devices with their start and end apart: 9, of which 2 were waited for; matrix products, arithmetic and copies ran while one was open for 0% of the time, Pallas kernels for 29%

profile of v4, /device:TPU:24, one launch (start us, length us, event | category | flops | bytes accessed | tf_op | source)
XLA Modules:
  0.0 59.0 jit_solution(9695355741692418470)
XLA Ops:
  0.6 0.1 stack.27.pos_ref.refs_0_
  0.7 1.9 %prepare.1 = (f32[4,8,1024]{2,1,0:T(8,128)S(1)}, f32[4,8,1024]{2,1,0:T(8,128)S(1)}, s32[4,1024]{1,0:T(4,128)S(1)}, f32[4,1024]{1,0:T(4,128)S(1)}, f32[3,40,1024]...) custom-call(s32[5]{0:T(128)S(1)} %stack.27.pos_ref.refs_0_, f32[1,3,64,1024]{3,2,1,0:T(8,128)} %states_ref.3, ...), custom_call_target="tpu_custom_call" | custom-call | flops 500000000 | bytes 1500000 | tf_op jit(solution)/shard_map/prepare/pallas_call | solution.py:378
  2.6 0.7 %collective-permute-start = (f32[4,8,1024]{2,1,0:T(8,128)S(1)}, f32[4,8,1024]{2,1,0:T(8,128)S(1)}, u32[]{:S(2)}, u32[]{:S(2)}) collective-permute-start(f32[4,8,1024]{2,1,0:T(8,128)S(1)} %get-tuple-element.45), channel_id=1, source_target_pairs={{1,2},{2,1},{5,6},{6,5},{9,10},{10,9},{13,14},{14,13},{17,18},{18,... | collective-permute-start | bytes 393224 | tf_op jit(solution)/shard_map/ppermute | solution.py:404
  3.3 2.9 %collective-permute-start.1 = (f32[4,8,1024]{2,1,0:T(8,128)S(1)}, f32[4,8,1024]{2,1,0:T(8,128)S(1)}, u32[]{:S(2)}, u32[]{:S(2)}) collective-permute-start(f32[4,8,1024]{2,1,0:T(8,128)S(1)} %get-tuple-element.46), channel_id=1, source_target_pairs={{0,1},{1,0},{2,3},{3,2},{4,5},{5,4},{6,7},{7,6},{8,9},{9,8},{10,11... | collective-permute-start | bytes 393224 | tf_op jit(solution)/shard_map/ppermute | solution.py:405
  6.2 10.1 %collective-permute-start.3 = (f32[3,40,1024]{2,1,0:T(8,128)S(1)}, f32[3,40,1024]{2,1,0:T(8,128)S(1)}, u32[]{:S(2)}, u32[]{:S(2)}) collective-permute-start(f32[3,40,1024]{2,1,0:T(8,128)S(1)} %get-tuple-element.59), channel_id=1, source_target_pairs={{4,0},{8,4},{12,8},{16,12},{20,16},{24,20},{28,24},{32,28},{36,32}... | collective-permute-start | bytes 1474568 | tf_op jit(solution)/shard_map/ppermute | solution.py:347
  16.3 2.9 %collective-permute-start.4 = (f32[3,24,1024]{2,1,0:T(8,128)S(1)}, f32[3,24,1024]{2,1,0:T(8,128)S(1)}, u32[]{:S(2)}, u32[]{:S(2)}) collective-permute-start(f32[3,24,1024]{2,1,0:T(8,128)S(1)} %get-tuple-element.61), channel_id=1, source_target_pairs={{4,0},{8,4},{12,8},{16,12},{20,16},{24,20},{28,24},{32,28},{36,32}... | collective-permute-start | bytes 884744 | tf_op jit(solution)/shard_map/ppermute | solution.py:347
  19.2 3.5 %maps.1 = (f32[4,80,1024]{2,1,0:T(8,128)S(1)}, f32[4,80,1024]{2,1,0:T(8,128)S(1)}, f32[3,80,1024]{2,1,0:T(8,128)S(1)}, s32[64,1024]{1,0:T(8,128)S(1)}) custom-call(s32[5]{0:T(128)S(1)} %stack.27.pos_ref.refs_0_, s32[4,1024]{1,0:T(4,128)S(1)} %get-tuple-element.41.cells_ref, f32[4,1024]{1,0:T(4,128)S(1)} %get-tuple-element.42.values_ref, ...), custom_call_target="tpu_custom_call" | custom-call | flops 4000000000 | bytes 12000000 | tf_op jit(solution)/shard_map/maps/pallas_call | solution.py:409
  22.8 0.0 collective-permute-done.cross_ref
  22.8 0.0 collective-permute-done.1.pair_ref
  22.8 0.1 slice_select_fusion
  22.9 2.9 %collective-permute-start.5 = (f32[3,8,1024]{2,1,0:T(8,128)S(1)}, f32[3,8,1024]{2,1,0:T(8,128)S(1)}, u32[]{:S(2)}, u32[]{:S(2)}) collective-permute-start(f32[3,8,1024]{2,1,0:T(8,128)S(1)} %slice_select_fusion), channel_id=1, source_target_pairs={{4,0},{8,4},{12,8},{16,12},{20,16},{24,20},{28,24},{32,28},{36,32}... | collective-permute-start | bytes 294920 | tf_op jit(solution)/shard_map/ppermute | solution.py:347
  25.8 3.6 %forward.1 = (f32[80,1024]{1,0:T(8,128)S(1)}, f32[3,64,1024]{2,1,0:T(8,128)S(1)}, f32[3,80,1024]{2,1,0:T(8,128)S(1)}, f32[3,80,1024]{2,1,0:T(8,128)S(1)}, f32[3,...) custom-call(s32[5]{0:T(128)S(1)} %stack.27.pos_ref.refs_0_, ...), custom_call_target="tpu_custom_call", output_to_operand_aliasing={{2}: (1, {})} | custom-call | flops 2000000000 | bytes 6000000 | tf_op jit(solution)/shard_map/forward/pallas_call | solution.py:430
  29.4 2.9 %collective-permute-start.2 = (f32[3,64,1024]{2,1,0:T(8,128)S(1)}, f32[3,64,1024]{2,1,0:T(8,128)S(1)}, u32[]{:S(2)}, u32[]{:S(2)}) collective-permute-start(f32[3,64,1024]{2,1,0:T(8,128)S(1)} %get-tuple-element.51.refs_1_), channel_id=1, source_target_pairs={{0,4},{4,8},{8,12},{12,16},{16,20},{20,24},{24,28},{28,32},{32,36}... | collective-permute-start | bytes 2359304 | tf_op jit(solution)/shard_map/ppermute | solution.py:347
  32.3 0.0 collective-permute-done.3.refs_9_
  32.4 2.1 %adjoint_near.1 = (f32[3,24,1024]{2,1,0:T(8,128)S(1)}, f32[3,24,1024]{2,1,0:T(8,128)S(1)}, f32[4,3,80,1024]{3,2,1,0:T(8,128)S(1)}) custom-call(s32[5]{0:T(128)S(1)} %stack.27.pos_ref.refs_0_, f32[80,1024]{1,0:T(8,128)S(1)} %get-tuple-element.52.refs_1_, f32[4,80,1024]{2,1,0:T(8,128)S(1)} %get-tuple-element.53.refs_2_, ...), custom_call_target="tpu_custom_call" | custom-call | flops 100000000 | bytes 300000 | tf_op jit(solution)/shard_map/adjoint_near/pallas_call | solution.py:449
  34.5 7.4 %collective-permute-start.8 = (f32[3,24,1024]{2,1,0:T(8,128)S(1)}, f32[3,24,1024]{2,1,0:T(8,128)S(1)}, u32[]{:S(2)}, u32[]{:S(2)}) collective-permute-start(f32[3,24,1024]{2,1,0:T(8,128)S(1)} %get-tuple-element.69), channel_id=1, source_target_pairs={{4,0},{8,4},{12,8},{16,12},{20,16},{24,20},{28,24},{32,28},{36,32}... | collective-permute-start | bytes 884744 | tf_op jit(solution)/shard_map/ppermute | solution.py:347
  41.9 0.0 collective-permute-done.4.refs_9_
  41.9 1.9 %adjoint_far.1 = (f32[3,24,1024]{2,1,0:T(8,128)S(1)}, f32[3,24,1024]{2,1,0:T(8,128)S(1)}, f32[4,3,80,1024]{3,2,1,0:T(8,128)S(1)}) custom-call(s32[5]{0:T(128)S(1)} %stack.27.pos_ref.refs_0_, f32[80,1024]{1,0:T(8,128)S(1)} %get-tuple-element.52.refs_1_, f32[4,80,1024]{2,1,0:T(8,128)S(1)} %get-tuple-element.53.refs_2_, ...), custom_call_target="tpu_custom_call", output_to_operand_aliasing={{2}: (10, {})} | custom-call | flops 60000002048 | bytes 180000000 | tf_op jit(solution)/shard_map/adjoint_far/pallas_call | solution.py:449
  43.8 1.9 %collective-permute-start.7 = (f32[3,24,1024]{2,1,0:T(8,128)S(1)}, f32[3,24,1024]{2,1,0:T(8,128)S(1)}, u32[]{:S(2)}, u32[]{:S(2)}) collective-permute-start(f32[3,24,1024]{2,1,0:T(8,128)S(1)} %get-tuple-element.68), channel_id=1, source_target_pairs={{4,0},{8,4},{12,8},{16,12},{20,16},{24,20},{28,24},{32,28},{36,32}... | collective-permute-start | bytes 884744 | tf_op jit(solution)/shard_map/ppermute | solution.py:347
  45.7 0.0 collective-permute-done.5.refs_9_
  45.7 1.8 %adjoint_edge.1 = (f32[3,16,1024]{2,1,0:T(8,128)S(1)}, f32[3,16,1024]{2,1,0:T(8,128)S(1)}, f32[4,3,80,1024]{3,2,1,0:T(8,128)S(1)}) custom-call(s32[5]{0:T(128)S(1)} %stack.27.pos_ref.refs_0_, f32[80,1024]{1,0:T(8,128)S(1)} %get-tuple-element.52.refs_1_, f32[4,80,1024]{2,1,0:T(8,128)S(1)} %get-tuple-element.53.refs_2_, ...), custom_call_target="tpu_custom_call", output_to_operand_aliasing={{2}: (10, {})} | custom-call | flops 500000000 | bytes 1500000 | tf_op jit(solution)/shard_map/adjoint_edge/pallas_call | solution.py:449
  47.5 1.9 %collective-permute-start.6 = (f32[3,16,1024]{2,1,0:T(8,128)S(1)}, f32[3,16,1024]{2,1,0:T(8,128)S(1)}, u32[]{:S(2)}, u32[]{:S(2)}) collective-permute-start(f32[3,16,1024]{2,1,0:T(8,128)S(1)} %get-tuple-element.67), channel_id=1, source_target_pairs={{4,0},{8,4},{12,8},{16,12},{20,16},{24,20},{28,24},{32,28},{36,32}... | collective-permute-start | bytes 589832 | tf_op jit(solution)/shard_map/ppermute | solution.py:347
  49.4 0.0 collective-permute-done.8.refs_2_
  49.4 1.3 %settle_near.1.refs_3_ = f32[1,3,64,1024]{3,2,1,0:T(8,128)} custom-call(s32[5]{0:T(128)S(1)} %stack.27.pos_ref.refs_0_, f32[3,64,1024]{2,1,0:T(8,128)S(1)} %get-tuple-element.51.refs_1_, f32[3,24,1024]{2,1,0:T(8,128)S(1)} %collective-permute-done.8.refs_2_), custom_call_target="tpu_custom_call" | custom-call | flops 10000000 | bytes 30000 | tf_op jit(solution)/shard_map/settle_near/pallas_call | solution.py:470
  50.7 3.7 %collective-permute-done.2.previous_ref = f32[3,64,1024]{2,1,0:T(8,128)S(1)} collective-permute-done((f32[3,64,1024]{2,1,0:T(8,128)S(1)}, f32[3,64,1024]{2,1,0:T(8,128)S(1)}, u32[]{:S(2)}, u32[]{:S(2)}) %collective-permute-start.2) | collective-permute-done | bytes 786464 | tf_op jit(solution)/shard_map/ppermute | solution.py:347
  54.4 1.6 %gradient.1.refs_4_ = f32[1,3,64,1024]{3,2,1,0:T(8,128)} custom-call(s32[5]{0:T(128)S(1)} %stack.27.pos_ref.refs_0_, f32[3,80,1024]{2,1,0:T(8,128)S(1)} %get-tuple-element.50.refs_4_.start_ref, f32[3,64,1024]{2,1,0:T(8,128)S(1)} %collective-permute-done.2.previous_ref, f32[3,64,1024]{2,1,0:T(8,128)} %background_ref.1, ...), custom_call_target="tpu_custom_call" | custom-call | flops 10000000 | bytes 30000 | tf_op jit(solution)/shard_map/gradient/pallas_call | solution.py:485
  56.0 0.0 collective-permute-done.7.refs_2_
  56.0 1.3 %settle_far.1.refs_3_ = f32[1,3,64,1024]{3,2,1,0:T(8,128)} custom-call(s32[5]{0:T(128)S(1)} %stack.27.pos_ref.refs_0_, f32[3,64,1024]{2,1,0:T(8,128)S(1)} %get-tuple-element.51.refs_1_, f32[3,24,1024]{2,1,0:T(8,128)S(1)} %collective-permute-done.7.refs_2_, f32[1,3,64,1024]{3,2,1,0:T(8,128)} %settle_near.1.refs_3_, ...), custom_call_target="tpu_custom_call", output_to_operand_aliasing={{}: (3, {})} | custom-call | flops 10000000 | bytes 30000 | tf_op jit(solution)/shard_map/settle_far/pallas_call | solution.py:470
  57.3 0.4 collective-permute-done.6.refs_2_
  57.8 1.2 %settle_edge.1 = f32[1,3,64,1024]{3,2,1,0:T(8,128)} custom-call(s32[5]{0:T(128)S(1)} %stack.27.pos_ref.refs_0_, f32[3,64,1024]{2,1,0:T(8,128)S(1)} %get-tuple-element.51.refs_1_, f32[3,16,1024]{2,1,0:T(8,128)S(1)} %collective-permute-done.6.refs_2_, f32[1,3,64,1024]{3,2,1,0:T(8,128)} %settle_far.1.refs_3_), custom_call_target="tpu_custom_call", output_to_operand_aliasing={{}: (3, {})} | custom-call | flops 10000000 | bytes 30000 | tf_op jit(solution)/shard_map/settle_edge/pallas_call | solution.py:470
  (1 shorter events, 0.0 us)
Async XLA Ops:
  2.6 20.1 %collective-permute-start = (f32[4,8,1024]{2,1,0:T(8,128)S(1)}, f32[4,8,1024]{2,1,0:T(8,128)S(1)}, u32[]{:S(2)}, u32[]{:S(2)}) collective-permute-start(f32[4,8,1024]{2,1,0:T(8,128)S(1)} %get-tuple-element.45), channel_id=1, source_target_pairs={{1,2},{2,1},{5,6},{6,5},{9,10},{10,9},{13,14},{14,13},{17,18},{18,... | collective-permute-start | bytes 393224 | tf_op jit(solution)/shard_map/ppermute | solution.py:404
  3.3 19.5 %collective-permute-start.1 = (f32[4,8,1024]{2,1,0:T(8,128)S(1)}, f32[4,8,1024]{2,1,0:T(8,128)S(1)}, u32[]{:S(2)}, u32[]{:S(2)}) collective-permute-start(f32[4,8,1024]{2,1,0:T(8,128)S(1)} %get-tuple-element.46), channel_id=1, source_target_pairs={{0,1},{1,0},{2,3},{3,2},{4,5},{5,4},{6,7},{7,6},{8,9},{9,8},{10,11... | collective-permute-start | bytes 393224 | tf_op jit(solution)/shard_map/ppermute | solution.py:405
  6.2 26.1 %collective-permute-start.3 = (f32[3,40,1024]{2,1,0:T(8,128)S(1)}, f32[3,40,1024]{2,1,0:T(8,128)S(1)}, u32[]{:S(2)}, u32[]{:S(2)}) collective-permute-start(f32[3,40,1024]{2,1,0:T(8,128)S(1)} %get-tuple-element.59), channel_id=1, source_target_pairs={{4,0},{8,4},{12,8},{16,12},{20,16},{24,20},{28,24},{32,28},{36,32}... | collective-permute-start | bytes 1474568 | tf_op jit(solution)/shard_map/ppermute | solution.py:347
  16.3 25.6 %collective-permute-start.4 = (f32[3,24,1024]{2,1,0:T(8,128)S(1)}, f32[3,24,1024]{2,1,0:T(8,128)S(1)}, u32[]{:S(2)}, u32[]{:S(2)}) collective-permute-start(f32[3,24,1024]{2,1,0:T(8,128)S(1)} %get-tuple-element.61), channel_id=1, source_target_pairs={{4,0},{8,4},{12,8},{16,12},{20,16},{24,20},{28,24},{32,28},{36,32}... | collective-permute-start | bytes 884744 | tf_op jit(solution)/shard_map/ppermute | solution.py:347
  22.9 22.9 %collective-permute-start.5 = (f32[3,8,1024]{2,1,0:T(8,128)S(1)}, f32[3,8,1024]{2,1,0:T(8,128)S(1)}, u32[]{:S(2)}, u32[]{:S(2)}) collective-permute-start(f32[3,8,1024]{2,1,0:T(8,128)S(1)} %slice_select_fusion), channel_id=1, source_target_pairs={{4,0},{8,4},{12,8},{16,12},{20,16},{24,20},{28,24},{32,28},{36,32}... | collective-permute-start | bytes 294920 | tf_op jit(solution)/shard_map/ppermute | solution.py:347
  29.4 25.0 %collective-permute-start.2 = (f32[3,64,1024]{2,1,0:T(8,128)S(1)}, f32[3,64,1024]{2,1,0:T(8,128)S(1)}, u32[]{:S(2)}, u32[]{:S(2)}) collective-permute-start(f32[3,64,1024]{2,1,0:T(8,128)S(1)} %get-tuple-element.51.refs_1_), channel_id=1, source_target_pairs={{0,4},{4,8},{8,12},{12,16},{16,20},{20,24},{24,28},{28,32},{32,36}... | collective-permute-start | bytes 2359304 | tf_op jit(solution)/shard_map/ppermute | solution.py:347
  34.5 14.9 %collective-permute-start.8 = (f32[3,24,1024]{2,1,0:T(8,128)S(1)}, f32[3,24,1024]{2,1,0:T(8,128)S(1)}, u32[]{:S(2)}, u32[]{:S(2)}) collective-permute-start(f32[3,24,1024]{2,1,0:T(8,128)S(1)} %get-tuple-element.69), channel_id=1, source_target_pairs={{4,0},{8,4},{12,8},{16,12},{20,16},{24,20},{28,24},{32,28},{36,32}... | collective-permute-start | bytes 884744 | tf_op jit(solution)/shard_map/ppermute | solution.py:347
  43.8 12.2 %collective-permute-start.7 = (f32[3,24,1024]{2,1,0:T(8,128)S(1)}, f32[3,24,1024]{2,1,0:T(8,128)S(1)}, u32[]{:S(2)}, u32[]{:S(2)}) collective-permute-start(f32[3,24,1024]{2,1,0:T(8,128)S(1)} %get-tuple-element.68), channel_id=1, source_target_pairs={{4,0},{8,4},{12,8},{16,12},{20,16},{24,20},{28,24},{32,28},{36,32}... | collective-permute-start | bytes 884744 | tf_op jit(solution)/shard_map/ppermute | solution.py:347
  47.5 10.3 %collective-permute-start.6 = (f32[3,16,1024]{2,1,0:T(8,128)S(1)}, f32[3,16,1024]{2,1,0:T(8,128)S(1)}, u32[]{:S(2)}, u32[]{:S(2)}) collective-permute-start(f32[3,16,1024]{2,1,0:T(8,128)S(1)} %get-tuple-element.67), channel_id=1, source_target_pairs={{4,0},{8,4},{12,8},{16,12},{20,16},{24,20},{28,24},{32,28},{36,32}... | collective-permute-start | bytes 589832 | tf_op jit(solution)/shard_map/ppermute | solution.py:347

commit v5 on v4

--- a/solution.py
+++ b/solution.py
@@ -8,6 +8,7 @@
 NSTEP = 4
 HALO = 8
 BLK = 8
+RING = 8
 
 advect = 0.25
 coriolis = 0.1
@@ -51,52 +52,7 @@
     return pltpu.roll(jnp.where(last, before, x), 1, axis=0)
 
 
-def prepare_kernel(
-    pos_ref, states_ref, mask_ref, cells_ref, values_ref,
-    cross_ref, pair_ref, seen_ref, wanted_ref, near_ref, far_ref, bits, sems
-):
-    strip = states_ref.shape[2]
-    bottom = strip - HALO
-    odd = pos_ref[3]
-    copies = []
-    for n, (out, at) in enumerate(((cross_ref, odd * bottom), (pair_ref, (1 - odd) * bottom))):
-        at = pl.multiple_of(at, HALO)
-        copies.append(
-            pltpu.make_async_copy(mask_ref.at[pl.ds(at, HALO)], bits.at[n], sems.at[2 * n])
-        )
-        copies.append(
-            pltpu.make_async_copy(
-                states_ref.at[0, :, pl.ds(at, HALO)], out.at[pl.ds(0, 3)], sems.at[2 * n + 1]
-            )
-        )
-    cut = near_ref.shape[1]
-    copies.append(pltpu.make_async_copy(states_ref.at[0, :, pl.ds(0, cut)], near_ref, sems.at[6]))
-    copies.append(
-        pltpu.make_async_copy(states_ref.at[0, :, pl.ds(cut, strip - cut)], far_ref, sems.at[7])
-    )
-    copies.append(pltpu.make_async_copy(cells_ref.at[0], seen_ref, sems.at[4]))
-    copies.append(pltpu.make_async_copy(values_ref.at[0], wanted_ref, sems.at[5]))
-    for copy in copies:
-        copy.start()
-    for copy in copies:
-        copy.wait()
-    cross_ref[3] = bits[0].astype(jnp.float32)
-    pair_ref[3] = bits[1].astype(jnp.float32)
-
-
-def maps_kernel(
-    pos_ref, cells_ref, values_ref, states_ref, mask_ref,
-    count_ref, total_ref, start_ref, bits_ref, sems
-):
-    strip = mask_ref.shape[0]
-    copies = (
-        pltpu.make_async_copy(
-            states_ref.at[0], start_ref.at[:, pl.ds(HALO, strip)], sems.at[0]
-        ),
-        pltpu.make_async_copy(mask_ref, bits_ref, sems.at[1]),
-    )
-    for copy in copies:
-        copy.start()
+def fill_maps(pos_ref, cells_ref, values_ref, count_ref, total_ref):
     rows, columns = count_ref.shape[1:]
     observed = cells_ref.shape[1]
     shift = columns.bit_length() - 1
@@ -132,8 +88,65 @@
             total_ref[step, :, start : start + width] = (
                 out[rows : 2 * rows] + out[2 * rows : 3 * rows] + out[3 * rows :]
             )
+
+
+def maps_kernel(
+    pos_ref, cells_ref, values_ref, states_ref, mask_ref, early_count_ref, early_total_ref,
+    count_ref, total_ref, start_ref, bits_ref, sems
+):
+    strip = mask_ref.shape[0]
+    copies = (
+        pltpu.make_async_copy(
+            states_ref.at[0], start_ref.at[:, pl.ds(HALO, strip)], sems.at[0]
+        ),
+        pltpu.make_async_copy(mask_ref, bits_ref, sems.at[1]),
+    )
+    for copy in copies:
+        copy.start()
+
+    @pl.when(pos_ref[5] == 0)
+    def _():
+        fill_maps(pos_ref, cells_ref, values_ref, count_ref, total_ref)
+
     for copy in copies:
         copy.wait()
+
+
+def prepare_kernel(
+    pos_ref, states_ref, mask_ref, cells_ref, values_ref,
+    cross_ref, pair_ref, seen_ref, wanted_ref, near_ref, far_ref, count_ref, total_ref, bits, sems
+):
+    strip = states_ref.shape[2]
+    bottom = strip - HALO
+    odd = pos_ref[3]
+    copies = []
+    for n, (out, at) in enumerate(((cross_ref, odd * bottom), (pair_ref, (1 - odd) * bottom))):
+        at = pl.multiple_of(at, HALO)
+        copies.append(
+            pltpu.make_async_copy(mask_ref.at[pl.ds(at, HALO)], bits.at[n], sems.at[2 * n])
+        )
+        copies.append(
+            pltpu.make_async_copy(
+                states_ref.at[0, :, pl.ds(at, HALO)], out.at[pl.ds(0, 3)], sems.at[2 * n + 1]
+            )
+        )
+    cut = near_ref.shape[1]
+    copies.append(pltpu.make_async_copy(states_ref.at[0, :, pl.ds(0, cut)], near_ref, sems.at[6]))
+    copies.append(
+        pltpu.make_async_copy(states_ref.at[0, :, pl.ds(cut, strip - cut)], far_ref, sems.at[7])
+    )
+    copies.append(pltpu.make_async_copy(cells_ref.at[0], seen_ref, sems.at[4]))
+    copies.append(pltpu.make_async_copy(values_ref.at[0], wanted_ref, sems.at[5]))
+    for copy in copies:
+        copy.start()
+    for copy in copies:
+        copy.wait()
+    cross_ref[3] = bits[0].astype(jnp.float32)
+    pair_ref[3] = bits[1].astype(jnp.float32)
+
+    @pl.when(pos_ref[5] != 0)
+    def _():
+        fill_maps(pos_ref, seen_ref, wanted_ref, count_ref, total_ref)
 
 
 def forward_kernel(
@@ -361,6 +374,7 @@
             at_final.astype(jnp.int32),
             odd,
             at_first.astype(jnp.int32),
+            ((lax.axis_index("tm") & (RING - 1) < 2) & (lax.axis_index("tm") >= RING)).astype(jnp.int32),
         ]
     ).astype(jnp.int32)
     f32 = jnp.float32
@@ -375,7 +389,7 @@
 
     observed = obs_cells.shape[2]
     cut = near_blocks(strip // BLK) * BLK
-    cross, pair, cells, values, near, far = pl.pallas_call(
+    cross, pair, cells, values, near, far, count, total = pl.pallas_call(
         prepare_kernel,
         out_shape=(
             jax.ShapeDtypeStruct((4, HALO, columns), f32),
@@ -384,14 +398,16 @@
             jax.ShapeDtypeStruct((NSTEP, observed), f32),
             jax.ShapeDtypeStruct((3, cut, columns), f32),
             jax.ShapeDtypeStruct((3, strip - cut, columns), f32),
+            jax.ShapeDtypeStruct((NSTEP, rows, columns), f32),
+            jax.ShapeDtypeStruct((NSTEP, rows, columns), f32),
         ),
         in_specs=[smem()] + [hbm()] * 4,
-        out_specs=(vmem(),) * 6,
+        out_specs=(vmem(),) * 8,
         scratch_shapes=[
             pltpu.VMEM((2, HALO, columns), jnp.int32),
             pltpu.SemaphoreType.DMA((8,)),
         ],
-        compiler_params=params(8),
+        compiler_params=params(16),
         cost_estimate=cost(0.5),
         name="prepare",
     )(pos, *(off_chip(x) for x in (states, land_mask, obs_cells, obs_values)))
@@ -414,13 +430,14 @@
             jax.ShapeDtypeStruct((3, rows, columns), f32),
             jax.ShapeDtypeStruct((strip, columns), jnp.int32),
         ),
-        in_specs=[smem(), vmem(), vmem(), hbm(), hbm()],
+        in_specs=[smem(), vmem(), vmem(), hbm(), hbm(), vmem(), vmem()],
         out_specs=(vmem(),) * 4,
+        input_output_aliases={5: 0, 6: 1},
         scratch_shapes=[pltpu.SemaphoreType.DMA((2,))],
         compiler_params=params(16),
         cost_estimate=cost(4),
         name="maps",
-    )(pos, cells, values, off_chip(states), off_chip(land_mask))
+    )(pos, cells, values, off_chip(states), off_chip(land_mask), count, total)
 
     row = lax.broadcasted_iota(jnp.int32, (3, HALO, columns), 1)
     rim = jnp.where((row < HALO // 2) != even, cross[:3], pair[:3])
@@ -497,8 +514,8 @@
         name="gradient",
     )(pos, path[0], previous, off_chip(background), first, second, outer)
     next_state = settle("near", [(BLK, cut - 2 * BLK)], near_sent)
-    next_state = settle("far", [(cut - BLK, strip - cut)], far_sent, next_state, gradient)
-    next_state = settle("edge", [(0, BLK), (strip - BLK, BLK)], edge_sent, next_state)
+    next_state = settle("far", [(cut - BLK, strip - cut)], far_sent, next_state)
+    next_state = settle("edge", [(0, BLK), (strip - BLK, BLK)], edge_sent, next_state, gradient)
     return (gradient, next_state)
 
 

time: 59.3 us -> 60.3 us (1.017)
  Pallas kernels: 20.1 us -> 21.3 us
  starting transfers between devices: 33.7 us -> 32.7 us
  waiting for transfers between devices: 4.16 us -> 4.78 us
    pallas_call x1, Pallas kernels: 1.87 us -> 4.8 us  [local(): pl.pallas_call(prepare_kernel, out_shape=(jax.ShapeDtypeStruct((4, HALO,...]
    pallas_call x1, Pallas kernels: 3.48 us -> 1.75 us  [local(): pl.pallas_call(maps_kernel, out_shape=(jax.ShapeDtypeStruct((NSTEP, rows,...]
    ppermute x7, starting transfers between devices: 30.1 us -> 29.1 us  [shifted(): return lax.ppermute(block, axis, route)]
    ppermute x7, waiting for transfers between devices: 4.15 us -> 4.78 us  [shifted(): return lax.ppermute(block, axis, route)]
  transfers between devices with their start and end apart: 9 -> 9, of which waited for: 2 -> 1; matrix products, arithmetic and copies ran while one was open for 0% -> 0% of each run, Pallas kernels for 29% -> 25%
where the time goes in v5:
time: 60.3 us; the launch traced here: 60 us
  starting transfers between devices  32.7 us (54%)
  Pallas kernels  21.3 us (35%)
  waiting for transfers between devices  4.78 us (8%)
  between operations  1 us (2%)
    ppermute x7, starting transfers between devices, shifted(): return lax.ppermute(block, axis, route)  29.1 us
    pallas_call x3, Pallas kernels, adjoint(): pl.pallas_call(adjoint_kernel(part), out_shape=(jax.ShapeDtypeStruct((3,...  5.74 us
    pallas_call x1, Pallas kernels, local(): pl.pallas_call(prepare_kernel, out_shape=(jax.ShapeDtypeStruct((4, HALO,...  4.8 us
    ppermute x7, waiting for transfers between devices, shifted(): return lax.ppermute(block, axis, route)  4.78 us
    pallas_call x3, Pallas kernels, settle(): pl.pallas_call(settle_kernel(places), out_shape=jax.ShapeDtypeStruct(stat...  3.84 us
    pallas_call x1, Pallas kernels, local(): pl.pallas_call(forward_kernel, out_shape=(jax.ShapeDtypeStruct((rows, col...  3.64 us
    ppermute x1, starting transfers between devices, local(): pair = lax.ppermute(pair, 'space', inner)  2.93 us
    pallas_call x1, Pallas kernels, local(): pl.pallas_call(maps_kernel, out_shape=(jax.ShapeDtypeStruct((NSTEP, rows,...  1.75 us
  transfers between devices with their start and end apart: 9, of which 1 were waited for; matrix products, arithmetic and copies ran while one was open for 0% of the time, Pallas kernels for 25%

profile of v5, /device:TPU:24, one launch (start us, length us, event | category | flops | bytes accessed | tf_op | source)
XLA Modules:
  0.0 60.0 jit_solution(2628216411970788822)
XLA Ops:
  0.6 0.1 stack.35.pos_ref.refs_0_
  0.7 4.8 %prepare.1 = (f32[4,8,1024]{2,1,0:T(8,128)S(1)}, f32[4,8,1024]{2,1,0:T(8,128)S(1)}, s32[4,1024]{1,0:T(4,128)S(1)}, f32[4,1024]{1,0:T(4,128)S(1)}, f32[3,40,1024]...) custom-call(s32[6]{0:T(128)S(1)} %stack.35.pos_ref.refs_0_, ...), custom_call_target="tpu_custom_call" | custom-call | flops 500000000 | bytes 1500000 | tf_op jit(solution)/shard_map/prepare/pallas_call | solution.py:392
  5.5 0.7 %collective-permute-start = (f32[4,8,1024]{2,1,0:T(8,128)S(1)}, f32[4,8,1024]{2,1,0:T(8,128)S(1)}, u32[]{:S(2)}, u32[]{:S(2)}) collective-permute-start(f32[4,8,1024]{2,1,0:T(8,128)S(1)} %get-tuple-element.49), channel_id=1, source_target_pairs={{1,2},{2,1},{5,6},{6,5},{9,10},{10,9},{13,14},{14,13},{17,18},{18,... | collective-permute-start | bytes 393224 | tf_op jit(solution)/shard_map/ppermute | solution.py:420
  6.2 2.9 %collective-permute-start.1 = (f32[4,8,1024]{2,1,0:T(8,128)S(1)}, f32[4,8,1024]{2,1,0:T(8,128)S(1)}, u32[]{:S(2)}, u32[]{:S(2)}) collective-permute-start(f32[4,8,1024]{2,1,0:T(8,128)S(1)} %get-tuple-element.50), channel_id=1, source_target_pairs={{0,1},{1,0},{2,3},{3,2},{4,5},{5,4},{6,7},{7,6},{8,9},{9,8},{10,11... | collective-permute-start | bytes 393224 | tf_op jit(solution)/shard_map/ppermute | solution.py:421
  9.1 7.2 %collective-permute-start.3 = (f32[3,40,1024]{2,1,0:T(8,128)S(1)}, f32[3,40,1024]{2,1,0:T(8,128)S(1)}, u32[]{:S(2)}, u32[]{:S(2)}) collective-permute-start(f32[3,40,1024]{2,1,0:T(8,128)S(1)} %get-tuple-element.63), channel_id=1, source_target_pairs={{4,0},{8,4},{12,8},{16,12},{20,16},{24,20},{28,24},{32,28},{36,32}... | collective-permute-start | bytes 1474568 | tf_op jit(solution)/shard_map/ppermute | solution.py:360
  16.3 2.9 %collective-permute-start.4 = (f32[3,24,1024]{2,1,0:T(8,128)S(1)}, f32[3,24,1024]{2,1,0:T(8,128)S(1)}, u32[]{:S(2)}, u32[]{:S(2)}) collective-permute-start(f32[3,24,1024]{2,1,0:T(8,128)S(1)} %get-tuple-element.65), channel_id=1, source_target_pairs={{4,0},{8,4},{12,8},{16,12},{20,16},{24,20},{28,24},{32,28},{36,32}... | collective-permute-start | bytes 884744 | tf_op jit(solution)/shard_map/ppermute | solution.py:360
  19.3 1.7 %maps.1 = (f32[4,80,1024]{2,1,0:T(8,128)S(1)}, f32[4,80,1024]{2,1,0:T(8,128)S(1)}, f32[3,80,1024]{2,1,0:T(8,128)S(1)}, s32[64,1024]{1,0:T(8,128)S(1)}) custom-call(s32[6]{0:T(128)S(1)} %stack.35.pos_ref.refs_0_, s32[4,1024]{1,0:T(4,128)S(1)} %get-tuple-element.43.cells_ref, ...), custom_call_target="tpu_custom_call", output_to_operand_aliasing={{0}: (5, {}), {1}: (6, {})} | custom-call | flops 4000000000 | bytes 12000000 | tf_op jit(solution)/shard_map/maps/pallas_call | solution.py:425
  21.0 0.0 collective-permute-done.cross_ref
  21.0 0.0 collective-permute-done.1.pair_ref
  21.0 0.1 slice_select_fusion
  21.1 4.6 %collective-permute-start.5 = (f32[3,8,1024]{2,1,0:T(8,128)S(1)}, f32[3,8,1024]{2,1,0:T(8,128)S(1)}, u32[]{:S(2)}, u32[]{:S(2)}) collective-permute-start(f32[3,8,1024]{2,1,0:T(8,128)S(1)} %slice_select_fusion), channel_id=1, source_target_pairs={{4,0},{8,4},{12,8},{16,12},{20,16},{24,20},{28,24},{32,28},{36,32}... | collective-permute-start | bytes 294920 | tf_op jit(solution)/shard_map/ppermute | solution.py:360
  25.8 3.6 %forward.1 = (f32[80,1024]{1,0:T(8,128)S(1)}, f32[3,64,1024]{2,1,0:T(8,128)S(1)}, f32[3,80,1024]{2,1,0:T(8,128)S(1)}, f32[3,80,1024]{2,1,0:T(8,128)S(1)}, f32[3,...) custom-call(s32[6]{0:T(128)S(1)} %stack.35.pos_ref.refs_0_, ...), custom_call_target="tpu_custom_call", output_to_operand_aliasing={{2}: (1, {})} | custom-call | flops 2000000000 | bytes 6000000 | tf_op jit(solution)/shard_map/forward/pallas_call | solution.py:447
  29.4 1.9 %collective-permute-start.2 = (f32[3,64,1024]{2,1,0:T(8,128)S(1)}, f32[3,64,1024]{2,1,0:T(8,128)S(1)}, u32[]{:S(2)}, u32[]{:S(2)}) collective-permute-start(f32[3,64,1024]{2,1,0:T(8,128)S(1)} %get-tuple-element.55.refs_1_), channel_id=1, source_target_pairs={{0,4},{4,8},{8,12},{12,16},{16,20},{20,24},{24,28},{28,32},{32,36}... | collective-permute-start | bytes 2359304 | tf_op jit(solution)/shard_map/ppermute | solution.py:360
  31.4 0.0 collective-permute-done.3.refs_9_
  31.4 2.1 %adjoint_near.1 = (f32[3,24,1024]{2,1,0:T(8,128)S(1)}, f32[3,24,1024]{2,1,0:T(8,128)S(1)}, f32[4,3,80,1024]{3,2,1,0:T(8,128)S(1)}) custom-call(s32[6]{0:T(128)S(1)} %stack.35.pos_ref.refs_0_, f32[80,1024]{1,0:T(8,128)S(1)} %get-tuple-element.56.refs_1_, f32[4,80,1024]{2,1,0:T(8,128)S(1)} %get-tuple-element.57.refs_2_, ...), custom_call_target="tpu_custom_call" | custom-call | flops 100000000 | bytes 300000 | tf_op jit(solution)/shard_map/adjoint_near/pallas_call | solution.py:466
  33.5 8.6 %collective-permute-start.8 = (f32[3,24,1024]{2,1,0:T(8,128)S(1)}, f32[3,24,1024]{2,1,0:T(8,128)S(1)}, u32[]{:S(2)}, u32[]{:S(2)}) collective-permute-start(f32[3,24,1024]{2,1,0:T(8,128)S(1)} %get-tuple-element.73), channel_id=1, source_target_pairs={{4,0},{8,4},{12,8},{16,12},{20,16},{24,20},{28,24},{32,28},{36,32}... | collective-permute-start | bytes 884744 | tf_op jit(solution)/shard_map/ppermute | solution.py:360
  42.1 0.0 collective-permute-done.4.refs_9_
  42.1 1.9 %adjoint_far.1 = (f32[3,24,1024]{2,1,0:T(8,128)S(1)}, f32[3,24,1024]{2,1,0:T(8,128)S(1)}, f32[4,3,80,1024]{3,2,1,0:T(8,128)S(1)}) custom-call(s32[6]{0:T(128)S(1)} %stack.35.pos_ref.refs_0_, f32[80,1024]{1,0:T(8,128)S(1)} %get-tuple-element.56.refs_1_, f32[4,80,1024]{2,1,0:T(8,128)S(1)} %get-tuple-element.57.refs_2_, ...), custom_call_target="tpu_custom_call", output_to_operand_aliasing={{2}: (10, {})} | custom-call | flops 60000002048 | bytes 180000000 | tf_op jit(solution)/shard_map/adjoint_far/pallas_call | solution.py:466
  44.0 1.9 %collective-permute-start.7 = (f32[3,24,1024]{2,1,0:T(8,128)S(1)}, f32[3,24,1024]{2,1,0:T(8,128)S(1)}, u32[]{:S(2)}, u32[]{:S(2)}) collective-permute-start(f32[3,24,1024]{2,1,0:T(8,128)S(1)} %get-tuple-element.72), channel_id=1, source_target_pairs={{4,0},{8,4},{12,8},{16,12},{20,16},{24,20},{28,24},{32,28},{36,32}... | collective-permute-start | bytes 884744 | tf_op jit(solution)/shard_map/ppermute | solution.py:360
  45.9 0.0 collective-permute-done.5.refs_9_
  45.9 1.8 %adjoint_edge.1 = (f32[3,16,1024]{2,1,0:T(8,128)S(1)}, f32[3,16,1024]{2,1,0:T(8,128)S(1)}, f32[4,3,80,1024]{3,2,1,0:T(8,128)S(1)}) custom-call(s32[6]{0:T(128)S(1)} %stack.35.pos_ref.refs_0_, f32[80,1024]{1,0:T(8,128)S(1)} %get-tuple-element.56.refs_1_, f32[4,80,1024]{2,1,0:T(8,128)S(1)} %get-tuple-element.57.refs_2_, ...), custom_call_target="tpu_custom_call", output_to_operand_aliasing={{2}: (10, {})} | custom-call | flops 500000000 | bytes 1500000 | tf_op jit(solution)/shard_map/adjoint_edge/pallas_call | solution.py:466
  47.7 1.9 %collective-permute-start.6 = (f32[3,16,1024]{2,1,0:T(8,128)S(1)}, f32[3,16,1024]{2,1,0:T(8,128)S(1)}, u32[]{:S(2)}, u32[]{:S(2)}) collective-permute-start(f32[3,16,1024]{2,1,0:T(8,128)S(1)} %get-tuple-element.71), channel_id=1, source_target_pairs={{4,0},{8,4},{12,8},{16,12},{20,16},{24,20},{28,24},{32,28},{36,32}... | collective-permute-start | bytes 589832 | tf_op jit(solution)/shard_map/ppermute | solution.py:360
  49.6 0.0 collective-permute-done.8.refs_2_
  49.6 1.3 %settle_near.1.refs_3_ = f32[1,3,64,1024]{3,2,1,0:T(8,128)} custom-call(s32[6]{0:T(128)S(1)} %stack.35.pos_ref.refs_0_, f32[3,64,1024]{2,1,0:T(8,128)S(1)} %get-tuple-element.55.refs_1_, f32[3,24,1024]{2,1,0:T(8,128)S(1)} %collective-permute-done.8.refs_2_), custom_call_target="tpu_custom_call" | custom-call | flops 10000000 | bytes 30000 | tf_op jit(solution)/shard_map/settle_near/pallas_call | solution.py:487
  50.9 4.8 %collective-permute-done.7.refs_2_ = f32[3,24,1024]{2,1,0:T(8,128)S(1)} collective-permute-done((f32[3,24,1024]{2,1,0:T(8,128)S(1)}, f32[3,24,1024]{2,1,0:T(8,128)S(1)}, u32[]{:S(2)}, u32[]{:S(2)}) %collective-permute-start.7) | collective-permute-done | bytes 294944 | tf_op jit(solution)/shard_map/ppermute | solution.py:360
  55.7 1.3 %settle_far.1.refs_3_ = f32[1,3,64,1024]{3,2,1,0:T(8,128)} custom-call(s32[6]{0:T(128)S(1)} %stack.35.pos_ref.refs_0_, f32[3,64,1024]{2,1,0:T(8,128)S(1)} %get-tuple-element.55.refs_1_, f32[3,24,1024]{2,1,0:T(8,128)S(1)} %collective-permute-done.7.refs_2_, f32[1,3,64,1024]{3,2,1,0:T(8,128)} %settle_near.1.refs_3_), custom_call_target="tpu_custom_call", output_to_operand_aliasing={{}: (3, {})} | custom-call | flops 10000000 | bytes 30000 | tf_op jit(solution)/shard_map/settle_far/pallas_call | solution.py:487
  57.0 0.0 collective-permute-done.2.previous_ref
  57.0 1.6 %gradient.1.refs_4_ = f32[1,3,64,1024]{3,2,1,0:T(8,128)} custom-call(s32[6]{0:T(128)S(1)} %stack.35.pos_ref.refs_0_, f32[3,80,1024]{2,1,0:T(8,128)S(1)} %get-tuple-element.54.refs_4_.start_ref, f32[3,64,1024]{2,1,0:T(8,128)S(1)} %collective-permute-done.2.previous_ref, f32[3,64,1024]{2,1,0:T(8,128)} %background_ref.1, ...), custom_call_target="tpu_custom_call" | custom-call | flops 10000000 | bytes 30000 | tf_op jit(solution)/shard_map/gradient/pallas_call | solution.py:502
  58.6 0.0 collective-permute-done.6.refs_2_
  58.6 1.2 %settle_edge.1 = f32[1,3,64,1024]{3,2,1,0:T(8,128)} custom-call(s32[6]{0:T(128)S(1)} %stack.35.pos_ref.refs_0_, f32[3,64,1024]{2,1,0:T(8,128)S(1)} %get-tuple-element.55.refs_1_, f32[3,16,1024]{2,1,0:T(8,128)S(1)} %collective-permute-done.6.refs_2_, f32[1,3,64,1024]{3,2,1,0:T(8,128)} %settle_far.1.refs_3_, ...), custom_call_target="tpu_custom_call", output_to_operand_aliasing={{}: (3, {})} | custom-call | flops 10000000 | bytes 30000 | tf_op jit(solution)/shard_map/settle_edge/pallas_call | solution.py:487
  (1 shorter events, 0.0 us)
Async XLA Ops:
  5.5 15.5 %collective-permute-start = (f32[4,8,1024]{2,1,0:T(8,128)S(1)}, f32[4,8,1024]{2,1,0:T(8,128)S(1)}, u32[]{:S(2)}, u32[]{:S(2)}) collective-permute-start(f32[4,8,1024]{2,1,0:T(8,128)S(1)} %get-tuple-element.49), channel_id=1, source_target_pairs={{1,2},{2,1},{5,6},{6,5},{9,10},{10,9},{13,14},{14,13},{17,18},{18,... | collective-permute-start | bytes 393224 | tf_op jit(solution)/shard_map/ppermute | solution.py:420
  6.2 14.8 %collective-permute-start.1 = (f32[4,8,1024]{2,1,0:T(8,128)S(1)}, f32[4,8,1024]{2,1,0:T(8,128)S(1)}, u32[]{:S(2)}, u32[]{:S(2)}) collective-permute-start(f32[4,8,1024]{2,1,0:T(8,128)S(1)} %get-tuple-element.50), channel_id=1, source_target_pairs={{0,1},{1,0},{2,3},{3,2},{4,5},{5,4},{6,7},{7,6},{8,9},{9,8},{10,11... | collective-permute-start | bytes 393224 | tf_op jit(solution)/shard_map/ppermute | solution.py:421
  9.1 22.2 %collective-permute-start.3 = (f32[3,40,1024]{2,1,0:T(8,128)S(1)}, f32[3,40,1024]{2,1,0:T(8,128)S(1)}, u32[]{:S(2)}, u32[]{:S(2)}) collective-permute-start(f32[3,40,1024]{2,1,0:T(8,128)S(1)} %get-tuple-element.63), channel_id=1, source_target_pairs={{4,0},{8,4},{12,8},{16,12},{20,16},{24,20},{28,24},{32,28},{36,32}... | collective-permute-start | bytes 1474568 | tf_op jit(solution)/shard_map/ppermute | solution.py:360
  16.3 25.8 %collective-permute-start.4 = (f32[3,24,1024]{2,1,0:T(8,128)S(1)}, f32[3,24,1024]{2,1,0:T(8,128)S(1)}, u32[]{:S(2)}, u32[]{:S(2)}) collective-permute-start(f32[3,24,1024]{2,1,0:T(8,128)S(1)} %get-tuple-element.65), channel_id=1, source_target_pairs={{4,0},{8,4},{12,8},{16,12},{20,16},{24,20},{28,24},{32,28},{36,32}... | collective-permute-start | bytes 884744 | tf_op jit(solution)/shard_map/ppermute | solution.py:360
  21.1 24.8 %collective-permute-start.5 = (f32[3,8,1024]{2,1,0:T(8,128)S(1)}, f32[3,8,1024]{2,1,0:T(8,128)S(1)}, u32[]{:S(2)}, u32[]{:S(2)}) collective-permute-start(f32[3,8,1024]{2,1,0:T(8,128)S(1)} %slice_select_fusion), channel_id=1, source_target_pairs={{4,0},{8,4},{12,8},{16,12},{20,16},{24,20},{28,24},{32,28},{36,32}... | collective-permute-start | bytes 294920 | tf_op jit(solution)/shard_map/ppermute | solution.py:360
  29.4 27.6 %collective-permute-start.2 = (f32[3,64,1024]{2,1,0:T(8,128)S(1)}, f32[3,64,1024]{2,1,0:T(8,128)S(1)}, u32[]{:S(2)}, u32[]{:S(2)}) collective-permute-start(f32[3,64,1024]{2,1,0:T(8,128)S(1)} %get-tuple-element.55.refs_1_), channel_id=1, source_target_pairs={{0,4},{4,8},{8,12},{12,16},{16,20},{20,24},{24,28},{28,32},{32,36}... | collective-permute-start | bytes 2359304 | tf_op jit(solution)/shard_map/ppermute | solution.py:360
  33.5 16.1 %collective-permute-start.8 = (f32[3,24,1024]{2,1,0:T(8,128)S(1)}, f32[3,24,1024]{2,1,0:T(8,128)S(1)}, u32[]{:S(2)}, u32[]{:S(2)}) collective-permute-start(f32[3,24,1024]{2,1,0:T(8,128)S(1)} %get-tuple-element.73), channel_id=1, source_target_pairs={{4,0},{8,4},{12,8},{16,12},{20,16},{24,20},{28,24},{32,28},{36,32}... | collective-permute-start | bytes 884744 | tf_op jit(solution)/shard_map/ppermute | solution.py:360
  44.0 11.7 %collective-permute-start.7 = (f32[3,24,1024]{2,1,0:T(8,128)S(1)}, f32[3,24,1024]{2,1,0:T(8,128)S(1)}, u32[]{:S(2)}, u32[]{:S(2)}) collective-permute-start(f32[3,24,1024]{2,1,0:T(8,128)S(1)} %get-tuple-element.72), channel_id=1, source_target_pairs={{4,0},{8,4},{12,8},{16,12},{20,16},{24,20},{28,24},{32,28},{36,32}... | collective-permute-start | bytes 884744 | tf_op jit(solution)/shard_map/ppermute | solution.py:360
  47.7 10.9 %collective-permute-start.6 = (f32[3,16,1024]{2,1,0:T(8,128)S(1)}, f32[3,16,1024]{2,1,0:T(8,128)S(1)}, u32[]{:S(2)}, u32[]{:S(2)}) collective-permute-start(f32[3,16,1024]{2,1,0:T(8,128)S(1)} %get-tuple-element.71), channel_id=1, source_target_pairs={{4,0},{8,4},{12,8},{16,12},{20,16},{24,20},{28,24},{32,28},{36,32}... | collective-permute-start | bytes 589832 | tf_op jit(solution)/shard_map/ppermute | solution.py:360

commit v6 on v5

--- a/solution.py
+++ b/solution.py
@@ -149,9 +149,7 @@
         fill_maps(pos_ref, seen_ref, wanted_ref, count_ref, total_ref)
 
 
-def forward_kernel(
-    pos_ref, start_ref, cross_ref, pair_ref, mask_ref, land_ref, ends_ref, *path_ref
-):
+def forward(pos_ref, cross_ref, pair_ref, mask_ref, land_ref, ends_ref, path_ref):
     strip, columns = mask_ref.shape
     rows = strip + 2 * HALO
     blocks = rows // BLK
@@ -201,6 +199,18 @@
             path_ref[step + 1][1, at] = u_new
             path_ref[step + 1][2, at] = v_new
     ends_ref[...] = path_ref[NSTEP][:, HALO : HALO + strip]
+
+
+def forward_kernel(early):
+    def kernel(*refs):
+        pos_ref, start_ref, cross_ref, pair_ref, mask_ref = refs[:5]
+        land_ref, ends_ref, *path_ref = refs[-(NSTEP + 3) :]
+
+        @pl.when(pos_ref[5] == (1 if early else 0))
+        def _():
+            forward(pos_ref, cross_ref, pair_ref, mask_ref, land_ref, ends_ref, path_ref)
+
+    return kernel
 
 
 def near_blocks(blocks):
@@ -439,25 +449,31 @@
         name="maps",
     )(pos, cells, values, off_chip(states), off_chip(land_mask), count, total)
 
+    def advanced(early, start, *held):
+        return pl.pallas_call(
+            forward_kernel(early),
+            out_shape=(
+                jax.ShapeDtypeStruct((rows, columns), f32),
+                jax.ShapeDtypeStruct((3, strip, columns), f32),
+            )
+            + (jax.ShapeDtypeStruct((3, rows, columns), f32),) * (NSTEP + 1),
+            in_specs=[smem()] + [vmem()] * (4 + len(held)),
+            out_specs=(vmem(),) * (NSTEP + 3),
+            input_output_aliases={1: 2}
+            | {5 + n: n if n < 2 else n + 1 for n in range(len(held))},
+            compiler_params=params(24),
+            cost_estimate=cost(0.01 if early else 2),
+            name="forward_early" if early else "forward_late",
+        )(pos, start, cross, pair, bits, *held)
+
     row = lax.broadcasted_iota(jnp.int32, (3, HALO, columns), 1)
     rim = jnp.where((row < HALO // 2) != even, cross[:3], pair[:3])
-    rim, cross, pair = lax.optimization_barrier((rim, cross, pair))
+    land, ends, *path = advanced(True, start)
+    rim, cross, pair, land, ends, path = lax.optimization_barrier(
+        (rim, cross, pair, land, ends, path)
+    )
     rim = shifted(rim, "tm", -1)
-
-    land, ends, *path = pl.pallas_call(
-        forward_kernel,
-        out_shape=(
-            jax.ShapeDtypeStruct((rows, columns), f32),
-            jax.ShapeDtypeStruct((3, strip, columns), f32),
-        )
-        + (jax.ShapeDtypeStruct((3, rows, columns), f32),) * (NSTEP + 1),
-        in_specs=[smem()] + [vmem()] * 4,
-        out_specs=(vmem(),) * (NSTEP + 3),
-        input_output_aliases={1: 2},
-        compiler_params=params(16),
-        cost_estimate=cost(2),
-        name="forward",
-    )(pos, start, cross, pair, bits)
+    land, ends, *path = advanced(False, path[0], land, ends, *path[1:])
 
     previous = shifted(ends, "tm", 1)
 

time: 60.3 us -> 58.5 us (0.970)
  starting transfers between devices: 32.7 us -> 31.1 us
  waiting for transfers between devices: 4.78 us -> 3.72 us
  Pallas kernels: 21.3 us -> 22.1 us
    ppermute x7, starting transfers between devices: 29.1 us -> 27.5 us  [shifted(): return lax.ppermute(block, axis, route)]
    ppermute x7, waiting for transfers between devices: 4.78 us -> 3.71 us  [shifted(): return lax.ppermute(block, axis, route)]
    pallas_call x1 -> x2, Pallas kernels: 3.64 us -> 4.38 us  [advanced(): pl.pallas_call(forward_kernel(early), out_shape=(jax.ShapeDtypeStruct((ro...]
  transfers between devices with their start and end apart: 9 -> 9, of which waited for: 1 -> 1; matrix products, arithmetic and copies ran while one was open for 0% -> 0% of each run, Pallas kernels for 25% -> 28%
where the time goes in v6:
time: 58.5 us; the launch traced here: 58 us
  starting transfers between devices  31.1 us (53%)
  Pallas kernels  22.1 us (38%)
  waiting for transfers between devices  3.72 us (6%)
  between operations  1.01 us (2%)
    ppermute x7, starting transfers between devices, shifted(): return lax.ppermute(block, axis, route)  27.5 us
    pallas_call x3, Pallas kernels, adjoint(): pl.pallas_call(adjoint_kernel(part), out_shape=(jax.ShapeDtypeStruct((3,...  5.74 us
    pallas_call x1, Pallas kernels, local(): pl.pallas_call(prepare_kernel, out_shape=(jax.ShapeDtypeStruct((4, HALO,...  4.8 us
    pallas_call x2, Pallas kernels, advanced(): pl.pallas_call(forward_kernel(early), out_shape=(jax.ShapeDtypeStruct((ro...  4.38 us
    pallas_call x3, Pallas kernels, settle(): pl.pallas_call(settle_kernel(places), out_shape=jax.ShapeDtypeStruct(stat...  3.84 us
    ppermute x7, waiting for transfers between devices, shifted(): return lax.ppermute(block, axis, route)  3.71 us
    ppermute x1, starting transfers between devices, local(): pair = lax.ppermute(pair, 'space', inner)  2.93 us
    pallas_call x1, Pallas kernels, local(): pl.pallas_call(maps_kernel, out_shape=(jax.ShapeDtypeStruct((NSTEP, rows,...  1.75 us
  transfers between devices with their start and end apart: 9, of which 1 were waited for; matrix products, arithmetic and copies ran while one was open for 0% of the time, Pallas kernels for 28%

profile of v6, /device:TPU:24, one launch (start us, length us, event | category | flops | bytes accessed | tf_op | source)
XLA Modules:
  0.0 58.0 jit_solution(16125397624842572245)
XLA Ops:
  0.6 0.1 stack.35.pos_ref.refs_0_
  0.7 4.8 %prepare.1 = (f32[4,8,1024]{2,1,0:T(8,128)S(1)}, f32[4,8,1024]{2,1,0:T(8,128)S(1)}, s32[4,1024]{1,0:T(4,128)S(1)}, f32[4,1024]{1,0:T(4,128)S(1)}, f32[3,40,1024]...) custom-call(s32[6]{0:T(128)S(1)} %stack.35.pos_ref.refs_0_, ...), custom_call_target="tpu_custom_call" | custom-call | flops 500000000 | bytes 1500000 | tf_op jit(solution)/shard_map/prepare/pallas_call | solution.py:402
  5.5 0.7 %collective-permute-start = (f32[4,8,1024]{2,1,0:T(8,128)S(1)}, f32[4,8,1024]{2,1,0:T(8,128)S(1)}, u32[]{:S(2)}, u32[]{:S(2)}) collective-permute-start(f32[4,8,1024]{2,1,0:T(8,128)S(1)} %get-tuple-element.58), channel_id=1, source_target_pairs={{1,2},{2,1},{5,6},{6,5},{9,10},{10,9},{13,14},{14,13},{17,18},{18,... | collective-permute-start | bytes 393224 | tf_op jit(solution)/shard_map/ppermute | solution.py:430
  6.2 2.9 %collective-permute-start.1 = (f32[4,8,1024]{2,1,0:T(8,128)S(1)}, f32[4,8,1024]{2,1,0:T(8,128)S(1)}, u32[]{:S(2)}, u32[]{:S(2)}) collective-permute-start(f32[4,8,1024]{2,1,0:T(8,128)S(1)} %get-tuple-element.59), channel_id=1, source_target_pairs={{0,1},{1,0},{2,3},{3,2},{4,5},{5,4},{6,7},{7,6},{8,9},{9,8},{10,11... | collective-permute-start | bytes 393224 | tf_op jit(solution)/shard_map/ppermute | solution.py:431
  9.1 7.2 %collective-permute-start.3 = (f32[3,40,1024]{2,1,0:T(8,128)S(1)}, f32[3,40,1024]{2,1,0:T(8,128)S(1)}, u32[]{:S(2)}, u32[]{:S(2)}) collective-permute-start(f32[3,40,1024]{2,1,0:T(8,128)S(1)} %get-tuple-element.91), channel_id=1, source_target_pairs={{4,0},{8,4},{12,8},{16,12},{20,16},{24,20},{28,24},{32,28},{36,32}... | collective-permute-start | bytes 1474568 | tf_op jit(solution)/shard_map/ppermute | solution.py:370
  16.3 2.9 %collective-permute-start.4 = (f32[3,24,1024]{2,1,0:T(8,128)S(1)}, f32[3,24,1024]{2,1,0:T(8,128)S(1)}, u32[]{:S(2)}, u32[]{:S(2)}) collective-permute-start(f32[3,24,1024]{2,1,0:T(8,128)S(1)} %get-tuple-element.93), channel_id=1, source_target_pairs={{4,0},{8,4},{12,8},{16,12},{20,16},{24,20},{28,24},{32,28},{36,32}... | collective-permute-start | bytes 884744 | tf_op jit(solution)/shard_map/ppermute | solution.py:370
  19.3 1.7 %maps.1 = (f32[4,80,1024]{2,1,0:T(8,128)S(1)}, f32[4,80,1024]{2,1,0:T(8,128)S(1)}, f32[3,80,1024]{2,1,0:T(8,128)S(1)}, s32[64,1024]{1,0:T(8,128)S(1)}) custom-call(s32[6]{0:T(128)S(1)} %stack.35.pos_ref.refs_0_, s32[4,1024]{1,0:T(4,128)S(1)} %get-tuple-element.60.cells_ref, ...), custom_call_target="tpu_custom_call", output_to_operand_aliasing={{0}: (5, {}), {1}: (6, {})} | custom-call | flops 4000000000 | bytes 12000000 | tf_op jit(solution)/shard_map/maps/pallas_call | solution.py:435
  21.0 0.0 collective-permute-done.refs_2_
  21.0 0.0 collective-permute-done.1.refs_3_
  21.0 0.1 slice_select_fusion
  21.1 3.6 %forward_early.1 = (f32[80,1024]{1,0:T(8,128)S(1)}, f32[3,64,1024]{2,1,0:T(8,128)S(1)}, f32[3,80,1024]{2,1,0:T(8,128)S(1)}, f32[3,80,1024]{2,1,0:T(8,128)S(1)}, ...) custom-call(s32[6]{0:T(128)S(1)} %stack.35.pos_ref.refs_0_, ...), custom_call_target="tpu_custom_call", output_to_operand_aliasing={{2}: (1, {})} | custom-call | flops 10000000 | bytes 30000 | tf_op jit(solution)/shard_map/forward_early/pallas_call | solution.py:453
  24.8 1.9 %collective-permute-start.5 = (f32[3,8,1024]{2,1,0:T(8,128)S(1)}, f32[3,8,1024]{2,1,0:T(8,128)S(1)}, u32[]{:S(2)}, u32[]{:S(2)}) collective-permute-start(f32[3,8,1024]{2,1,0:T(8,128)S(1)} %slice_select_fusion), channel_id=1, source_target_pairs={{4,0},{8,4},{12,8},{16,12},{20,16},{24,20},{28,24},{32,28},{36,32}... | collective-permute-start | bytes 294920 | tf_op jit(solution)/shard_map/ppermute | solution.py:370
  26.7 0.7 %forward_late.1 = (f32[80,1024]{1,0:T(8,128)S(1)}, f32[3,64,1024]{2,1,0:T(8,128)S(1)}, f32[3,80,1024]{2,1,0:T(8,128)S(1)}, f32[3,80,1024]{2,1,0:T(8,128)S(1)}, f...) custom-call(s32[6]{0:T(128)S(1)} %stack.35.pos_ref.refs_0_, ...), custom_call_target="tpu_custom_call", output_to_operand_aliasing={{2}: (1, {}), {0}: (5, {}), {1}: (6, {}), {3}: (7, {}), {4}... | custom-call | flops 2000000000 | bytes 6000000 | tf_op jit(solution)/shard_map/forward_late/pallas_call | solution.py:453
  27.4 3.9 %collective-permute-start.2 = (f32[3,64,1024]{2,1,0:T(8,128)S(1)}, f32[3,64,1024]{2,1,0:T(8,128)S(1)}, u32[]{:S(2)}, u32[]{:S(2)}) collective-permute-start(f32[3,64,1024]{2,1,0:T(8,128)S(1)} %get-tuple-element.83.refs_1_), channel_id=1, source_target_pairs={{0,4},{4,8},{8,12},{12,16},{16,20},{20,24},{24,28},{28,32},{32,36}... | collective-permute-start | bytes 2359304 | tf_op jit(solution)/shard_map/ppermute | solution.py:370
  31.4 0.0 collective-permute-done.3.refs_9_
  31.4 2.1 %adjoint_near.1 = (f32[3,24,1024]{2,1,0:T(8,128)S(1)}, f32[3,24,1024]{2,1,0:T(8,128)S(1)}, f32[4,3,80,1024]{3,2,1,0:T(8,128)S(1)}) custom-call(s32[6]{0:T(128)S(1)} %stack.35.pos_ref.refs_0_, f32[80,1024]{1,0:T(8,128)S(1)} %get-tuple-element.84.refs_1_, f32[4,80,1024]{2,1,0:T(8,128)S(1)} %get-tuple-element.85.refs_2_, ...), custom_call_target="tpu_custom_call" | custom-call | flops 100000000 | bytes 300000 | tf_op jit(solution)/shard_map/adjoint_near/pallas_call | solution.py:482
  33.5 6.4 %collective-permute-start.8 = (f32[3,24,1024]{2,1,0:T(8,128)S(1)}, f32[3,24,1024]{2,1,0:T(8,128)S(1)}, u32[]{:S(2)}, u32[]{:S(2)}) collective-permute-start(f32[3,24,1024]{2,1,0:T(8,128)S(1)} %get-tuple-element.101), channel_id=1, source_target_pairs={{4,0},{8,4},{12,8},{16,12},{20,16},{24,20},{28,24},{32,28},{36,32}... | collective-permute-start | bytes 884744 | tf_op jit(solution)/shard_map/ppermute | solution.py:370
  40.0 0.0 collective-permute-done.4.refs_9_
  40.0 1.9 %adjoint_far.1 = (f32[3,24,1024]{2,1,0:T(8,128)S(1)}, f32[3,24,1024]{2,1,0:T(8,128)S(1)}, f32[4,3,80,1024]{3,2,1,0:T(8,128)S(1)}) custom-call(s32[6]{0:T(128)S(1)} %stack.35.pos_ref.refs_0_, f32[80,1024]{1,0:T(8,128)S(1)} %get-tuple-element.84.refs_1_, f32[4,80,1024]{2,1,0:T(8,128)S(1)} %get-tuple-element.85.refs_2_, ...), custom_call_target="tpu_custom_call", output_to_operand_aliasing={{2}: (10, {})} | custom-call | flops 60000002048 | bytes 180000000 | tf_op jit(solution)/shard_map/adjoint_far/pallas_call | solution.py:482
  41.8 3.2 %collective-permute-start.7 = (f32[3,24,1024]{2,1,0:T(8,128)S(1)}, f32[3,24,1024]{2,1,0:T(8,128)S(1)}, u32[]{:S(2)}, u32[]{:S(2)}) collective-permute-start(f32[3,24,1024]{2,1,0:T(8,128)S(1)} %get-tuple-element.100), channel_id=1, source_target_pairs={{4,0},{8,4},{12,8},{16,12},{20,16},{24,20},{28,24},{32,28},{36,32}... | collective-permute-start | bytes 884744 | tf_op jit(solution)/shard_map/ppermute | solution.py:370
  45.0 0.0 collective-permute-done.5.refs_9_
  45.0 1.8 %adjoint_edge.1 = (f32[3,16,1024]{2,1,0:T(8,128)S(1)}, f32[3,16,1024]{2,1,0:T(8,128)S(1)}, f32[4,3,80,1024]{3,2,1,0:T(8,128)S(1)}) custom-call(s32[6]{0:T(128)S(1)} %stack.35.pos_ref.refs_0_, f32[80,1024]{1,0:T(8,128)S(1)} %get-tuple-element.84.refs_1_, f32[4,80,1024]{2,1,0:T(8,128)S(1)} %get-tuple-element.85.refs_2_, ...), custom_call_target="tpu_custom_call", output_to_operand_aliasing={{2}: (10, {})} | custom-call | flops 500000000 | bytes 1500000 | tf_op jit(solution)/shard_map/adjoint_edge/pallas_call | solution.py:482
  46.8 1.9 %collective-permute-start.6 = (f32[3,16,1024]{2,1,0:T(8,128)S(1)}, f32[3,16,1024]{2,1,0:T(8,128)S(1)}, u32[]{:S(2)}, u32[]{:S(2)}) collective-permute-start(f32[3,16,1024]{2,1,0:T(8,128)S(1)} %get-tuple-element.99), channel_id=1, source_target_pairs={{4,0},{8,4},{12,8},{16,12},{20,16},{24,20},{28,24},{32,28},{36,32}... | collective-permute-start | bytes 589832 | tf_op jit(solution)/shard_map/ppermute | solution.py:370
  48.7 0.0 collective-permute-done.8.refs_2_
  48.7 1.3 %settle_near.1.refs_3_ = f32[1,3,64,1024]{3,2,1,0:T(8,128)} custom-call(s32[6]{0:T(128)S(1)} %stack.35.pos_ref.refs_0_, f32[3,64,1024]{2,1,0:T(8,128)S(1)} %get-tuple-element.83.refs_1_, f32[3,24,1024]{2,1,0:T(8,128)S(1)} %collective-permute-done.8.refs_2_), custom_call_target="tpu_custom_call" | custom-call | flops 10000000 | bytes 30000 | tf_op jit(solution)/shard_map/settle_near/pallas_call | solution.py:503
  50.0 3.7 %collective-permute-done.7.refs_2_ = f32[3,24,1024]{2,1,0:T(8,128)S(1)} collective-permute-done((f32[3,24,1024]{2,1,0:T(8,128)S(1)}, f32[3,24,1024]{2,1,0:T(8,128)S(1)}, u32[]{:S(2)}, u32[]{:S(2)}) %collective-permute-start.7) | collective-permute-done | bytes 294944 | tf_op jit(solution)/shard_map/ppermute | solution.py:370
  53.7 1.3 %settle_far.1.refs_3_ = f32[1,3,64,1024]{3,2,1,0:T(8,128)} custom-call(s32[6]{0:T(128)S(1)} %stack.35.pos_ref.refs_0_, f32[3,64,1024]{2,1,0:T(8,128)S(1)} %get-tuple-element.83.refs_1_, f32[3,24,1024]{2,1,0:T(8,128)S(1)} %collective-permute-done.7.refs_2_, f32[1,3,64,1024]{3,2,1,0:T(8,128)} %settle_near.1.refs_3_), custom_call_target="tpu_custom_call", output_to_operand_aliasing={{}: (3, {})} | custom-call | flops 10000000 | bytes 30000 | tf_op jit(solution)/shard_map/settle_far/pallas_call | solution.py:503
  55.0 0.0 collective-permute-done.2.previous_ref
  55.0 1.6 %gradient.1.refs_4_ = f32[1,3,64,1024]{3,2,1,0:T(8,128)} custom-call(s32[6]{0:T(128)S(1)} %stack.35.pos_ref.refs_0_, f32[3,80,1024]{2,1,0:T(8,128)S(1)} %get-tuple-element.82.refs_4_.start_ref, f32[3,64,1024]{2,1,0:T(8,128)S(1)} %collective-permute-done.2.previous_ref, f32[3,64,1024]{2,1,0:T(8,128)} %background_ref.1, ...), custom_call_target="tpu_custom_call" | custom-call | flops 10000000 | bytes 30000 | tf_op jit(solution)/shard_map/gradient/pallas_call | solution.py:518
  56.6 0.0 collective-permute-done.6.refs_2_
  56.6 1.2 %settle_edge.1 = f32[1,3,64,1024]{3,2,1,0:T(8,128)} custom-call(s32[6]{0:T(128)S(1)} %stack.35.pos_ref.refs_0_, f32[3,64,1024]{2,1,0:T(8,128)S(1)} %get-tuple-element.83.refs_1_, f32[3,16,1024]{2,1,0:T(8,128)S(1)} %collective-permute-done.6.refs_2_, f32[1,3,64,1024]{3,2,1,0:T(8,128)} %settle_far.1.refs_3_, ...), custom_call_target="tpu_custom_call", output_to_operand_aliasing={{}: (3, {})} | custom-call | flops 10000000 | bytes 30000 | tf_op jit(solution)/shard_map/settle_edge/pallas_call | solution.py:503
  (1 shorter events, 0.0 us)
Async XLA Ops:
  5.5 15.5 %collective-permute-start = (f32[4,8,1024]{2,1,0:T(8,128)S(1)}, f32[4,8,1024]{2,1,0:T(8,128)S(1)}, u32[]{:S(2)}, u32[]{:S(2)}) collective-permute-start(f32[4,8,1024]{2,1,0:T(8,128)S(1)} %get-tuple-element.58), channel_id=1, source_target_pairs={{1,2},{2,1},{5,6},{6,5},{9,10},{10,9},{13,14},{14,13},{17,18},{18,... | collective-permute-start | bytes 393224 | tf_op jit(solution)/shard_map/ppermute | solution.py:430
  6.2 14.8 %collective-permute-start.1 = (f32[4,8,1024]{2,1,0:T(8,128)S(1)}, f32[4,8,1024]{2,1,0:T(8,128)S(1)}, u32[]{:S(2)}, u32[]{:S(2)}) collective-permute-start(f32[4,8,1024]{2,1,0:T(8,128)S(1)} %get-tuple-element.59), channel_id=1, source_target_pairs={{0,1},{1,0},{2,3},{3,2},{4,5},{5,4},{6,7},{7,6},{8,9},{9,8},{10,11... | collective-permute-start | bytes 393224 | tf_op jit(solution)/shard_map/ppermute | solution.py:431
  9.1 22.2 %collective-permute-start.3 = (f32[3,40,1024]{2,1,0:T(8,128)S(1)}, f32[3,40,1024]{2,1,0:T(8,128)S(1)}, u32[]{:S(2)}, u32[]{:S(2)}) collective-permute-start(f32[3,40,1024]{2,1,0:T(8,128)S(1)} %get-tuple-element.91), channel_id=1, source_target_pairs={{4,0},{8,4},{12,8},{16,12},{20,16},{24,20},{28,24},{32,28},{36,32}... | collective-permute-start | bytes 1474568 | tf_op jit(solution)/shard_map/ppermute | solution.py:370
  16.3 23.6 %collective-permute-start.4 = (f32[3,24,1024]{2,1,0:T(8,128)S(1)}, f32[3,24,1024]{2,1,0:T(8,128)S(1)}, u32[]{:S(2)}, u32[]{:S(2)}) collective-permute-start(f32[3,24,1024]{2,1,0:T(8,128)S(1)} %get-tuple-element.93), channel_id=1, source_target_pairs={{4,0},{8,4},{12,8},{16,12},{20,16},{24,20},{28,24},{32,28},{36,32}... | collective-permute-start | bytes 884744 | tf_op jit(solution)/shard_map/ppermute | solution.py:370
  24.8 20.2 %collective-permute-start.5 = (f32[3,8,1024]{2,1,0:T(8,128)S(1)}, f32[3,8,1024]{2,1,0:T(8,128)S(1)}, u32[]{:S(2)}, u32[]{:S(2)}) collective-permute-start(f32[3,8,1024]{2,1,0:T(8,128)S(1)} %slice_select_fusion), channel_id=1, source_target_pairs={{4,0},{8,4},{12,8},{16,12},{20,16},{24,20},{28,24},{32,28},{36,32}... | collective-permute-start | bytes 294920 | tf_op jit(solution)/shard_map/ppermute | solution.py:370
  27.4 27.6 %collective-permute-start.2 = (f32[3,64,1024]{2,1,0:T(8,128)S(1)}, f32[3,64,1024]{2,1,0:T(8,128)S(1)}, u32[]{:S(2)}, u32[]{:S(2)}) collective-permute-start(f32[3,64,1024]{2,1,0:T(8,128)S(1)} %get-tuple-element.83.refs_1_), channel_id=1, source_target_pairs={{0,4},{4,8},{8,12},{12,16},{16,20},{20,24},{24,28},{28,32},{32,36}... | collective-permute-start | bytes 2359304 | tf_op jit(solution)/shard_map/ppermute | solution.py:370
  33.5 15.2 %collective-permute-start.8 = (f32[3,24,1024]{2,1,0:T(8,128)S(1)}, f32[3,24,1024]{2,1,0:T(8,128)S(1)}, u32[]{:S(2)}, u32[]{:S(2)}) collective-permute-start(f32[3,24,1024]{2,1,0:T(8,128)S(1)} %get-tuple-element.101), channel_id=1, source_target_pairs={{4,0},{8,4},{12,8},{16,12},{20,16},{24,20},{28,24},{32,28},{36,32}... | collective-permute-start | bytes 884744 | tf_op jit(solution)/shard_map/ppermute | solution.py:370
  41.8 11.9 %collective-permute-start.7 = (f32[3,24,1024]{2,1,0:T(8,128)S(1)}, f32[3,24,1024]{2,1,0:T(8,128)S(1)}, u32[]{:S(2)}, u32[]{:S(2)}) collective-permute-start(f32[3,24,1024]{2,1,0:T(8,128)S(1)} %get-tuple-element.100), channel_id=1, source_target_pairs={{4,0},{8,4},{12,8},{16,12},{20,16},{24,20},{28,24},{32,28},{36,32}... | collective-permute-start | bytes 884744 | tf_op jit(solution)/shard_map/ppermute | solution.py:370
  46.8 9.8 %collective-permute-start.6 = (f32[3,16,1024]{2,1,0:T(8,128)S(1)}, f32[3,16,1024]{2,1,0:T(8,128)S(1)}, u32[]{:S(2)}, u32[]{:S(2)}) collective-permute-start(f32[3,16,1024]{2,1,0:T(8,128)S(1)} %get-tuple-element.99), channel_id=1, source_target_pairs={{4,0},{8,4},{12,8},{16,12},{20,16},{24,20},{28,24},{32,28},{36,32}... | collective-permute-start | bytes 589832 | tf_op jit(solution)/shard_map/ppermute | solution.py:370

commit v7 on v6

--- a/solution.py
+++ b/solution.py
@@ -90,31 +90,34 @@
             )
 
 
-def maps_kernel(
-    pos_ref, cells_ref, values_ref, states_ref, mask_ref, early_count_ref, early_total_ref,
-    count_ref, total_ref, start_ref, bits_ref, sems
-):
+def fetch(states_ref, mask_ref, start_ref, bits_ref, sems, first):
     strip = mask_ref.shape[0]
-    copies = (
+    return (
         pltpu.make_async_copy(
-            states_ref.at[0], start_ref.at[:, pl.ds(HALO, strip)], sems.at[0]
+            states_ref.at[0], start_ref.at[:, pl.ds(HALO, strip)], sems.at[first]
         ),
-        pltpu.make_async_copy(mask_ref, bits_ref, sems.at[1]),
+        pltpu.make_async_copy(mask_ref, bits_ref, sems.at[first + 1]),
     )
-    for copy in copies:
-        copy.start()
+
+
+def maps_kernel(*refs):
+    pos_ref, cells_ref, values_ref, states_ref, mask_ref = refs[:5]
+    count_ref, total_ref, start_ref, bits_ref, sems = refs[-5:]
 
     @pl.when(pos_ref[5] == 0)
     def _():
+        copies = fetch(states_ref, mask_ref, start_ref, bits_ref, sems, 0)
+        for copy in copies:
+            copy.start()
         fill_maps(pos_ref, cells_ref, values_ref, count_ref, total_ref)
-
-    for copy in copies:
-        copy.wait()
+        for copy in copies:
+            copy.wait()
 
 
 def prepare_kernel(
     pos_ref, states_ref, mask_ref, cells_ref, values_ref,
-    cross_ref, pair_ref, seen_ref, wanted_ref, near_ref, far_ref, count_ref, total_ref, bits, sems
+    cross_ref, pair_ref, seen_ref, wanted_ref, near_ref, far_ref,
+    count_ref, total_ref, start_ref, bits_ref, bits, sems
 ):
     strip = states_ref.shape[2]
     bottom = strip - HALO
@@ -146,7 +149,12 @@
 
     @pl.when(pos_ref[5] != 0)
     def _():
+        later = fetch(states_ref, mask_ref, start_ref, bits_ref, sems, 8)
+        for copy in later:
+            copy.start()
         fill_maps(pos_ref, seen_ref, wanted_ref, count_ref, total_ref)
+        for copy in later:
+            copy.wait()
 
 
 def forward(pos_ref, cross_ref, pair_ref, mask_ref, land_ref, ends_ref, path_ref):
@@ -384,7 +392,7 @@
             at_final.astype(jnp.int32),
             odd,
             at_first.astype(jnp.int32),
-            ((lax.axis_index("tm") & (RING - 1) < 2) & (lax.axis_index("tm") >= RING)).astype(jnp.int32),
+            ((lax.axis_index("tm") & (RING - 1) < 3) & (lax.axis_index("tm") >= RING)).astype(jnp.int32),
         ]
     ).astype(jnp.int32)
     f32 = jnp.float32
@@ -399,7 +407,13 @@
 
     observed = obs_cells.shape[2]
     cut = near_blocks(strip // BLK) * BLK
-    cross, pair, cells, values, near, far, count, total = pl.pallas_call(
+    map_shapes = (
+        jax.ShapeDtypeStruct((NSTEP, rows, columns), f32),
+        jax.ShapeDtypeStruct((NSTEP, rows, columns), f32),
+        jax.ShapeDtypeStruct((3, rows, columns), f32),
+        jax.ShapeDtypeStruct((strip, columns), jnp.int32),
+    )
+    cross, pair, cells, values, near, far, *maps = pl.pallas_call(
         prepare_kernel,
         out_shape=(
             jax.ShapeDtypeStruct((4, HALO, columns), f32),
@@ -408,14 +422,13 @@
             jax.ShapeDtypeStruct((NSTEP, observed), f32),
             jax.ShapeDtypeStruct((3, cut, columns), f32),
             jax.ShapeDtypeStruct((3, strip - cut, columns), f32),
-            jax.ShapeDtypeStruct((NSTEP, rows, columns), f32),
-            jax.ShapeDtypeStruct((NSTEP, rows, columns), f32),
-        ),
+        )
+        + map_shapes,
         in_specs=[smem()] + [hbm()] * 4,
-        out_specs=(vmem(),) * 8,
+        out_specs=(vmem(),) * 10,
         scratch_shapes=[
             pltpu.VMEM((2, HALO, columns), jnp.int32),
-            pltpu.SemaphoreType.DMA((8,)),
+            pltpu.SemaphoreType.DMA((10,)),
         ],
         compiler_params=params(16),
         cost_estimate=cost(0.5),
@@ -434,20 +447,15 @@
 
     count, total, start, bits = pl.pallas_call(
         maps_kernel,
-        out_shape=(
-            jax.ShapeDtypeStruct((NSTEP, rows, columns), f32),
-            jax.ShapeDtypeStruct((NSTEP, rows, columns), f32),
-            jax.ShapeDtypeStruct((3, rows, columns), f32),
-            jax.ShapeDtypeStruct((strip, columns), jnp.int32),
-        ),
-        in_specs=[smem(), vmem(), vmem(), hbm(), hbm(), vmem(), vmem()],
+        out_shape=map_shapes,
+        in_specs=[smem(), vmem(), vmem(), hbm(), hbm()] + [vmem()] * 4,
         out_specs=(vmem(),) * 4,
-        input_output_aliases={5: 0, 6: 1},
+        input_output_aliases={5: 0, 6: 1, 7: 2, 8: 3},
         scratch_shapes=[pltpu.SemaphoreType.DMA((2,))],
         compiler_params=params(16),
         cost_estimate=cost(4),
         name="maps",
-    )(pos, cells, values, off_chip(states), off_chip(land_mask), count, total)
+    )(pos, cells, values, off_chip(states), off_chip(land_mask), *maps)
 
     def advanced(early, start, *held):
         return pl.pallas_call(
@@ -530,8 +538,8 @@
         name="gradient",
     )(pos, path[0], previous, off_chip(background), first, second, outer)
     next_state = settle("near", [(BLK, cut - 2 * BLK)], near_sent)
-    next_state = settle("far", [(cut - BLK, strip - cut)], far_sent, next_state)
-    next_state = settle("edge", [(0, BLK), (strip - BLK, BLK)], edge_sent, next_state, gradient)
+    next_state = settle("far", [(cut - BLK, strip - cut)], far_sent, next_state, gradient)
+    next_state = settle("edge", [(0, BLK), (strip - BLK, BLK)], edge_sent, next_state)
     return (gradient, next_state)
 
 

time: 58.5 us -> 57.2 us (0.978)
  waiting for transfers between devices: 3.72 us -> 2.56 us
  Pallas kernels: 22.1 us -> 21.2 us
  starting transfers between devices: 31.1 us -> 32 us
    pallas_call x1, Pallas kernels: 1.75 us -> 0.57 us  [local(): pl.pallas_call(maps_kernel, out_shape=map_shapes, in_specs=[smem(), vmem(...]
    ppermute x7, waiting for transfers between devices: 3.71 us -> 2.55 us  [shifted(): return lax.ppermute(block, axis, route)]
    ppermute x7, starting transfers between devices: 27.5 us -> 28.4 us  [shifted(): return lax.ppermute(block, axis, route)]
  transfers between devices with their start and end apart: 9 -> 9, of which waited for: 1 -> 2; matrix products, arithmetic and copies ran while one was open for 0% -> 0% of each run, Pallas kernels for 28% -> 26%
where the time goes in v7:
time: 57.2 us; the launch traced here: 56.9 us
  starting transfers between devices  32 us (56%)
  Pallas kernels  21.2 us (37%)
  waiting for transfers between devices  2.56 us (4%)
  between operations  1 us (2%)
    ppermute x7, starting transfers between devices, shifted(): return lax.ppermute(block, axis, route)  28.4 us
    pallas_call x3, Pallas kernels, adjoint(): pl.pallas_call(adjoint_kernel(part), out_shape=(jax.ShapeDtypeStruct((3,...  5.74 us
    pallas_call x1, Pallas kernels, local(): pl.pallas_call(prepare_kernel, out_shape=(jax.ShapeDtypeStruct((4, HALO,...  5.08 us
    pallas_call x2, Pallas kernels, advanced(): pl.pallas_call(forward_kernel(early), out_shape=(jax.ShapeDtypeStruct((ro...  4.38 us
    pallas_call x3, Pallas kernels, settle(): pl.pallas_call(settle_kernel(places), out_shape=jax.ShapeDtypeStruct(stat...  3.84 us
    ppermute x1, starting transfers between devices, local(): pair = lax.ppermute(pair, 'space', inner)  2.93 us
    ppermute x7, waiting for transfers between devices, shifted(): return lax.ppermute(block, axis, route)  2.55 us
    pallas_call x1, Pallas kernels, local(): pl.pallas_call(gradient_kernel, out_shape=jax.ShapeDtypeStruct(states.sha...  1.56 us
  transfers between devices with their start and end apart: 9, of which 2 were waited for; matrix products, arithmetic and copies ran while one was open for 0% of the time, Pallas kernels for 26%

profile of v7, /device:TPU:24, one launch (start us, length us, event | category | flops | bytes accessed | tf_op | source)
XLA Modules:
  0.0 56.9 jit_solution(9389639671382086515)
XLA Ops:
  0.6 0.1 stack.35.pos_ref.refs_0_
  0.7 5.1 %prepare.1 = (f32[4,8,1024]{2,1,0:T(8,128)S(1)}, f32[4,8,1024]{2,1,0:T(8,128)S(1)}, s32[4,1024]{1,0:T(4,128)S(1)}, f32[4,1024]{1,0:T(4,128)S(1)}, f32[3,40,1024]...) custom-call(s32[6]{0:T(128)S(1)} %stack.35.pos_ref.refs_0_, ...), custom_call_target="tpu_custom_call" | custom-call | flops 500000000 | bytes 1500000 | tf_op jit(solution)/shard_map/prepare/pallas_call | solution.py:416
  5.8 0.7 %collective-permute-start = (f32[4,8,1024]{2,1,0:T(8,128)S(1)}, f32[4,8,1024]{2,1,0:T(8,128)S(1)}, u32[]{:S(2)}, u32[]{:S(2)}) collective-permute-start(f32[4,8,1024]{2,1,0:T(8,128)S(1)} %get-tuple-element.60), channel_id=1, source_target_pairs={{1,2},{2,1},{5,6},{6,5},{9,10},{10,9},{13,14},{14,13},{17,18},{18,... | collective-permute-start | bytes 393224 | tf_op jit(solution)/shard_map/ppermute | solution.py:443
  6.5 2.9 %collective-permute-start.1 = (f32[4,8,1024]{2,1,0:T(8,128)S(1)}, f32[4,8,1024]{2,1,0:T(8,128)S(1)}, u32[]{:S(2)}, u32[]{:S(2)}) collective-permute-start(f32[4,8,1024]{2,1,0:T(8,128)S(1)} %get-tuple-element.61), channel_id=1, source_target_pairs={{0,1},{1,0},{2,3},{3,2},{4,5},{5,4},{6,7},{7,6},{8,9},{9,8},{10,11... | collective-permute-start | bytes 393224 | tf_op jit(solution)/shard_map/ppermute | solution.py:444
  9.4 6.9 %collective-permute-start.3 = (f32[3,40,1024]{2,1,0:T(8,128)S(1)}, f32[3,40,1024]{2,1,0:T(8,128)S(1)}, u32[]{:S(2)}, u32[]{:S(2)}) collective-permute-start(f32[3,40,1024]{2,1,0:T(8,128)S(1)} %get-tuple-element.95), channel_id=1, source_target_pairs={{4,0},{8,4},{12,8},{16,12},{20,16},{24,20},{28,24},{32,28},{36,32}... | collective-permute-start | bytes 1474568 | tf_op jit(solution)/shard_map/ppermute | solution.py:378
  16.3 2.9 %collective-permute-start.4 = (f32[3,24,1024]{2,1,0:T(8,128)S(1)}, f32[3,24,1024]{2,1,0:T(8,128)S(1)}, u32[]{:S(2)}, u32[]{:S(2)}) collective-permute-start(f32[3,24,1024]{2,1,0:T(8,128)S(1)} %get-tuple-element.97), channel_id=1, source_target_pairs={{4,0},{8,4},{12,8},{16,12},{20,16},{24,20},{28,24},{32,28},{36,32}... | collective-permute-start | bytes 884744 | tf_op jit(solution)/shard_map/ppermute | solution.py:378
  19.3 0.6 %maps.1 = (f32[4,80,1024]{2,1,0:T(8,128)S(1)}, f32[4,80,1024]{2,1,0:T(8,128)S(1)}, f32[3,80,1024]{2,1,0:T(8,128)S(1)}, s32[64,1024]{1,0:T(8,128)S(1)}) custom-call(s32[6]{0:T(128)S(1)} %stack.35.pos_ref.refs_0_, s32[4,1024]{1,0:T(4,128)S(1)} %get-tuple-element.62.refs_1_, ...), custom_call_target="tpu_custom_call", output_to_operand_aliasing={{0}: (5, {}), {1}: (6, {}), {2}: (7, {}), {3}: (8, {})} | custom-call | flops 4000000000 | bytes 12000000 | tf_op jit(solution)/shard_map/maps/pallas_call | solution.py:448
  19.9 0.0 collective-permute-done.refs_2_
  19.9 0.0 collective-permute-done.1.refs_3_
  19.9 0.1 slice_select_fusion
  20.0 3.6 %forward_early.1 = (f32[80,1024]{1,0:T(8,128)S(1)}, f32[3,64,1024]{2,1,0:T(8,128)S(1)}, f32[3,80,1024]{2,1,0:T(8,128)S(1)}, f32[3,80,1024]{2,1,0:T(8,128)S(1)}, ...) custom-call(s32[6]{0:T(128)S(1)} %stack.35.pos_ref.refs_0_, ...), custom_call_target="tpu_custom_call", output_to_operand_aliasing={{2}: (1, {})} | custom-call | flops 10000000 | bytes 30000 | tf_op jit(solution)/shard_map/forward_early/pallas_call | solution.py:461
  23.6 2.7 %collective-permute-start.5 = (f32[3,8,1024]{2,1,0:T(8,128)S(1)}, f32[3,8,1024]{2,1,0:T(8,128)S(1)}, u32[]{:S(2)}, u32[]{:S(2)}) collective-permute-start(f32[3,8,1024]{2,1,0:T(8,128)S(1)} %slice_select_fusion), channel_id=1, source_target_pairs={{4,0},{8,4},{12,8},{16,12},{20,16},{24,20},{28,24},{32,28},{36,32}... | collective-permute-start | bytes 294920 | tf_op jit(solution)/shard_map/ppermute | solution.py:378
  26.4 0.7 %forward_late.1 = (f32[80,1024]{1,0:T(8,128)S(1)}, f32[3,64,1024]{2,1,0:T(8,128)S(1)}, f32[3,80,1024]{2,1,0:T(8,128)S(1)}, f32[3,80,1024]{2,1,0:T(8,128)S(1)}, f...) custom-call(s32[6]{0:T(128)S(1)} %stack.35.pos_ref.refs_0_, ...), custom_call_target="tpu_custom_call", output_to_operand_aliasing={{2}: (1, {}), {0}: (5, {}), {1}: (6, {}), {3}: (7, {}), {4}... | custom-call | flops 2000000000 | bytes 6000000 | tf_op jit(solution)/shard_map/forward_late/pallas_call | solution.py:461
  27.1 3.1 %collective-permute-start.2 = (f32[3,64,1024]{2,1,0:T(8,128)S(1)}, f32[3,64,1024]{2,1,0:T(8,128)S(1)}, u32[]{:S(2)}, u32[]{:S(2)}) collective-permute-start(f32[3,64,1024]{2,1,0:T(8,128)S(1)} %get-tuple-element.87.refs_1_), channel_id=1, source_target_pairs={{0,4},{4,8},{8,12},{12,16},{16,20},{20,24},{24,28},{28,32},{32,36}... | collective-permute-start | bytes 2359304 | tf_op jit(solution)/shard_map/ppermute | solution.py:378
  30.2 0.0 collective-permute-done.3.refs_9_
  30.2 2.1 %adjoint_near.1 = (f32[3,24,1024]{2,1,0:T(8,128)S(1)}, f32[3,24,1024]{2,1,0:T(8,128)S(1)}, f32[4,3,80,1024]{3,2,1,0:T(8,128)S(1)}) custom-call(s32[6]{0:T(128)S(1)} %stack.35.pos_ref.refs_0_, f32[80,1024]{1,0:T(8,128)S(1)} %get-tuple-element.88.refs_1_, f32[4,80,1024]{2,1,0:T(8,128)S(1)} %get-tuple-element.89.refs_2_, ...), custom_call_target="tpu_custom_call" | custom-call | flops 100000000 | bytes 300000 | tf_op jit(solution)/shard_map/adjoint_near/pallas_call | solution.py:490
  32.4 7.3 %collective-permute-start.8 = (f32[3,24,1024]{2,1,0:T(8,128)S(1)}, f32[3,24,1024]{2,1,0:T(8,128)S(1)}, u32[]{:S(2)}, u32[]{:S(2)}) collective-permute-start(f32[3,24,1024]{2,1,0:T(8,128)S(1)} %get-tuple-element.105), channel_id=1, source_target_pairs={{4,0},{8,4},{12,8},{16,12},{20,16},{24,20},{28,24},{32,28},{36,32}... | collective-permute-start | bytes 884744 | tf_op jit(solution)/shard_map/ppermute | solution.py:378
  39.6 0.0 collective-permute-done.4.refs_9_
  39.6 1.9 %adjoint_far.1 = (f32[3,24,1024]{2,1,0:T(8,128)S(1)}, f32[3,24,1024]{2,1,0:T(8,128)S(1)}, f32[4,3,80,1024]{3,2,1,0:T(8,128)S(1)}) custom-call(s32[6]{0:T(128)S(1)} %stack.35.pos_ref.refs_0_, f32[80,1024]{1,0:T(8,128)S(1)} %get-tuple-element.88.refs_1_, f32[4,80,1024]{2,1,0:T(8,128)S(1)} %get-tuple-element.89.refs_2_, ...), custom_call_target="tpu_custom_call", output_to_operand_aliasing={{2}: (10, {})} | custom-call | flops 60000002048 | bytes 180000000 | tf_op jit(solution)/shard_map/adjoint_far/pallas_call | solution.py:490
  41.5 3.5 %collective-permute-start.7 = (f32[3,24,1024]{2,1,0:T(8,128)S(1)}, f32[3,24,1024]{2,1,0:T(8,128)S(1)}, u32[]{:S(2)}, u32[]{:S(2)}) collective-permute-start(f32[3,24,1024]{2,1,0:T(8,128)S(1)} %get-tuple-element.104), channel_id=1, source_target_pairs={{4,0},{8,4},{12,8},{16,12},{20,16},{24,20},{28,24},{32,28},{36,32}... | collective-permute-start | bytes 884744 | tf_op jit(solution)/shard_map/ppermute | solution.py:378
  45.0 0.0 collective-permute-done.5.refs_9_
  45.0 1.8 %adjoint_edge.1 = (f32[3,16,1024]{2,1,0:T(8,128)S(1)}, f32[3,16,1024]{2,1,0:T(8,128)S(1)}, f32[4,3,80,1024]{3,2,1,0:T(8,128)S(1)}) custom-call(s32[6]{0:T(128)S(1)} %stack.35.pos_ref.refs_0_, f32[80,1024]{1,0:T(8,128)S(1)} %get-tuple-element.88.refs_1_, f32[4,80,1024]{2,1,0:T(8,128)S(1)} %get-tuple-element.89.refs_2_, ...), custom_call_target="tpu_custom_call", output_to_operand_aliasing={{2}: (10, {})} | custom-call | flops 500000000 | bytes 1500000 | tf_op jit(solution)/shard_map/adjoint_edge/pallas_call | solution.py:490
  46.8 1.9 %collective-permute-start.6 = (f32[3,16,1024]{2,1,0:T(8,128)S(1)}, f32[3,16,1024]{2,1,0:T(8,128)S(1)}, u32[]{:S(2)}, u32[]{:S(2)}) collective-permute-start(f32[3,16,1024]{2,1,0:T(8,128)S(1)} %get-tuple-element.103), channel_id=1, source_target_pairs={{4,0},{8,4},{12,8},{16,12},{20,16},{24,20},{28,24},{32,28},{36,32}... | collective-permute-start | bytes 589832 | tf_op jit(solution)/shard_map/ppermute | solution.py:378
  48.7 0.0 collective-permute-done.8.refs_2_
  48.7 1.3 %settle_near.1.refs_3_ = f32[1,3,64,1024]{3,2,1,0:T(8,128)} custom-call(s32[6]{0:T(128)S(1)} %stack.35.pos_ref.refs_0_, f32[3,64,1024]{2,1,0:T(8,128)S(1)} %get-tuple-element.87.refs_1_, f32[3,24,1024]{2,1,0:T(8,128)S(1)} %collective-permute-done.8.refs_2_), custom_call_target="tpu_custom_call" | custom-call | flops 10000000 | bytes 30000 | tf_op jit(solution)/shard_map/settle_near/pallas_call | solution.py:511
  50.0 2.1 %collective-permute-done.2.previous_ref = f32[3,64,1024]{2,1,0:T(8,128)S(1)} collective-permute-done((f32[3,64,1024]{2,1,0:T(8,128)S(1)}, f32[3,64,1024]{2,1,0:T(8,128)S(1)}, u32[]{:S(2)}, u32[]{:S(2)}) %collective-permute-start.2) | collective-permute-done | bytes 786464 | tf_op jit(solution)/shard_map/ppermute | solution.py:378
  52.1 1.6 %gradient.1.refs_4_ = f32[1,3,64,1024]{3,2,1,0:T(8,128)} custom-call(s32[6]{0:T(128)S(1)} %stack.35.pos_ref.refs_0_, f32[3,80,1024]{2,1,0:T(8,128)S(1)} %get-tuple-element.86.refs_4_.start_ref, f32[3,64,1024]{2,1,0:T(8,128)S(1)} %collective-permute-done.2.previous_ref, f32[3,64,1024]{2,1,0:T(8,128)} %background_ref.1, ...), custom_call_target="tpu_custom_call" | custom-call | flops 10000000 | bytes 30000 | tf_op jit(solution)/shard_map/gradient/pallas_call | solution.py:526
  53.7 0.0 collective-permute-done.7.refs_2_
  53.7 1.3 %settle_far.1.refs_3_ = f32[1,3,64,1024]{3,2,1,0:T(8,128)} custom-call(s32[6]{0:T(128)S(1)} %stack.35.pos_ref.refs_0_, f32[3,64,1024]{2,1,0:T(8,128)S(1)} %get-tuple-element.87.refs_1_, f32[3,24,1024]{2,1,0:T(8,128)S(1)} %collective-permute-done.7.refs_2_, f32[1,3,64,1024]{3,2,1,0:T(8,128)} %settle_near.1.refs_3_, ...), custom_call_target="tpu_custom_call", output_to_operand_aliasing={{}: (3, {})} | custom-call | flops 10000000 | bytes 30000 | tf_op jit(solution)/shard_map/settle_far/pallas_call | solution.py:511
  55.0 0.4 collective-permute-done.6.refs_2_
  55.5 1.2 %settle_edge.1 = f32[1,3,64,1024]{3,2,1,0:T(8,128)} custom-call(s32[6]{0:T(128)S(1)} %stack.35.pos_ref.refs_0_, f32[3,64,1024]{2,1,0:T(8,128)S(1)} %get-tuple-element.87.refs_1_, f32[3,16,1024]{2,1,0:T(8,128)S(1)} %collective-permute-done.6.refs_2_, f32[1,3,64,1024]{3,2,1,0:T(8,128)} %settle_far.1.refs_3_), custom_call_target="tpu_custom_call", output_to_operand_aliasing={{}: (3, {})} | custom-call | flops 10000000 | bytes 30000 | tf_op jit(solution)/shard_map/settle_edge/pallas_call | solution.py:511
  (1 shorter events, 0.0 us)
Async XLA Ops:
  5.8 14.0 %collective-permute-start = (f32[4,8,1024]{2,1,0:T(8,128)S(1)}, f32[4,8,1024]{2,1,0:T(8,128)S(1)}, u32[]{:S(2)}, u32[]{:S(2)}) collective-permute-start(f32[4,8,1024]{2,1,0:T(8,128)S(1)} %get-tuple-element.60), channel_id=1, source_target_pairs={{1,2},{2,1},{5,6},{6,5},{9,10},{10,9},{13,14},{14,13},{17,18},{18,... | collective-permute-start | bytes 393224 | tf_op jit(solution)/shard_map/ppermute | solution.py:443
  6.5 13.4 %collective-permute-start.1 = (f32[4,8,1024]{2,1,0:T(8,128)S(1)}, f32[4,8,1024]{2,1,0:T(8,128)S(1)}, u32[]{:S(2)}, u32[]{:S(2)}) collective-permute-start(f32[4,8,1024]{2,1,0:T(8,128)S(1)} %get-tuple-element.61), channel_id=1, source_target_pairs={{0,1},{1,0},{2,3},{3,2},{4,5},{5,4},{6,7},{7,6},{8,9},{9,8},{10,11... | collective-permute-start | bytes 393224 | tf_op jit(solution)/shard_map/ppermute | solution.py:444
  9.4 20.8 %collective-permute-start.3 = (f32[3,40,1024]{2,1,0:T(8,128)S(1)}, f32[3,40,1024]{2,1,0:T(8,128)S(1)}, u32[]{:S(2)}, u32[]{:S(2)}) collective-permute-start(f32[3,40,1024]{2,1,0:T(8,128)S(1)} %get-tuple-element.95), channel_id=1, source_target_pairs={{4,0},{8,4},{12,8},{16,12},{20,16},{24,20},{28,24},{32,28},{36,32}... | collective-permute-start | bytes 1474568 | tf_op jit(solution)/shard_map/ppermute | solution.py:378
  16.3 23.3 %collective-permute-start.4 = (f32[3,24,1024]{2,1,0:T(8,128)S(1)}, f32[3,24,1024]{2,1,0:T(8,128)S(1)}, u32[]{:S(2)}, u32[]{:S(2)}) collective-permute-start(f32[3,24,1024]{2,1,0:T(8,128)S(1)} %get-tuple-element.97), channel_id=1, source_target_pairs={{4,0},{8,4},{12,8},{16,12},{20,16},{24,20},{28,24},{32,28},{36,32}... | collective-permute-start | bytes 884744 | tf_op jit(solution)/shard_map/ppermute | solution.py:378
  23.6 21.4 %collective-permute-start.5 = (f32[3,8,1024]{2,1,0:T(8,128)S(1)}, f32[3,8,1024]{2,1,0:T(8,128)S(1)}, u32[]{:S(2)}, u32[]{:S(2)}) collective-permute-start(f32[3,8,1024]{2,1,0:T(8,128)S(1)} %slice_select_fusion), channel_id=1, source_target_pairs={{4,0},{8,4},{12,8},{16,12},{20,16},{24,20},{28,24},{32,28},{36,32}... | collective-permute-start | bytes 294920 | tf_op jit(solution)/shard_map/ppermute | solution.py:378
  27.1 25.0 %collective-permute-start.2 = (f32[3,64,1024]{2,1,0:T(8,128)S(1)}, f32[3,64,1024]{2,1,0:T(8,128)S(1)}, u32[]{:S(2)}, u32[]{:S(2)}) collective-permute-start(f32[3,64,1024]{2,1,0:T(8,128)S(1)} %get-tuple-element.87.refs_1_), channel_id=1, source_target_pairs={{0,4},{4,8},{8,12},{12,16},{16,20},{20,24},{24,28},{28,32},{32,36}... | collective-permute-start | bytes 2359304 | tf_op jit(solution)/shard_map/ppermute | solution.py:378
  32.4 16.4 %collective-permute-start.8 = (f32[3,24,1024]{2,1,0:T(8,128)S(1)}, f32[3,24,1024]{2,1,0:T(8,128)S(1)}, u32[]{:S(2)}, u32[]{:S(2)}) collective-permute-start(f32[3,24,1024]{2,1,0:T(8,128)S(1)} %get-tuple-element.105), channel_id=1, source_target_pairs={{4,0},{8,4},{12,8},{16,12},{20,16},{24,20},{28,24},{32,28},{36,32}... | collective-permute-start | bytes 884744 | tf_op jit(solution)/shard_map/ppermute | solution.py:378
  41.5 12.2 %collective-permute-start.7 = (f32[3,24,1024]{2,1,0:T(8,128)S(1)}, f32[3,24,1024]{2,1,0:T(8,128)S(1)}, u32[]{:S(2)}, u32[]{:S(2)}) collective-permute-start(f32[3,24,1024]{2,1,0:T(8,128)S(1)} %get-tuple-element.104), channel_id=1, source_target_pairs={{4,0},{8,4},{12,8},{16,12},{20,16},{24,20},{28,24},{32,28},{36,32}... | collective-permute-start | bytes 884744 | tf_op jit(solution)/shard_map/ppermute | solution.py:378
  46.8 8.7 %collective-permute-start.6 = (f32[3,16,1024]{2,1,0:T(8,128)S(1)}, f32[3,16,1024]{2,1,0:T(8,128)S(1)}, u32[]{:S(2)}, u32[]{:S(2)}) collective-permute-start(f32[3,16,1024]{2,1,0:T(8,128)S(1)} %get-tuple-element.103), channel_id=1, source_target_pairs={{4,0},{8,4},{12,8},{16,12},{20,16},{24,20},{28,24},{32,28},{36,32}... | collective-permute-start | bytes 589832 | tf_op jit(solution)/shard_map/ppermute | solution.py:378

commit v8 on v7

--- a/solution.py
+++ b/solution.py
@@ -100,20 +100,6 @@
     )
 
 
-def maps_kernel(*refs):
-    pos_ref, cells_ref, values_ref, states_ref, mask_ref = refs[:5]
-    count_ref, total_ref, start_ref, bits_ref, sems = refs[-5:]
-
-    @pl.when(pos_ref[5] == 0)
-    def _():
-        copies = fetch(states_ref, mask_ref, start_ref, bits_ref, sems, 0)
-        for copy in copies:
-            copy.start()
-        fill_maps(pos_ref, cells_ref, values_ref, count_ref, total_ref)
-        for copy in copies:
-            copy.wait()
-
-
 def prepare_kernel(
     pos_ref, states_ref, mask_ref, cells_ref, values_ref,
     cross_ref, pair_ref, seen_ref, wanted_ref, near_ref, far_ref,
@@ -209,16 +195,26 @@
     ends_ref[...] = path_ref[NSTEP][:, HALO : HALO + strip]
 
 
-def forward_kernel(early):
-    def kernel(*refs):
-        pos_ref, start_ref, cross_ref, pair_ref, mask_ref = refs[:5]
-        land_ref, ends_ref, *path_ref = refs[-(NSTEP + 3) :]
-
-        @pl.when(pos_ref[5] == (1 if early else 0))
-        def _():
-            forward(pos_ref, cross_ref, pair_ref, mask_ref, land_ref, ends_ref, path_ref)
-
-    return kernel
+def early_kernel(pos_ref, start_ref, cross_ref, pair_ref, bits_ref, land_ref, ends_ref, *path_ref):
+    @pl.when(pos_ref[5] != 0)
+    def _():
+        forward(pos_ref, cross_ref, pair_ref, bits_ref, land_ref, ends_ref, path_ref)
+
+
+def late_kernel(*refs):
+    pos_ref, cells_ref, values_ref, states_ref, mask_ref, cross_ref, pair_ref = refs[:7]
+    count_ref, total_ref, bits_ref, land_ref, ends_ref, *path_ref = refs[-(NSTEP + 7) : -1]
+    sems = refs[-1]
+
+    @pl.when(pos_ref[5] == 0)
+    def _():
+        copies = fetch(states_ref, mask_ref, path_ref[0], bits_ref, sems, 0)
+        for copy in copies:
+            copy.start()
+        fill_maps(pos_ref, cells_ref, values_ref, count_ref, total_ref)
+        for copy in copies:
+            copy.wait()
+        forward(pos_ref, cross_ref, pair_ref, bits_ref, land_ref, ends_ref, path_ref)
 
 
 def near_blocks(blocks):
@@ -445,43 +441,37 @@
     far = shifted(far, "tm", -1)
     near = shifted(near, "tm", -1)
 
-    count, total, start, bits = pl.pallas_call(
-        maps_kernel,
-        out_shape=map_shapes,
-        in_specs=[smem(), vmem(), vmem(), hbm(), hbm()] + [vmem()] * 4,
-        out_specs=(vmem(),) * 4,
-        input_output_aliases={5: 0, 6: 1, 7: 2, 8: 3},
-        scratch_shapes=[pltpu.SemaphoreType.DMA((2,))],
-        compiler_params=params(16),
-        cost_estimate=cost(4),
-        name="maps",
-    )(pos, cells, values, off_chip(states), off_chip(land_mask), *maps)
-
-    def advanced(early, start, *held):
-        return pl.pallas_call(
-            forward_kernel(early),
-            out_shape=(
-                jax.ShapeDtypeStruct((rows, columns), f32),
-                jax.ShapeDtypeStruct((3, strip, columns), f32),
-            )
-            + (jax.ShapeDtypeStruct((3, rows, columns), f32),) * (NSTEP + 1),
-            in_specs=[smem()] + [vmem()] * (4 + len(held)),
-            out_specs=(vmem(),) * (NSTEP + 3),
-            input_output_aliases={1: 2}
-            | {5 + n: n if n < 2 else n + 1 for n in range(len(held))},
-            compiler_params=params(24),
-            cost_estimate=cost(0.01 if early else 2),
-            name="forward_early" if early else "forward_late",
-        )(pos, start, cross, pair, bits, *held)
-
+    count, total, start, bits = maps
+    step_shapes = (
+        jax.ShapeDtypeStruct((rows, columns), f32),
+        jax.ShapeDtypeStruct((3, strip, columns), f32),
+    ) + (jax.ShapeDtypeStruct((3, rows, columns), f32),) * (NSTEP + 1)
     row = lax.broadcasted_iota(jnp.int32, (3, HALO, columns), 1)
     rim = jnp.where((row < HALO // 2) != even, cross[:3], pair[:3])
-    land, ends, *path = advanced(True, start)
-    rim, cross, pair, land, ends, path = lax.optimization_barrier(
-        (rim, cross, pair, land, ends, path)
-    )
+    steps = pl.pallas_call(
+        early_kernel,
+        out_shape=step_shapes,
+        in_specs=[smem()] + [vmem()] * 4,
+        out_specs=(vmem(),) * len(step_shapes),
+        input_output_aliases={1: 2},
+        compiler_params=params(24),
+        cost_estimate=cost(0.01),
+        name="early",
+    )(pos, start, cross, pair, bits)
+    rim, cross, pair, steps = lax.optimization_barrier((rim, cross, pair, steps))
     rim = shifted(rim, "tm", -1)
-    land, ends, *path = advanced(False, path[0], land, ends, *path[1:])
+    held = (count, total, bits, *steps)
+    count, total, bits, land, ends, *path = pl.pallas_call(
+        late_kernel,
+        out_shape=(map_shapes[0], map_shapes[1], map_shapes[3]) + step_shapes,
+        in_specs=[smem(), vmem(), vmem(), hbm(), hbm(), vmem(), vmem()] + [vmem()] * len(held),
+        out_specs=(vmem(),) * len(held),
+        input_output_aliases={7 + n: n for n in range(len(held))},
+        scratch_shapes=[pltpu.SemaphoreType.DMA((2,))],
+        compiler_params=params(28),
+        cost_estimate=cost(6),
+        name="late",
+    )(pos, cells, values, off_chip(states), off_chip(land_mask), cross, pair, *held)
 
     previous = shifted(ends, "tm", 1)
 

time: 57.2 us -> 56.1 us (0.981)
  waiting for transfers between devices: 2.56 us -> 1.46 us
  Pallas kernels: 21.2 us -> 20.6 us
    ppermute x7, waiting for transfers between devices: 2.55 us -> 1.46 us  [shifted(): return lax.ppermute(block, axis, route)]
    pallas_call x3 -> x2, Pallas kernels: 4.95 us -> 4.4 us  [the longest x1 3.64 us: local(): pl.pallas_call(early_kernel, out_shape=step_shapes, in_specs=[smem()] + [...]
where the time goes in v8:
time: 56.1 us; the launch traced here: 55.8 us
  starting transfers between devices  32.5 us (58%)
  Pallas kernels  20.6 us (37%)
  waiting for transfers between devices  1.46 us (3%)
  between operations  0.99 us (2%)
    ppermute x7, starting transfers between devices, shifted(): return lax.ppermute(block, axis, route)  28.9 us
    pallas_call x3, Pallas kernels, adjoint(): pl.pallas_call(adjoint_kernel(part), out_shape=(jax.ShapeDtypeStruct((3,...  5.74 us
    pallas_call x1, Pallas kernels, local(): pl.pallas_call(prepare_kernel, out_shape=(jax.ShapeDtypeStruct((4, HALO,...  5.08 us
    pallas_call x3, Pallas kernels, settle(): pl.pallas_call(settle_kernel(places), out_shape=jax.ShapeDtypeStruct(stat...  3.84 us
    pallas_call x1, Pallas kernels, local(): pl.pallas_call(early_kernel, out_shape=step_shapes, in_specs=[smem()] + [...  3.64 us
    ppermute x1, starting transfers between devices, local(): pair = lax.ppermute(pair, 'space', inner)  2.93 us
    pallas_call x1, Pallas kernels, local(): pl.pallas_call(gradient_kernel, out_shape=jax.ShapeDtypeStruct(states.sha...  1.56 us
    ppermute x7, waiting for transfers between devices, shifted(): return lax.ppermute(block, axis, route)  1.46 us
  transfers between devices with their start and end apart: 9, of which 2 were waited for; matrix products, arithmetic and copies ran while one was open for 0% of the time, Pallas kernels for 26%

profile of v8, /device:TPU:24, one launch (start us, length us, event | category | flops | bytes accessed | tf_op | source)
XLA Modules:
  0.0 55.8 jit_solution(1632471512035207426)
XLA Ops:
  0.6 0.1 stack.35.pos_ref.refs_0_
  0.7 5.1 %prepare.1 = (f32[4,8,1024]{2,1,0:T(8,128)S(1)}, f32[4,8,1024]{2,1,0:T(8,128)S(1)}, s32[4,1024]{1,0:T(4,128)S(1)}, f32[4,1024]{1,0:T(4,128)S(1)}, f32[3,40,1024]...) custom-call(s32[6]{0:T(128)S(1)} %stack.35.pos_ref.refs_0_, ...), custom_call_target="tpu_custom_call" | custom-call | flops 500000000 | bytes 1500000 | tf_op jit(solution)/shard_map/prepare/pallas_call | solution.py:412
  5.8 0.7 %collective-permute-start = (f32[4,8,1024]{2,1,0:T(8,128)S(1)}, f32[4,8,1024]{2,1,0:T(8,128)S(1)}, u32[]{:S(2)}, u32[]{:S(2)}) collective-permute-start(f32[4,8,1024]{2,1,0:T(8,128)S(1)} %get-tuple-element.60), channel_id=1, source_target_pairs={{1,2},{2,1},{5,6},{6,5},{9,10},{10,9},{13,14},{14,13},{17,18},{18,... | collective-permute-start | bytes 393224 | tf_op jit(solution)/shard_map/ppermute | solution.py:439
  6.5 2.9 %collective-permute-start.1 = (f32[4,8,1024]{2,1,0:T(8,128)S(1)}, f32[4,8,1024]{2,1,0:T(8,128)S(1)}, u32[]{:S(2)}, u32[]{:S(2)}) collective-permute-start(f32[4,8,1024]{2,1,0:T(8,128)S(1)} %get-tuple-element.61), channel_id=1, source_target_pairs={{0,1},{1,0},{2,3},{3,2},{4,5},{5,4},{6,7},{7,6},{8,9},{9,8},{10,11... | collective-permute-start | bytes 393224 | tf_op jit(solution)/shard_map/ppermute | solution.py:440
  9.4 6.9 %collective-permute-start.3 = (f32[3,40,1024]{2,1,0:T(8,128)S(1)}, f32[3,40,1024]{2,1,0:T(8,128)S(1)}, u32[]{:S(2)}, u32[]{:S(2)}) collective-permute-start(f32[3,40,1024]{2,1,0:T(8,128)S(1)} %get-tuple-element.91), channel_id=1, source_target_pairs={{4,0},{8,4},{12,8},{16,12},{20,16},{24,20},{28,24},{32,28},{36,32}... | collective-permute-start | bytes 1474568 | tf_op jit(solution)/shard_map/ppermute | solution.py:374
  16.3 2.9 %collective-permute-start.4 = (f32[3,24,1024]{2,1,0:T(8,128)S(1)}, f32[3,24,1024]{2,1,0:T(8,128)S(1)}, u32[]{:S(2)}, u32[]{:S(2)}) collective-permute-start(f32[3,24,1024]{2,1,0:T(8,128)S(1)} %get-tuple-element.93), channel_id=1, source_target_pairs={{4,0},{8,4},{12,8},{16,12},{20,16},{24,20},{28,24},{32,28},{36,32}... | collective-permute-start | bytes 884744 | tf_op jit(solution)/shard_map/ppermute | solution.py:374
  19.3 0.0 collective-permute-done.cross_ref.refs_5_
  19.3 0.0 collective-permute-done.1.pair_ref.refs_6_
  19.3 0.1 slice_select_fusion
  19.4 3.6 %early.1 = (f32[80,1024]{1,0:T(8,128)S(1)}, f32[3,64,1024]{2,1,0:T(8,128)S(1)}, f32[3,80,1024]{2,1,0:T(8,128)S(1)}, f32[3,80,1024]{2,1,0:T(8,128)S(1)}, f32[3,80...) custom-call(s32[6]{0:T(128)S(1)} %stack.35.pos_ref.refs_0_, ...), custom_call_target="tpu_custom_call", output_to_operand_aliasing={{2}: (1, {})} | custom-call | flops 10000000 | bytes 30000 | tf_op jit(solution)/shard_map/early/pallas_call | solution.py:451
  23.0 1.9 %collective-permute-start.5 = (f32[3,8,1024]{2,1,0:T(8,128)S(1)}, f32[3,8,1024]{2,1,0:T(8,128)S(1)}, u32[]{:S(2)}, u32[]{:S(2)}) collective-permute-start(f32[3,8,1024]{2,1,0:T(8,128)S(1)} %slice_select_fusion), channel_id=1, source_target_pairs={{4,0},{8,4},{12,8},{16,12},{20,16},{24,20},{28,24},{32,28},{36,32}... | collective-permute-start | bytes 294920 | tf_op jit(solution)/shard_map/ppermute | solution.py:374
  25.0 0.8 %late.1 = (f32[4,80,1024]{2,1,0:T(8,128)S(1)}, f32[4,80,1024]{2,1,0:T(8,128)S(1)}, s32[64,1024]{1,0:T(8,128)S(1)}, f32[80,1024]{1,0:T(8,128)S(1)}, f32[3,64,1024...) custom-call(s32[6]{0:T(128)S(1)} %stack.35.pos_ref.refs_0_, ...), custom_call_target="tpu_custom_call", output_to_operand_aliasing={{0}: (7, {}), {1}: (8, {}), {2}: (9, {}), {3}: (10, {}), {4... | custom-call | flops 6000000000 | bytes 18000000 | tf_op jit(solution)/shard_map/late/pallas_call | solution.py:464
  25.7 3.9 %collective-permute-start.2 = (f32[3,64,1024]{2,1,0:T(8,128)S(1)}, f32[3,64,1024]{2,1,0:T(8,128)S(1)}, u32[]{:S(2)}, u32[]{:S(2)}) collective-permute-start(f32[3,64,1024]{2,1,0:T(8,128)S(1)} %get-tuple-element.83.refs_1_), channel_id=1, source_target_pairs={{0,4},{4,8},{8,12},{12,16},{16,20},{20,24},{24,28},{28,32},{32,36}... | collective-permute-start | bytes 2359304 | tf_op jit(solution)/shard_map/ppermute | solution.py:374
  29.7 0.0 collective-permute-done.3.refs_9_
  29.7 2.1 %adjoint_near.1 = (f32[3,24,1024]{2,1,0:T(8,128)S(1)}, f32[3,24,1024]{2,1,0:T(8,128)S(1)}, f32[4,3,80,1024]{3,2,1,0:T(8,128)S(1)}) custom-call(s32[6]{0:T(128)S(1)} %stack.35.pos_ref.refs_0_, f32[80,1024]{1,0:T(8,128)S(1)} %get-tuple-element.84.refs_1_, f32[4,80,1024]{2,1,0:T(8,128)S(1)} %get-tuple-element.85.refs_2_, ...), custom_call_target="tpu_custom_call" | custom-call | flops 100000000 | bytes 300000 | tf_op jit(solution)/shard_map/adjoint_near/pallas_call | solution.py:480
  31.8 7.2 %collective-permute-start.8 = (f32[3,24,1024]{2,1,0:T(8,128)S(1)}, f32[3,24,1024]{2,1,0:T(8,128)S(1)}, u32[]{:S(2)}, u32[]{:S(2)}) collective-permute-start(f32[3,24,1024]{2,1,0:T(8,128)S(1)} %get-tuple-element.101), channel_id=1, source_target_pairs={{4,0},{8,4},{12,8},{16,12},{20,16},{24,20},{28,24},{32,28},{36,32}... | collective-permute-start | bytes 884744 | tf_op jit(solution)/shard_map/ppermute | solution.py:374
  39.0 0.0 collective-permute-done.4.refs_9_
  39.0 1.9 %adjoint_far.1 = (f32[3,24,1024]{2,1,0:T(8,128)S(1)}, f32[3,24,1024]{2,1,0:T(8,128)S(1)}, f32[4,3,80,1024]{3,2,1,0:T(8,128)S(1)}) custom-call(s32[6]{0:T(128)S(1)} %stack.35.pos_ref.refs_0_, f32[80,1024]{1,0:T(8,128)S(1)} %get-tuple-element.84.refs_1_, f32[4,80,1024]{2,1,0:T(8,128)S(1)} %get-tuple-element.85.refs_2_, ...), custom_call_target="tpu_custom_call", output_to_operand_aliasing={{2}: (10, {})} | custom-call | flops 60000002048 | bytes 180000000 | tf_op jit(solution)/shard_map/adjoint_far/pallas_call | solution.py:480
  40.8 4.2 %collective-permute-start.7 = (f32[3,24,1024]{2,1,0:T(8,128)S(1)}, f32[3,24,1024]{2,1,0:T(8,128)S(1)}, u32[]{:S(2)}, u32[]{:S(2)}) collective-permute-start(f32[3,24,1024]{2,1,0:T(8,128)S(1)} %get-tuple-element.100), channel_id=1, source_target_pairs={{4,0},{8,4},{12,8},{16,12},{20,16},{24,20},{28,24},{32,28},{36,32}... | collective-permute-start | bytes 884744 | tf_op jit(solution)/shard_map/ppermute | solution.py:374
  45.0 0.0 collective-permute-done.5.refs_9_
  45.0 1.8 %adjoint_edge.1 = (f32[3,16,1024]{2,1,0:T(8,128)S(1)}, f32[3,16,1024]{2,1,0:T(8,128)S(1)}, f32[4,3,80,1024]{3,2,1,0:T(8,128)S(1)}) custom-call(s32[6]{0:T(128)S(1)} %stack.35.pos_ref.refs_0_, f32[80,1024]{1,0:T(8,128)S(1)} %get-tuple-element.84.refs_1_, f32[4,80,1024]{2,1,0:T(8,128)S(1)} %get-tuple-element.85.refs_2_, ...), custom_call_target="tpu_custom_call", output_to_operand_aliasing={{2}: (10, {})} | custom-call | flops 500000000 | bytes 1500000 | tf_op jit(solution)/shard_map/adjoint_edge/pallas_call | solution.py:480
  46.8 1.9 %collective-permute-start.6 = (f32[3,16,1024]{2,1,0:T(8,128)S(1)}, f32[3,16,1024]{2,1,0:T(8,128)S(1)}, u32[]{:S(2)}, u32[]{:S(2)}) collective-permute-start(f32[3,16,1024]{2,1,0:T(8,128)S(1)} %get-tuple-element.99), channel_id=1, source_target_pairs={{4,0},{8,4},{12,8},{16,12},{20,16},{24,20},{28,24},{32,28},{36,32}... | collective-permute-start | bytes 589832 | tf_op jit(solution)/shard_map/ppermute | solution.py:374
  48.7 0.0 collective-permute-done.8.refs_2_
  48.7 1.3 %settle_near.1.refs_3_ = f32[1,3,64,1024]{3,2,1,0:T(8,128)} custom-call(s32[6]{0:T(128)S(1)} %stack.35.pos_ref.refs_0_, f32[3,64,1024]{2,1,0:T(8,128)S(1)} %get-tuple-element.83.refs_1_, f32[3,24,1024]{2,1,0:T(8,128)S(1)} %collective-permute-done.8.refs_2_), custom_call_target="tpu_custom_call" | custom-call | flops 10000000 | bytes 30000 | tf_op jit(solution)/shard_map/settle_near/pallas_call | solution.py:501
  50.0 1.0 %collective-permute-done.2.previous_ref = f32[3,64,1024]{2,1,0:T(8,128)S(1)} collective-permute-done((f32[3,64,1024]{2,1,0:T(8,128)S(1)}, f32[3,64,1024]{2,1,0:T(8,128)S(1)}, u32[]{:S(2)}, u32[]{:S(2)}) %collective-permute-start.2) | collective-permute-done | bytes 786464 | tf_op jit(solution)/shard_map/ppermute | solution.py:374
  51.1 1.6 %gradient.1.refs_4_ = f32[1,3,64,1024]{3,2,1,0:T(8,128)} custom-call(s32[6]{0:T(128)S(1)} %stack.35.pos_ref.refs_0_, f32[3,80,1024]{2,1,0:T(8,128)S(1)} %get-tuple-element.82.refs_4_.start_ref, f32[3,64,1024]{2,1,0:T(8,128)S(1)} %collective-permute-done.2.previous_ref, f32[3,64,1024]{2,1,0:T(8,128)} %background_ref.1, ...), custom_call_target="tpu_custom_call" | custom-call | flops 10000000 | bytes 30000 | tf_op jit(solution)/shard_map/gradient/pallas_call | solution.py:516
  52.6 0.0 collective-permute-done.7.refs_2_
  52.6 1.3 %settle_far.1.refs_3_ = f32[1,3,64,1024]{3,2,1,0:T(8,128)} custom-call(s32[6]{0:T(128)S(1)} %stack.35.pos_ref.refs_0_, f32[3,64,1024]{2,1,0:T(8,128)S(1)} %get-tuple-element.83.refs_1_, f32[3,24,1024]{2,1,0:T(8,128)S(1)} %collective-permute-done.7.refs_2_, f32[1,3,64,1024]{3,2,1,0:T(8,128)} %settle_near.1.refs_3_, ...), custom_call_target="tpu_custom_call", output_to_operand_aliasing={{}: (3, {})} | custom-call | flops 10000000 | bytes 30000 | tf_op jit(solution)/shard_map/settle_far/pallas_call | solution.py:501
  53.9 0.4 collective-permute-done.6.refs_2_
  54.4 1.2 %settle_edge.1 = f32[1,3,64,1024]{3,2,1,0:T(8,128)} custom-call(s32[6]{0:T(128)S(1)} %stack.35.pos_ref.refs_0_, f32[3,64,1024]{2,1,0:T(8,128)S(1)} %get-tuple-element.83.refs_1_, f32[3,16,1024]{2,1,0:T(8,128)S(1)} %collective-permute-done.6.refs_2_, f32[1,3,64,1024]{3,2,1,0:T(8,128)} %settle_far.1.refs_3_), custom_call_target="tpu_custom_call", output_to_operand_aliasing={{}: (3, {})} | custom-call | flops 10000000 | bytes 30000 | tf_op jit(solution)/shard_map/settle_edge/pallas_call | solution.py:501
  (1 shorter events, 0.0 us)
Async XLA Ops:
  5.8 13.5 %collective-permute-start = (f32[4,8,1024]{2,1,0:T(8,128)S(1)}, f32[4,8,1024]{2,1,0:T(8,128)S(1)}, u32[]{:S(2)}, u32[]{:S(2)}) collective-permute-start(f32[4,8,1024]{2,1,0:T(8,128)S(1)} %get-tuple-element.60), channel_id=1, source_target_pairs={{1,2},{2,1},{5,6},{6,5},{9,10},{10,9},{13,14},{14,13},{17,18},{18,... | collective-permute-start | bytes 393224 | tf_op jit(solution)/shard_map/ppermute | solution.py:439
  6.5 12.8 %collective-permute-start.1 = (f32[4,8,1024]{2,1,0:T(8,128)S(1)}, f32[4,8,1024]{2,1,0:T(8,128)S(1)}, u32[]{:S(2)}, u32[]{:S(2)}) collective-permute-start(f32[4,8,1024]{2,1,0:T(8,128)S(1)} %get-tuple-element.61), channel_id=1, source_target_pairs={{0,1},{1,0},{2,3},{3,2},{4,5},{5,4},{6,7},{7,6},{8,9},{9,8},{10,11... | collective-permute-start | bytes 393224 | tf_op jit(solution)/shard_map/ppermute | solution.py:440
  9.4 20.2 %collective-permute-start.3 = (f32[3,40,1024]{2,1,0:T(8,128)S(1)}, f32[3,40,1024]{2,1,0:T(8,128)S(1)}, u32[]{:S(2)}, u32[]{:S(2)}) collective-permute-start(f32[3,40,1024]{2,1,0:T(8,128)S(1)} %get-tuple-element.91), channel_id=1, source_target_pairs={{4,0},{8,4},{12,8},{16,12},{20,16},{24,20},{28,24},{32,28},{36,32}... | collective-permute-start | bytes 1474568 | tf_op jit(solution)/shard_map/ppermute | solution.py:374
  16.3 22.6 %collective-permute-start.4 = (f32[3,24,1024]{2,1,0:T(8,128)S(1)}, f32[3,24,1024]{2,1,0:T(8,128)S(1)}, u32[]{:S(2)}, u32[]{:S(2)}) collective-permute-start(f32[3,24,1024]{2,1,0:T(8,128)S(1)} %get-tuple-element.93), channel_id=1, source_target_pairs={{4,0},{8,4},{12,8},{16,12},{20,16},{24,20},{28,24},{32,28},{36,32}... | collective-permute-start | bytes 884744 | tf_op jit(solution)/shard_map/ppermute | solution.py:374
  23.0 22.0 %collective-permute-start.5 = (f32[3,8,1024]{2,1,0:T(8,128)S(1)}, f32[3,8,1024]{2,1,0:T(8,128)S(1)}, u32[]{:S(2)}, u32[]{:S(2)}) collective-permute-start(f32[3,8,1024]{2,1,0:T(8,128)S(1)} %slice_select_fusion), channel_id=1, source_target_pairs={{4,0},{8,4},{12,8},{16,12},{20,16},{24,20},{28,24},{32,28},{36,32}... | collective-permute-start | bytes 294920 | tf_op jit(solution)/shard_map/ppermute | solution.py:374
  25.7 25.3 %collective-permute-start.2 = (f32[3,64,1024]{2,1,0:T(8,128)S(1)}, f32[3,64,1024]{2,1,0:T(8,128)S(1)}, u32[]{:S(2)}, u32[]{:S(2)}) collective-permute-start(f32[3,64,1024]{2,1,0:T(8,128)S(1)} %get-tuple-element.83.refs_1_), channel_id=1, source_target_pairs={{0,4},{4,8},{8,12},{12,16},{16,20},{20,24},{24,28},{28,32},{32,36}... | collective-permute-start | bytes 2359304 | tf_op jit(solution)/shard_map/ppermute | solution.py:374
  31.8 16.9 %collective-permute-start.8 = (f32[3,24,1024]{2,1,0:T(8,128)S(1)}, f32[3,24,1024]{2,1,0:T(8,128)S(1)}, u32[]{:S(2)}, u32[]{:S(2)}) collective-permute-start(f32[3,24,1024]{2,1,0:T(8,128)S(1)} %get-tuple-element.101), channel_id=1, source_target_pairs={{4,0},{8,4},{12,8},{16,12},{20,16},{24,20},{28,24},{32,28},{36,32}... | collective-permute-start | bytes 884744 | tf_op jit(solution)/shard_map/ppermute | solution.py:374
  40.8 11.8 %collective-permute-start.7 = (f32[3,24,1024]{2,1,0:T(8,128)S(1)}, f32[3,24,1024]{2,1,0:T(8,128)S(1)}, u32[]{:S(2)}, u32[]{:S(2)}) collective-permute-start(f32[3,24,1024]{2,1,0:T(8,128)S(1)} %get-tuple-element.100), channel_id=1, source_target_pairs={{4,0},{8,4},{12,8},{16,12},{20,16},{24,20},{28,24},{32,28},{36,32}... | collective-permute-start | bytes 884744 | tf_op jit(solution)/shard_map/ppermute | solution.py:374
  46.8 7.6 %collective-permute-start.6 = (f32[3,16,1024]{2,1,0:T(8,128)S(1)}, f32[3,16,1024]{2,1,0:T(8,128)S(1)}, u32[]{:S(2)}, u32[]{:S(2)}) collective-permute-start(f32[3,16,1024]{2,1,0:T(8,128)S(1)} %get-tuple-element.99), channel_id=1, source_target_pairs={{4,0},{8,4},{12,8},{16,12},{20,16},{24,20},{28,24},{32,28},{36,32}... | collective-permute-start | bytes 589832 | tf_op jit(solution)/shard_map/ppermute | solution.py:374

commit v9 on v8

--- a/solution.py
+++ b/solution.py
@@ -50,6 +50,11 @@
 def above(x, before):
     last = lax.broadcasted_iota(jnp.int32, x.shape, 0) == BLK - 1
     return pltpu.roll(jnp.where(last, before, x), 1, axis=0)
+
+
+def within(base, grid_rows, block, columns):
+    number = base + block * BLK + lax.broadcasted_iota(jnp.int32, (BLK, columns), 0)
+    return (number >= 0) & (number < grid_rows)
 
 
 def fill_maps(pos_ref, cells_ref, values_ref, count_ref, total_ref):
@@ -186,9 +191,8 @@
                 + diffuse * (vn + vs + east(v) + west(v))
                 - half * (hn - hs)
             )
-            number = base + i * BLK + lax.broadcasted_iota(jnp.int32, (BLK, columns), 0)
-            inside = (number >= 0) & (number < grid_rows)
-            h_new = jnp.where(inside, h_new, 0.0)
+            if i in (0, blocks - 1):
+                h_new = jnp.where(within(base, grid_rows, i, columns), h_new, 0.0)
             path_ref[step + 1][0, at] = h_new
             path_ref[step + 1][1, at] = u_new
             path_ref[step + 1][2, at] = v_new
@@ -250,11 +254,12 @@
 
         def put(step, i, lam):
             at = slice(i * BLK, (i + 1) * BLK)
-            number = base + i * BLK + lax.broadcasted_iota(jnp.int32, (BLK, columns), 0)
-            inside = (number >= 0) & (number < grid_rows)
             force = count_ref[step, at] * path_ref[step + 1][0, at] - total_ref[step, at]
             land = land_ref[at]
-            work[step, 0, at] = jnp.where(inside, lam[0] + force, 0.0)
+            height = lam[0] + force
+            if i in (0, blocks - 1):
+                height = jnp.where(within(base, grid_rows, i, columns), height, 0.0)
+            work[step, 0, at] = height
             work[step, 1, at] = land * lam[1]
             work[step, 2, at] = land * lam[2]
 

time: 56.1 us -> 56.1 us (level)
  no operation moved by 1% of the time
where the time goes in v9:
time: 56.1 us; the launch traced here: 55.7 us
  starting transfers between devices  32.6 us (58%)
  Pallas kernels  20.5 us (37%)
  waiting for transfers between devices  1.46 us (3%)
  between operations  1 us (2%)
    ppermute x7, starting transfers between devices, shifted(): return lax.ppermute(block, axis, route)  29 us
    pallas_call x3, Pallas kernels, adjoint(): pl.pallas_call(adjoint_kernel(part), out_shape=(jax.ShapeDtypeStruct((3,...  5.68 us
    pallas_call x1, Pallas kernels, local(): pl.pallas_call(prepare_kernel, out_shape=(jax.ShapeDtypeStruct((4, HALO,...  5.08 us
    pallas_call x3, Pallas kernels, settle(): pl.pallas_call(settle_kernel(places), out_shape=jax.ShapeDtypeStruct(stat...  3.84 us
    pallas_call x1, Pallas kernels, local(): pl.pallas_call(early_kernel, out_shape=step_shapes, in_specs=[smem()] + [...  3.61 us
    ppermute x1, starting transfers between devices, local(): pair = lax.ppermute(pair, 'space', inner)  2.93 us
    pallas_call x1, Pallas kernels, local(): pl.pallas_call(gradient_kernel, out_shape=jax.ShapeDtypeStruct(states.sha...  1.56 us
    ppermute x7, waiting for transfers between devices, shifted(): return lax.ppermute(block, axis, route)  1.45 us
  transfers between devices with their start and end apart: 9, of which 2 were waited for; matrix products, arithmetic and copies ran while one was open for 0% of the time, Pallas kernels for 26%

profile of v9, /device:TPU:24, one launch (start us, length us, event | category | flops | bytes accessed | tf_op | source)
XLA Modules:
  0.0 55.7 jit_solution(8474175043785708184)
XLA Ops:
  0.6 0.1 stack.35.pos_ref.refs_0_
  0.7 5.1 %prepare.1 = (f32[4,8,1024]{2,1,0:T(8,128)S(1)}, f32[4,8,1024]{2,1,0:T(8,128)S(1)}, s32[4,1024]{1,0:T(4,128)S(1)}, f32[4,1024]{1,0:T(4,128)S(1)}, f32[3,40,1024]...) custom-call(s32[6]{0:T(128)S(1)} %stack.35.pos_ref.refs_0_, ...), custom_call_target="tpu_custom_call" | custom-call | flops 500000000 | bytes 1500000 | tf_op jit(solution)/shard_map/prepare/pallas_call | solution.py:417
  5.8 0.7 %collective-permute-start = (f32[4,8,1024]{2,1,0:T(8,128)S(1)}, f32[4,8,1024]{2,1,0:T(8,128)S(1)}, u32[]{:S(2)}, u32[]{:S(2)}) collective-permute-start(f32[4,8,1024]{2,1,0:T(8,128)S(1)} %get-tuple-element.60), channel_id=1, source_target_pairs={{1,2},{2,1},{5,6},{6,5},{9,10},{10,9},{13,14},{14,13},{17,18},{18,... | collective-permute-start | bytes 393224 | tf_op jit(solution)/shard_map/ppermute | solution.py:444
  6.5 2.9 %collective-permute-start.1 = (f32[4,8,1024]{2,1,0:T(8,128)S(1)}, f32[4,8,1024]{2,1,0:T(8,128)S(1)}, u32[]{:S(2)}, u32[]{:S(2)}) collective-permute-start(f32[4,8,1024]{2,1,0:T(8,128)S(1)} %get-tuple-element.61), channel_id=1, source_target_pairs={{0,1},{1,0},{2,3},{3,2},{4,5},{5,4},{6,7},{7,6},{8,9},{9,8},{10,11... | collective-permute-start | bytes 393224 | tf_op jit(solution)/shard_map/ppermute | solution.py:445
  9.4 6.9 %collective-permute-start.3 = (f32[3,40,1024]{2,1,0:T(8,128)S(1)}, f32[3,40,1024]{2,1,0:T(8,128)S(1)}, u32[]{:S(2)}, u32[]{:S(2)}) collective-permute-start(f32[3,40,1024]{2,1,0:T(8,128)S(1)} %get-tuple-element.91), channel_id=1, source_target_pairs={{4,0},{8,4},{12,8},{16,12},{20,16},{24,20},{28,24},{32,28},{36,32}... | collective-permute-start | bytes 1474568 | tf_op jit(solution)/shard_map/ppermute | solution.py:379
  16.3 2.9 %collective-permute-start.4 = (f32[3,24,1024]{2,1,0:T(8,128)S(1)}, f32[3,24,1024]{2,1,0:T(8,128)S(1)}, u32[]{:S(2)}, u32[]{:S(2)}) collective-permute-start(f32[3,24,1024]{2,1,0:T(8,128)S(1)} %get-tuple-element.93), channel_id=1, source_target_pairs={{4,0},{8,4},{12,8},{16,12},{20,16},{24,20},{28,24},{32,28},{36,32}... | collective-permute-start | bytes 884744 | tf_op jit(solution)/shard_map/ppermute | solution.py:379
  19.3 0.0 collective-permute-done.cross_ref.refs_5_
  19.3 0.0 collective-permute-done.1.pair_ref.refs_6_
  19.3 0.1 slice_select_fusion
  19.4 3.6 %early.1 = (f32[80,1024]{1,0:T(8,128)S(1)}, f32[3,64,1024]{2,1,0:T(8,128)S(1)}, f32[3,80,1024]{2,1,0:T(8,128)S(1)}, f32[3,80,1024]{2,1,0:T(8,128)S(1)}, f32[3,80...) custom-call(s32[6]{0:T(128)S(1)} %stack.35.pos_ref.refs_0_, ...), custom_call_target="tpu_custom_call", output_to_operand_aliasing={{2}: (1, {})} | custom-call | flops 10000000 | bytes 30000 | tf_op jit(solution)/shard_map/early/pallas_call | solution.py:456
  23.0 1.9 %collective-permute-start.5 = (f32[3,8,1024]{2,1,0:T(8,128)S(1)}, f32[3,8,1024]{2,1,0:T(8,128)S(1)}, u32[]{:S(2)}, u32[]{:S(2)}) collective-permute-start(f32[3,8,1024]{2,1,0:T(8,128)S(1)} %slice_select_fusion), channel_id=1, source_target_pairs={{4,0},{8,4},{12,8},{16,12},{20,16},{24,20},{28,24},{32,28},{36,32}... | collective-permute-start | bytes 294920 | tf_op jit(solution)/shard_map/ppermute | solution.py:379
  24.9 0.8 %late.1 = (f32[4,80,1024]{2,1,0:T(8,128)S(1)}, f32[4,80,1024]{2,1,0:T(8,128)S(1)}, s32[64,1024]{1,0:T(8,128)S(1)}, f32[80,1024]{1,0:T(8,128)S(1)}, f32[3,64,1024...) custom-call(s32[6]{0:T(128)S(1)} %stack.35.pos_ref.refs_0_, ...), custom_call_target="tpu_custom_call", output_to_operand_aliasing={{0}: (7, {}), {1}: (8, {}), {2}: (9, {}), {3}: (10, {}), {4... | custom-call | flops 6000000000 | bytes 18000000 | tf_op jit(solution)/shard_map/late/pallas_call | solution.py:469
  25.7 3.9 %collective-permute-start.2 = (f32[3,64,1024]{2,1,0:T(8,128)S(1)}, f32[3,64,1024]{2,1,0:T(8,128)S(1)}, u32[]{:S(2)}, u32[]{:S(2)}) collective-permute-start(f32[3,64,1024]{2,1,0:T(8,128)S(1)} %get-tuple-element.83.refs_1_), channel_id=1, source_target_pairs={{0,4},{4,8},{8,12},{12,16},{16,20},{20,24},{24,28},{28,32},{32,36}... | collective-permute-start | bytes 2359304 | tf_op jit(solution)/shard_map/ppermute | solution.py:379
  29.6 0.0 collective-permute-done.3.refs_9_
  29.6 2.1 %adjoint_near.1 = (f32[3,24,1024]{2,1,0:T(8,128)S(1)}, f32[3,24,1024]{2,1,0:T(8,128)S(1)}, f32[4,3,80,1024]{3,2,1,0:T(8,128)S(1)}) custom-call(s32[6]{0:T(128)S(1)} %stack.35.pos_ref.refs_0_, f32[80,1024]{1,0:T(8,128)S(1)} %get-tuple-element.84.refs_1_, f32[4,80,1024]{2,1,0:T(8,128)S(1)} %get-tuple-element.85.refs_2_, ...), custom_call_target="tpu_custom_call" | custom-call | flops 100000000 | bytes 300000 | tf_op jit(solution)/shard_map/adjoint_near/pallas_call | solution.py:485
  31.7 7.2 %collective-permute-start.8 = (f32[3,24,1024]{2,1,0:T(8,128)S(1)}, f32[3,24,1024]{2,1,0:T(8,128)S(1)}, u32[]{:S(2)}, u32[]{:S(2)}) collective-permute-start(f32[3,24,1024]{2,1,0:T(8,128)S(1)} %get-tuple-element.101), channel_id=1, source_target_pairs={{4,0},{8,4},{12,8},{16,12},{20,16},{24,20},{28,24},{32,28},{36,32}... | collective-permute-start | bytes 884744 | tf_op jit(solution)/shard_map/ppermute | solution.py:379
  38.9 0.0 collective-permute-done.4.refs_9_
  38.9 1.8 %adjoint_far.1 = (f32[3,24,1024]{2,1,0:T(8,128)S(1)}, f32[3,24,1024]{2,1,0:T(8,128)S(1)}, f32[4,3,80,1024]{3,2,1,0:T(8,128)S(1)}) custom-call(s32[6]{0:T(128)S(1)} %stack.35.pos_ref.refs_0_, f32[80,1024]{1,0:T(8,128)S(1)} %get-tuple-element.84.refs_1_, f32[4,80,1024]{2,1,0:T(8,128)S(1)} %get-tuple-element.85.refs_2_, ...), custom_call_target="tpu_custom_call", output_to_operand_aliasing={{2}: (10, {})} | custom-call | flops 60000002048 | bytes 180000000 | tf_op jit(solution)/shard_map/adjoint_far/pallas_call | solution.py:485
  40.8 4.2 %collective-permute-start.7 = (f32[3,24,1024]{2,1,0:T(8,128)S(1)}, f32[3,24,1024]{2,1,0:T(8,128)S(1)}, u32[]{:S(2)}, u32[]{:S(2)}) collective-permute-start(f32[3,24,1024]{2,1,0:T(8,128)S(1)} %get-tuple-element.100), channel_id=1, source_target_pairs={{4,0},{8,4},{12,8},{16,12},{20,16},{24,20},{28,24},{32,28},{36,32}... | collective-permute-start | bytes 884744 | tf_op jit(solution)/shard_map/ppermute | solution.py:379
  45.0 0.0 collective-permute-done.5.refs_9_
  45.0 1.7 %adjoint_edge.1 = (f32[3,16,1024]{2,1,0:T(8,128)S(1)}, f32[3,16,1024]{2,1,0:T(8,128)S(1)}, f32[4,3,80,1024]{3,2,1,0:T(8,128)S(1)}) custom-call(s32[6]{0:T(128)S(1)} %stack.35.pos_ref.refs_0_, f32[80,1024]{1,0:T(8,128)S(1)} %get-tuple-element.84.refs_1_, f32[4,80,1024]{2,1,0:T(8,128)S(1)} %get-tuple-element.85.refs_2_, ...), custom_call_target="tpu_custom_call", output_to_operand_aliasing={{2}: (10, {})} | custom-call | flops 500000000 | bytes 1500000 | tf_op jit(solution)/shard_map/adjoint_edge/pallas_call | solution.py:485
  46.8 1.9 %collective-permute-start.6 = (f32[3,16,1024]{2,1,0:T(8,128)S(1)}, f32[3,16,1024]{2,1,0:T(8,128)S(1)}, u32[]{:S(2)}, u32[]{:S(2)}) collective-permute-start(f32[3,16,1024]{2,1,0:T(8,128)S(1)} %get-tuple-element.99), channel_id=1, source_target_pairs={{4,0},{8,4},{12,8},{16,12},{20,16},{24,20},{28,24},{32,28},{36,32}... | collective-permute-start | bytes 589832 | tf_op jit(solution)/shard_map/ppermute | solution.py:379
  48.7 0.0 collective-permute-done.8.refs_2_
  48.7 1.3 %settle_near.1.refs_3_ = f32[1,3,64,1024]{3,2,1,0:T(8,128)} custom-call(s32[6]{0:T(128)S(1)} %stack.35.pos_ref.refs_0_, f32[3,64,1024]{2,1,0:T(8,128)S(1)} %get-tuple-element.83.refs_1_, f32[3,24,1024]{2,1,0:T(8,128)S(1)} %collective-permute-done.8.refs_2_), custom_call_target="tpu_custom_call" | custom-call | flops 10000000 | bytes 30000 | tf_op jit(solution)/shard_map/settle_near/pallas_call | solution.py:506
  50.0 1.0 %collective-permute-done.2.previous_ref = f32[3,64,1024]{2,1,0:T(8,128)S(1)} collective-permute-done((f32[3,64,1024]{2,1,0:T(8,128)S(1)}, f32[3,64,1024]{2,1,0:T(8,128)S(1)}, u32[]{:S(2)}, u32[]{:S(2)}) %collective-permute-start.2) | collective-permute-done | bytes 786464 | tf_op jit(solution)/shard_map/ppermute | solution.py:379
  51.0 1.6 %gradient.1.refs_4_ = f32[1,3,64,1024]{3,2,1,0:T(8,128)} custom-call(s32[6]{0:T(128)S(1)} %stack.35.pos_ref.refs_0_, f32[3,80,1024]{2,1,0:T(8,128)S(1)} %get-tuple-element.82.refs_4_.start_ref, f32[3,64,1024]{2,1,0:T(8,128)S(1)} %collective-permute-done.2.previous_ref, f32[3,64,1024]{2,1,0:T(8,128)} %background_ref.1, ...), custom_call_target="tpu_custom_call" | custom-call | flops 10000000 | bytes 30000 | tf_op jit(solution)/shard_map/gradient/pallas_call | solution.py:521
  52.6 0.0 collective-permute-done.7.refs_2_
  52.6 1.3 %settle_far.1.refs_3_ = f32[1,3,64,1024]{3,2,1,0:T(8,128)} custom-call(s32[6]{0:T(128)S(1)} %stack.35.pos_ref.refs_0_, f32[3,64,1024]{2,1,0:T(8,128)S(1)} %get-tuple-element.83.refs_1_, f32[3,24,1024]{2,1,0:T(8,128)S(1)} %collective-permute-done.7.refs_2_, f32[1,3,64,1024]{3,2,1,0:T(8,128)} %settle_near.1.refs_3_, ...), custom_call_target="tpu_custom_call", output_to_operand_aliasing={{}: (3, {})} | custom-call | flops 10000000 | bytes 30000 | tf_op jit(solution)/shard_map/settle_far/pallas_call | solution.py:506
  53.9 0.4 collective-permute-done.6.refs_2_
  54.3 1.2 %settle_edge.1 = f32[1,3,64,1024]{3,2,1,0:T(8,128)} custom-call(s32[6]{0:T(128)S(1)} %stack.35.pos_ref.refs_0_, f32[3,64,1024]{2,1,0:T(8,128)S(1)} %get-tuple-element.83.refs_1_, f32[3,16,1024]{2,1,0:T(8,128)S(1)} %collective-permute-done.6.refs_2_, f32[1,3,64,1024]{3,2,1,0:T(8,128)} %settle_far.1.refs_3_), custom_call_target="tpu_custom_call", output_to_operand_aliasing={{}: (3, {})} | custom-call | flops 10000000 | bytes 30000 | tf_op jit(solution)/shard_map/settle_edge/pallas_call | solution.py:506
  (1 shorter events, 0.0 us)
Async XLA Ops:
  5.8 13.5 %collective-permute-start = (f32[4,8,1024]{2,1,0:T(8,128)S(1)}, f32[4,8,1024]{2,1,0:T(8,128)S(1)}, u32[]{:S(2)}, u32[]{:S(2)}) collective-permute-start(f32[4,8,1024]{2,1,0:T(8,128)S(1)} %get-tuple-element.60), channel_id=1, source_target_pairs={{1,2},{2,1},{5,6},{6,5},{9,10},{10,9},{13,14},{14,13},{17,18},{18,... | collective-permute-start | bytes 393224 | tf_op jit(solution)/shard_map/ppermute | solution.py:444
  6.5 12.8 %collective-permute-start.1 = (f32[4,8,1024]{2,1,0:T(8,128)S(1)}, f32[4,8,1024]{2,1,0:T(8,128)S(1)}, u32[]{:S(2)}, u32[]{:S(2)}) collective-permute-start(f32[4,8,1024]{2,1,0:T(8,128)S(1)} %get-tuple-element.61), channel_id=1, source_target_pairs={{0,1},{1,0},{2,3},{3,2},{4,5},{5,4},{6,7},{7,6},{8,9},{9,8},{10,11... | collective-permute-start | bytes 393224 | tf_op jit(solution)/shard_map/ppermute | solution.py:445
  9.4 20.2 %collective-permute-start.3 = (f32[3,40,1024]{2,1,0:T(8,128)S(1)}, f32[3,40,1024]{2,1,0:T(8,128)S(1)}, u32[]{:S(2)}, u32[]{:S(2)}) collective-permute-start(f32[3,40,1024]{2,1,0:T(8,128)S(1)} %get-tuple-element.91), channel_id=1, source_target_pairs={{4,0},{8,4},{12,8},{16,12},{20,16},{24,20},{28,24},{32,28},{36,32}... | collective-permute-start | bytes 1474568 | tf_op jit(solution)/shard_map/ppermute | solution.py:379
  16.3 22.6 %collective-permute-start.4 = (f32[3,24,1024]{2,1,0:T(8,128)S(1)}, f32[3,24,1024]{2,1,0:T(8,128)S(1)}, u32[]{:S(2)}, u32[]{:S(2)}) collective-permute-start(f32[3,24,1024]{2,1,0:T(8,128)S(1)} %get-tuple-element.93), channel_id=1, source_target_pairs={{4,0},{8,4},{12,8},{16,12},{20,16},{24,20},{28,24},{32,28},{36,32}... | collective-permute-start | bytes 884744 | tf_op jit(solution)/shard_map/ppermute | solution.py:379
  23.0 22.0 %collective-permute-start.5 = (f32[3,8,1024]{2,1,0:T(8,128)S(1)}, f32[3,8,1024]{2,1,0:T(8,128)S(1)}, u32[]{:S(2)}, u32[]{:S(2)}) collective-permute-start(f32[3,8,1024]{2,1,0:T(8,128)S(1)} %slice_select_fusion), channel_id=1, source_target_pairs={{4,0},{8,4},{12,8},{16,12},{20,16},{24,20},{28,24},{32,28},{36,32}... | collective-permute-start | bytes 294920 | tf_op jit(solution)/shard_map/ppermute | solution.py:379
  25.7 25.3 %collective-permute-start.2 = (f32[3,64,1024]{2,1,0:T(8,128)S(1)}, f32[3,64,1024]{2,1,0:T(8,128)S(1)}, u32[]{:S(2)}, u32[]{:S(2)}) collective-permute-start(f32[3,64,1024]{2,1,0:T(8,128)S(1)} %get-tuple-element.83.refs_1_), channel_id=1, source_target_pairs={{0,4},{4,8},{8,12},{12,16},{16,20},{20,24},{24,28},{28,32},{32,36}... | collective-permute-start | bytes 2359304 | tf_op jit(solution)/shard_map/ppermute | solution.py:379
  31.7 17.0 %collective-permute-start.8 = (f32[3,24,1024]{2,1,0:T(8,128)S(1)}, f32[3,24,1024]{2,1,0:T(8,128)S(1)}, u32[]{:S(2)}, u32[]{:S(2)}) collective-permute-start(f32[3,24,1024]{2,1,0:T(8,128)S(1)} %get-tuple-element.101), channel_id=1, source_target_pairs={{4,0},{8,4},{12,8},{16,12},{20,16},{24,20},{28,24},{32,28},{36,32}... | collective-permute-start | bytes 884744 | tf_op jit(solution)/shard_map/ppermute | solution.py:379
  40.8 11.8 %collective-permute-start.7 = (f32[3,24,1024]{2,1,0:T(8,128)S(1)}, f32[3,24,1024]{2,1,0:T(8,128)S(1)}, u32[]{:S(2)}, u32[]{:S(2)}) collective-permute-start(f32[3,24,1024]{2,1,0:T(8,128)S(1)} %get-tuple-element.100), channel_id=1, source_target_pairs={{4,0},{8,4},{12,8},{16,12},{20,16},{24,20},{28,24},{32,28},{36,32}... | collective-permute-start | bytes 884744 | tf_op jit(solution)/shard_map/ppermute | solution.py:379
  46.8 7.6 %collective-permute-start.6 = (f32[3,16,1024]{2,1,0:T(8,128)S(1)}, f32[3,16,1024]{2,1,0:T(8,128)S(1)}, u32[]{:S(2)}, u32[]{:S(2)}) collective-permute-start(f32[3,16,1024]{2,1,0:T(8,128)S(1)} %get-tuple-element.99), channel_id=1, source_target_pairs={{4,0},{8,4},{12,8},{16,12},{20,16},{24,20},{28,24},{32,28},{36,32}... | collective-permute-start | bytes 589832 | tf_op jit(solution)/shard_map/ppermute | solution.py:379
